TPU v7x, 128 devices: a whole 4x4x4 slice. The times are simulated.
128 devices in a mesh: seq: 16 (over z, y_hi, core), col: 4 (over x), batch: 2 (over y_lo).
Axes of the slice: x: 4, y: 4 (y_hi: 2, y_lo: 2; y = y_hi * 2 + y_lo), z: 4, core: 2. Of those that a mesh axis runs over, the one named last changes fastest.
Arguments:
- tokens: int32 [2, 1048576], P('batch', ('seq', 'col')), may hold values from 0 to 3
- stem_weight: bfloat16 [64, 768], replicated, may hold values from -1.5 to 1.5
- conv_weight: bfloat16 [3840, 768], replicated, may hold values from -0.09375 to 0.09375
- conv_bias: float32 [768], replicated, may hold values from -1 to 1
- up_weight: bfloat16 [768, 1536], replicated, may hold values from -0.21875 to 0.21875
- norm_gain: float32 [1536], replicated, may hold values from 0.1 to 1.9
- pair_weight: bfloat16 [1536, 64], replicated, may hold values from -0.15625 to 0.15625
- out_weight: bfloat16 [1024, 128], replicated, may hold values from -0.1875 to 0.1875
- cotangent: bfloat16 [2, 512, 512, 128], P('batch', 'seq', 'col'), may hold values from -24 to 24
- projection: float32 [768, 128], replicated, may hold values from -0.21875 to 0.21875
- buckets: int32 [3840], replicated, may hold values from 0 to 31
Outputs:
- input_grad: bfloat16 [2, 65536, 768], P('batch', ('seq', 'col'))
- embedding: float32 [2, 32, 128], P('batch')
All inputs are finite; a program needn't handle non-finite values.
Results may differ from a plain program's by a relative error of at most 0.012.
Values may be sent and summed in bfloat16 or wider, within the bound.
No kernel may reach another device: no remote copies, remote signals or barrier semaphores. Data moves between devices by JAX's collectives and lax.ppermute only.
A program may use at most 128 MiB of HBM per device.

v0:
```python
import jax
import jax.numpy as jnp
from jax import lax
from jax.sharding import PartitionSpec as P

OP = 32
PATCH = 16
POOL = 128
BUCKETS = 32


highest = lax.Precision.HIGHEST


def extended(cells, sides, width):
    for axis, dim in sides:
        count = lax.axis_size(axis)
        ends = count - 1
        head = lax.slice_in_dim(cells, 0, width, axis=dim)
        tail = lax.slice_in_dim(cells, cells.shape[dim] - width, cells.shape[dim], axis=dim)
        cells = jnp.concatenate(
            [
                lax.ppermute(tail, axis, [(i, (i + 1) % count) for i in range(ends)]),
                cells,
                lax.ppermute(head, axis, [((i + 1) % count, i) for i in range(ends)]),
            ],
            axis=dim,
        )
    return cells


def shards(
    tokens,
    stem_weight,
    conv_weight,
    conv_bias,
    up_weight,
    norm_gain,
    pair_weight,
    out_weight,
    cotangent,
    projection,
    buckets,
):
    channels = conv_weight.shape[1]
    kernel = conv_weight.shape[0] // channels
    reach = (kernel - 1) // 2
    patches = tokens.shape[1] // PATCH
    bins_dev = patches // POOL
    bases = tokens[0].reshape(patches, PATCH)
    onehot = (
        (bases[:, :, None] == jnp.arange(4, dtype=jnp.int32))
        .astype(jnp.bfloat16)
        .reshape(patches, PATCH * 4)
    )
    embedded = jnp.dot(onehot, stem_weight, preferred_element_type=jnp.float32).astype(jnp.bfloat16)
    padded = extended(embedded, ((("seq", "col"), 0),), reach)
    unfolded = jnp.concatenate(
        [padded[offset : offset + patches] for offset in range(kernel)], axis=1
    )
    before = jnp.dot(unfolded, conv_weight, preferred_element_type=jnp.float32) + conv_bias
    after, gelu_back = jax.vjp(jax.nn.gelu, before)
    pooled = jnp.mean(after.reshape(bins_dev, POOL, channels), axis=1).astype(jnp.bfloat16)
    hidden = jnp.dot(pooled, up_weight, preferred_element_type=jnp.float32)
    inverse = lax.rsqrt(jnp.mean(hidden * hidden, axis=1, keepdims=True) + 1e-06)
    normed = (hidden * inverse * norm_gain).astype(jnp.bfloat16)
    seq_count = lax.axis_size("seq")
    col_count = lax.axis_size("col")
    row_len = bins_dev * col_count
    col_len = bins_dev * seq_count
    all_bins = row_len * seq_count
    row_index = lax.axis_index("seq")
    col_index = lax.axis_index("col")
    every = lax.all_gather(normed, ("seq", "col"), axis=0, tiled=True)
    row_part = lax.dynamic_slice_in_dim(every, row_index * row_len, row_len, 0)
    col_part = lax.dynamic_slice_in_dim(every, col_index * col_len, col_len, 0)
    left = jnp.dot(row_part, pair_weight[:, :OP], preferred_element_type=jnp.float32).astype(
        jnp.bfloat16
    )
    right = jnp.dot(col_part, pair_weight[:, OP:], preferred_element_type=jnp.float32).astype(
        jnp.bfloat16
    )
    pair_channels = cotangent.shape[3]
    blocks = cotangent[0].reshape(col_count, bins_dev, col_len, pair_channels)
    left_groups = left.astype(jnp.float32).reshape(col_count, bins_dev, OP)
    right_wide = right.astype(jnp.float32)

    def pair_step(carry, inputs):
        block, rows_left = inputs
        outer_grad = lax.dot_general(
            block.reshape(bins_dev * col_len, pair_channels),
            out_weight,
            (((1,), (1,)), ((), ())),
            preferred_element_type=jnp.float32,
        ).reshape(bins_dev, col_len, OP, OP)
        grad_left = jnp.einsum("ijkl,jl->ik", outer_grad, right_wide, precision=highest)
        carry = carry + jnp.einsum("ijkl,ik->jl", outer_grad, rows_left, precision=highest)
        return (carry, grad_left)

    grad_right, grad_left = lax.scan(
        pair_step, jnp.zeros((col_len, OP), jnp.float32), (blocks, left_groups)
    )
    grad_left = grad_left.reshape(row_len, OP)
    row_term = lax.dot_general(
        grad_left,
        pair_weight[:, :OP].astype(jnp.float32),
        (((1,), (1,)), ((), ())),
        precision=highest,
    )
    col_term = lax.dot_general(
        grad_right,
        pair_weight[:, OP:].astype(jnp.float32),
        (((1,), (1,)), ((), ())),
        precision=highest,
    )
    empty_rows = jnp.zeros((all_bins, row_term.shape[1]), jnp.float32)
    placed = lax.dynamic_update_slice_in_dim(
        empty_rows, row_term, row_index * row_len, 0
    ) + lax.dynamic_update_slice_in_dim(empty_rows, col_term, col_index * col_len, 0)
    d_normed = lax.psum_scatter(placed, ("seq", "col"), scatter_dimension=0, tiled=True)
    scaled = d_normed * norm_gain
    inner = jnp.mean(scaled * hidden, axis=1, keepdims=True)
    d_hidden = inverse * scaled - hidden * inverse**3 * inner
    d_pooled = lax.dot_general(
        d_hidden, up_weight.astype(jnp.float32), (((1,), (1,)), ((), ())), precision=highest
    )
    spread = jnp.broadcast_to(d_pooled[:, None, :] / POOL, (bins_dev, POOL, channels)).reshape(
        patches, channels
    )
    d_before = gelu_back(spread)[0].astype(jnp.bfloat16)
    grads_padded = extended(d_before, ((("seq", "col"), 0),), reach)
    stacked = jnp.stack(
        [
            grads_padded[2 * reach - offset : 2 * reach - offset + patches]
            for offset in range(kernel)
        ],
        axis=1,
    )
    input_grad = jnp.einsum(
        "tko,kio->ti",
        stacked,
        conv_weight.reshape(kernel, channels, channels),
        preferred_element_type=jnp.float32,
    ).astype(jnp.bfloat16)
    share_rows = unfolded.shape[1] // lax.axis_size(("seq", "col"))
    share = lax.psum_scatter(
        lax.dot_general(
            unfolded, d_before, (((0,), (0,)), ((), ())), preferred_element_type=jnp.float32
        ),
        ("seq", "col"),
        scatter_dimension=0,
        tiled=True,
    )
    labels = lax.dynamic_slice_in_dim(
        buckets, lax.axis_index(("seq", "col")) * share_rows, share_rows, 0
    )
    projected = jnp.dot(share, projection, precision=highest)
    member = (labels[None, :] == jnp.arange(BUCKETS, dtype=jnp.int32)[:, None]).astype(jnp.float32)
    sketch = lax.psum(jnp.dot(member, projected, precision=highest), ("seq", "col"))
    unit = sketch * lax.rsqrt(jnp.mean(sketch * sketch) + 1e-06)
    center = lax.psum(unit, "batch") / lax.axis_size("batch")
    return (input_grad[None], (unit - center)[None])


def solution(mesh):
    in_specs = (
        P("batch", ("seq", "col")),
        P(),
        P(),
        P(),
        P(),
        P(),
        P(),
        P(),
        P("batch", "seq", "col", None),
        P(),
        P(),
    )
    out_specs = (P("batch", ("seq", "col"), None), P("batch", None, None))
    return jax.shard_map(shards, mesh=mesh, in_specs=in_specs, out_specs=out_specs, check_vma=False)
```

profile of v0, /device:TPU:1, one launch (start us, length us, event | category | flops | bytes accessed | tf_op | source)
XLA Modules:
  0.0 915.9 jit_solution(1880735338173199356)
XLA Ops:
  11.8 3.9 collective-permute-start
  15.7 3.7 collective-permute-start.1
  22.4 8.4 bitcast_reduce_fusion
  32.4 73.3 %all-gather.2.cloned.1.call-done = bf16[512,1536]{1,0:T(8,128)(2,1)} async-done(((bf16[8,1536]{1,0:T(8,128)(2,1)}), bf16[512,1536]{1,0:T(8,128)(2,1)}) %all-gather.2.cloned.1.call-update) | async-done | bytes 1572880 | tf_op jit(solution)/shard_map/all_gather | solution.py:74
  108.0 78.4 %while.13 = (s32[]{:T(128)}, f32[128,32]{1,0:T(8,128)S(1)}, f32[4,8,32]{2,1,0:T(8,128)S(1)}, bf16[4,8,128,128]{3,2,1,0:T(8,128)(2,1)}, bf16[1024,128]{1,0:T(8,12...) while((s32[]{:T(128)}, f32[128,32]{1,0:T(8,128)S(1)}, ...), condition=%wide.region_3.4_spmd.clone, body=%wide.region_2.3_spmd.clone.sunk | while | flops 293609472 | bytes 30050948 | solution.py:100
  108.0 3.6 fusion.101
  111.7 11.1 %fusion.102 = f32[1,8,32,1]{2,0,3,1:T(1,128)S(1)} fusion(f32[128,32,1,1]{0,2,1,3:T(1,128)S(1)} %copy.35, f32[8,128,32,32]{1,3,2,0:T(8,128)} %fusion.101), kind=kOutput, calls=%fused_computation.clone.1 | convolution fusion | flops 12582912 | bytes 4211712 | tf_op jit(solution)/shard_map/while/body/eval_jaxpr/ijkl,jl->ik/dot_general | solution.py:96
  122.8 4.7 fusion.103
  127.6 3.6 fusion.101
  131.3 11.1 %fusion.102 = f32[1,8,32,1]{2,0,3,1:T(1,128)S(1)} fusion(f32[128,32,1,1]{0,2,1,3:T(1,128)S(1)} %copy.35, f32[8,128,32,32]{1,3,2,0:T(8,128)} %fusion.101), kind=kOutput, calls=%fused_computation.clone.1 | convolution fusion | flops 12582912 | bytes 4211712 | tf_op jit(solution)/shard_map/while/body/eval_jaxpr/ijkl,jl->ik/dot_general | solution.py:96
  142.4 4.7 fusion.103
  147.2 3.6 fusion.101
  150.9 11.1 %fusion.102 = f32[1,8,32,1]{2,0,3,1:T(1,128)S(1)} fusion(f32[128,32,1,1]{0,2,1,3:T(1,128)S(1)} %copy.35, f32[8,128,32,32]{1,3,2,0:T(8,128)} %fusion.101), kind=kOutput, calls=%fused_computation.clone.1 | convolution fusion | flops 12582912 | bytes 4211712 | tf_op jit(solution)/shard_map/while/body/eval_jaxpr/ijkl,jl->ik/dot_general | solution.py:96
  162.0 4.7 fusion.103
  166.8 3.6 fusion.101
  170.5 11.1 %fusion.102 = f32[1,8,32,1]{2,0,3,1:T(1,128)S(1)} fusion(f32[128,32,1,1]{0,2,1,3:T(1,128)S(1)} %copy.35, f32[8,128,32,32]{1,3,2,0:T(8,128)} %fusion.101), kind=kOutput, calls=%fused_computation.clone.1 | convolution fusion | flops 12582912 | bytes 4211712 | tf_op jit(solution)/shard_map/while/body/eval_jaxpr/ijkl,jl->ik/dot_general | solution.py:96
  181.6 4.7 fusion.103
  186.4 2.0 broadcast_in_dim.16
  189.3 2.5 fusion.19
  193.9 141.0 %reduce-scatter.4.cloned.1.call-done = f32[8,1536]{1,0:T(8,128)} async-done(((f32[512,1536]{1,0:T(8,128)}), f32[8,1536]{1,0:T(8,128)}) %reduce-scatter.4.cloned.1.call-update) | async-done | bytes 49168 | tf_op jit(solution)/shard_map/reduce_scatter | solution.py:120
  335.8 2.7 convolution_multiply_fusion
  338.6 3.7 fusion.15
  342.3 12.6 %fusion.70 = f32[3840,768]{1,0:T(8,128)} fusion(bf16[1024,3840]{1,0:T(8,128)(2,1)} %copy-done.6, bf16[1024,768]{1,0:T(8,128)(2,1)S(1)} %fusion.15), kind=kOutput, calls=%fused_computation.110 | convolution fusion | flops 6039797760 | bytes 21233664 | tf_op jit(solution)/shard_map/dot_general | solution.py:147
  354.9 5.2 collective-permute-start.2
  360.1 192.2 %fusion = f32[64,768]{1,0:T(8,128)S(1)} fusion(f32[3840,768]{1,0:T(8,128)} %fusion.70), kind=kCustom, calls=%all-reduce-scatter | all-reduce-scatter fusion | flops 3145729 | bytes 11993600
  552.4 2.1 collective-permute-start.4
  562.2 1.9 fusion.25
  564.6 1.9 collective-permute-done.3
  567.4 7.4 fusion.36
  576.2 4.3 concatenate.26
  582.0 319.9 %psum.14 = f32[32,128]{1,0:T(8,128)S(1)} all-reduce(f32[32,128]{1,0:T(8,128)S(1)} %fusion.60), channel_id=1, replica_groups=mesh['seq'=16,'col'=4,'batch'=2] {'seq','col'}, use_global_device_ids=true, to_apply=%region_7.8 | all-reduce | flops 4096 | bytes 32768 | tf_op jit(solution)/shard_map/psum | solution.py:159
  903.2 5.3 psum.15
  (112 shorter events, 28.3 us)
Async XLA Ops:
  7.2 23.7 %copy-start = (bf16[768,1536]{1,0:T(8,128)(2,1)S(1)}, bf16[768,1536]{1,0:T(8,128)(2,1)}, u32[]{:S(2)}) copy-start(bf16[768,1536]{1,0:T(8,128)(2,1)} %param.17) | copy-start | bytes 7077892
  7.2 98.4 %all-gather.2.cloned.1.call-start = ((), (), s32[]{:S(2)}) async-start(), calls=%async_computation.1 | async-start | bytes 1597440 | tf_op jit(solution)/shard_map/all_gather | solution.py:74
  11.8 7.7 collective-permute-start
  15.7 4.7 collective-permute-start.1
  19.5 2.2 slice-start
  20.3 2.1 slice-start.1
  20.4 2.0 copy-start.11
  22.4 8.4 copy-start.6
  22.4 9.0 copy-start.10
  22.4 83.2 %copy-start.5 = (bf16[1536,64]{0,1:T(8,128)(2,1)S(1)}, bf16[1536,64]{0,1:T(8,128)(2,1)}, u32[]{:S(2)}) copy-start(bf16[1536,64]{0,1:T(8,128)(2,1)} %param.19) | copy-start | bytes 589828
  30.8 77.2 %copy-start.4 = (bf16[1024,128]{1,0:T(8,128)(2,1)S(1)}, bf16[1024,128]{1,0:T(8,128)(2,1)}, u32[]{:S(2)}) copy-start(bf16[1024,128]{1,0:T(8,128)(2,1)} %param.20) | copy-start | bytes 786436
  32.1 302.8 %reduce-scatter.4.cloned.1.call-start = ((), (), s32[]{:S(2)}) async-start(), calls=%async_computation.2 | async-start | bytes 3194880 | tf_op jit(solution)/shard_map/reduce_scatter | solution.py:120
  111.7 11.1 %copy-start.1 = (f32[8,128,32,32]{1,3,2,0:T(8,128)S(1)}, f32[8,128,32,32]{1,3,2,0:T(8,128)}, u32[]{:S(2)}) copy-start(f32[8,128,32,32]{1,3,2,0:T(8,128)} %fusion.101) | copy-start | bytes 12582916 | tf_op jit(solution)/shard_map/while
  131.3 11.1 %copy-start.1 = (f32[8,128,32,32]{1,3,2,0:T(8,128)S(1)}, f32[8,128,32,32]{1,3,2,0:T(8,128)}, u32[]{:S(2)}) copy-start(f32[8,128,32,32]{1,3,2,0:T(8,128)} %fusion.101) | copy-start | bytes 12582916 | tf_op jit(solution)/shard_map/while
  150.9 11.1 %copy-start.1 = (f32[8,128,32,32]{1,3,2,0:T(8,128)S(1)}, f32[8,128,32,32]{1,3,2,0:T(8,128)}, u32[]{:S(2)}) copy-start(f32[8,128,32,32]{1,3,2,0:T(8,128)} %fusion.101) | copy-start | bytes 12582916 | tf_op jit(solution)/shard_map/while
  170.5 11.1 %copy-start.1 = (f32[8,128,32,32]{1,3,2,0:T(8,128)S(1)}, f32[8,128,32,32]{1,3,2,0:T(8,128)}, u32[]{:S(2)}) copy-start(f32[8,128,32,32]{1,3,2,0:T(8,128)} %fusion.101) | copy-start | bytes 12582916 | tf_op jit(solution)/shard_map/while
  188.4 3.4 copy-start.12
  342.2 12.6 %copy-start.2 = (bf16[1024,768]{1,0:T(8,128)(2,1)}, bf16[1024,768]{1,0:T(8,128)(2,1)S(1)}, u32[]{:S(2)}) copy-start(bf16[1024,768]{1,0:T(8,128)(2,1)S(1)} %fusion.15) | copy-start | bytes 4718596
  354.9 205.4 %collective-permute-start.2 = (bf16[2,768]{1,0:T(2,128)(2,1)S(1)}, bf16[2,768]{1,0:T(2,128)(2,1)S(1)}, u32[]{:S(2)}, u32[]{:S(2)}) collective-permute-start(bf16[2,768]{1,0:T(2,128)(2,1)S(1)} %get-tuple-element.104), channel_id=1, source_target_pairs={{2,0},{4,2},{6,4},{8,6},{10,8},{12,10},{14,12},{16,14},{18,16},{20... | collective-permute-start | bytes 9224 | tf_op jit(solution)/shard_map/ppermute | solution.py:25
  552.4 11.8 %copy-start.3 = (bf16[1024,768]{1,0:T(8,128)(2,1)S(1)}, bf16[1024,768]{1,0:T(8,128)(2,1)}, u32[]{:S(2)}) copy-start(bf16[1024,768]{1,0:T(8,128)(2,1)} %copy-done.2) | copy-start | bytes 4718596
  552.4 22.4 %collective-permute-start.4 = (f32[64,768]{1,0:T(8,128)S(1)}, f32[64,768]{1,0:T(8,128)S(1)}, u32[]{:S(2)}, u32[]{:S(2)}) collective-permute-start(f32[64,768]{1,0:T(8,128)S(1)} %fusion), channel_id=1, source_target_pairs={{0,2},{2,4},{4,6},{6,8},{8,10},{10,12},{12,14},{14,16},{16,18},{18... | collective-permute-start | bytes 589832
  554.4 20.3 %collective-permute-start.5 = (f32[64,768]{1,0:T(8,128)S(1)}, f32[64,768]{1,0:T(8,128)S(1)}, u32[]{:S(2)}, u32[]{:S(2)}) collective-permute-start(f32[64,768]{1,0:T(8,128)S(1)} %fusion), channel_id=1, source_target_pairs={{0,4},{2,6},{4,8},{6,10},{8,12},{10,14},{12,16},{14,18},{16,20},{1... | collective-permute-start | bytes 589832
  556.4 19.8 %collective-permute-start.6 = (f32[64,768]{1,0:T(8,128)S(1)}, f32[64,768]{1,0:T(8,128)}, u32[]{:S(2)}, u32[]{:S(2)}) collective-permute-start(f32[64,768]{1,0:T(8,128)S(1)} %fusion), channel_id=1, source_target_pairs={{0,6},{2,8},{4,10},{6,12},{8,14},{10,16},{12,18},{14,20},{16,22},{... | collective-permute-start | bytes 589832
  558.3 16.4 %collective-permute-start.7 = (f32[60,768]{1,0:T(8,128)S(1)}, f32[60,768]{1,0:T(8,128)S(1)}, u32[]{:S(2)}, u32[]{:S(2)}) collective-permute-start(f32[60,768]{1,0:T(8,128)S(1)} %slice.78), channel_id=1, source_target_pairs={{0,8},{2,10},{4,12},{6,14},{8,16},{10,18},{12,20},{14,22},{16,24},... | collective-permute-start | bytes 552968
  560.2 6.3 collective-permute-start.3
  562.2 5.2 slice-start.2
  564.5 2.8 slice-start.3
  574.8 0.7 copy-start.9
  574.8 0.7 copy-start.7
  575.5 0.7 copy-start.8
Sparse Core Ops, SparseCore 0:
  32.2 73.3 all-gather.1
  192.0 142.8 reduce-scatter.3
where the time goes:
time: 927 us; the launch traced here: 916 us
  blocking collectives  517 us (56%)
  waiting for transfers between devices  216 us (23%)
  matrix products  118 us (13%)
  starting transfers between devices  22.9 us (2%)
  between operations  15.8 us (2%)
  other arithmetic  13 us (1%)
  local copies, waits for them, and re-layouts  12.5 us (1%)
    psum x1, blocking collectives, shards(): lax.psum(jnp.dot(member, projected, precision=highest), ('seq', 'col'))  320 us
    unnamed x1, blocking collectives  192 us
    reduce_scatter x1, waiting for transfers between devices, shards(): lax.psum_scatter(placed, ('seq', 'col'), scatter_dimension=0, tiled=True)  141 us
    all_gather x1, waiting for transfers between devices, shards(): every = lax.all_gather(normed, ('seq', 'col'), axis=0, tiled=True)  73.3 us
    dot_general x4, matrix products, pair_step(): jnp.einsum('ijkl,jl->ik', outer_grad, right_wide, precision=highest)  44.3 us
    dot_general x4, matrix products, pair_step(): jnp.einsum('ijkl,ik->jl', outer_grad, rows_left, precision=highest)  18.7 us
  transfers between devices with their start and end apart: 10, of which 3 were waited for; matrix products, arithmetic and copies ran while one was open for 22% of the time, Pallas kernels for 0%

commit v1 on v0

v1 whole, which is shorter than its diff:
```python
import functools
import jax
import jax.numpy as jnp
from jax import lax
from jax.experimental import pallas as pl
from jax.experimental.pallas import tpu as pltpu
from jax.sharding import PartitionSpec as P

OP = 32
PATCH = 16
POOL = 128
BUCKETS = 32
LANES = 128
PAD = 8
ROOT = 0.7978845608028654
CUBIC = 0.044715

f32 = jnp.float32
bf16 = jnp.bfloat16
NT = (((1,), (1,)), ((), ()))
highest = lax.Precision.HIGHEST


def split(x):
    hi = lax.reduce_precision(x, 8, 7)
    return hi.astype(bf16), (x - hi).astype(bf16)


def split_rows(x):
    hi, lo = split(x)
    return jnp.concatenate([hi, lo], axis=0)


def split_in_kernel(x):
    hi = x.astype(bf16)
    return hi, (x - hi.astype(f32)).astype(bf16)


def pair_kernel(where, parts, cot, wide, out, moved):
    rows, cols, _ = cot.shape
    bins = parts.shape[1]
    seq, col = where[0], where[1]
    mine = parts[pl.ds(seq * (rows // bins), rows // bins)].astype(f32).reshape(rows, LANES)
    left = mine[:, :OP].astype(bf16)
    other = parts[pl.ds(col * (cols // bins), cols // bins)].astype(f32).reshape(cols, LANES)
    right = other.T[OP : 2 * OP].astype(bf16)
    grid = jnp.concatenate([cot[i] for i in range(rows)], axis=1)
    weighted = jnp.dot(left, wide[...], preferred_element_type=f32)
    for l in range(OP):
        moved[pl.ds(l, rows, stride=OP), :] = weighted[:, l * LANES : (l + 1) * LANES]
    stacked = jnp.concatenate([moved[i * OP : (i + 1) * OP, :] for i in range(rows)], axis=1)
    hi, lo = split_in_kernel(stacked)
    both = lax.dot_general(
        grid, jnp.concatenate([hi, lo], axis=0), NT, preferred_element_type=f32
    )
    grad_right = both[:, :OP] + both[:, OP:]
    summed = jnp.dot(right, grid, preferred_element_type=f32)
    for i in range(rows):
        moved[i * OP : (i + 1) * OP, :] = summed[:, i * LANES : (i + 1) * LANES]
    by_row = jnp.concatenate([moved[pl.ds(l, rows, stride=OP), :] for l in range(OP)], axis=1)
    hi, lo = split_in_kernel(by_row)
    both = lax.dot_general(
        jnp.concatenate([hi, lo], axis=0), wide[...], NT, preferred_element_type=f32
    )
    grad_left = both[:rows] + both[rows:]
    out[...] = jnp.zeros_like(out)
    out[pl.ds(seq * (rows // bins), rows // bins), :, :OP] = grad_left.reshape(-1, bins, OP)
    out[pl.ds(col * (cols // bins), cols // bins), :, OP : 2 * OP] = grad_right.reshape(
        -1, bins, OP
    )


def pair_stage(where, parts, cot, wide):
    vmem = pl.BlockSpec(memory_space=pltpu.VMEM)
    return pl.pallas_call(
        pair_kernel,
        out_shape=jax.ShapeDtypeStruct(parts.shape, f32),
        in_specs=[pl.BlockSpec(memory_space=pltpu.SMEM), vmem, vmem, vmem],
        out_specs=vmem,
        scratch_shapes=[pltpu.VMEM((cot.shape[0] * OP, LANES), f32)],
        compiler_params=pltpu.CompilerParams(vmem_limit_bytes=32 << 20),
        cost_estimate=pl.CostEstimate(flops=200_000_000, bytes_accessed=2_000_000, transcendentals=0),
        name="pair",
    )(where, parts, cot, wide)


def iota(shape, dim): return lax.broadcasted_iota(jnp.int32, shape, dim)

def forward_kernel(chunk, tokens, ends, stem, taps, bias, up, gain, pair, spread, slope, hidden_out, inverse_out, parts, cells, unfolded, pools):
    lines = tokens.shape[0]
    patches = lines * LANES // PATCH
    per = LANES // PATCH
    channels = stem.shape[1]
    blocks = channels // LANES
    kernel = taps.shape[0] // channels
    reach = (kernel - 1) // 2
    t = iota((patches, LANES), 0)
    lane = iota((patches, LANES), 1)
    repeat = (t // per == lane).astype(bf16)
    rows = jnp.dot(repeat, tokens[...].astype(f32).astype(bf16), preferred_element_type=f32)
    own = jnp.where(lane // PATCH == t % per, rows + 1.0, 0.0).astype(bf16)
    fold = (iota((LANES, 4 * PATCH), 0) % PATCH == iota((LANES, 4 * PATCH), 1) // 4).astype(bf16)
    base = jnp.dot(own, fold, preferred_element_type=f32)
    onehot = (base == (iota((patches, 4 * PATCH), 1) % 4 + 1).astype(f32)).astype(f32).astype(bf16)
    main = jnp.dot(onehot, stem[...], preferred_element_type=f32).astype(bf16)
    edges = jnp.dot(ends[...].astype(bf16), stem[...], preferred_element_type=f32).astype(bf16).astype(f32)
    spread[PAD:PAD + patches, :] = main
    wide = main.astype(f32)
    for c in range(blocks):
        at = slice(c * LANES, (c + 1) * LANES)
        cells[c, :PAD, :] = edges[:PAD, at]
        cells[c, PAD:PAD + patches, :] = wide[:, at]
        cells[c, PAD + patches:, :] = edges[PAD:, at]
    spread[:PAD, :] = edges[:PAD].astype(bf16)
    spread[PAD + patches:, :] = edges[PAD:].astype(bf16)
    for r in range(patches // chunk):
        slot = r % 2
        for k in range(kernel):
            for c in range(blocks):
                start = r * chunk + PAD - reach + k
                j = (k * blocks + c) * LANES
                unfolded[slot, :, j:j + LANES] = cells[c, start:start + chunk, :].astype(bf16)
        before = jnp.dot(unfolded[slot], taps[...], preferred_element_type=f32) + bias[...]
        square = before * before
        bent = jnp.tanh(before * (ROOT + ROOT * CUBIC * square))
        half = 0.5 * (1.0 + bent)
        after = before * half
        tilt = half + before * (0.5 - 0.5 * bent * bent) * (ROOT + 3.0 * ROOT * CUBIC * square)
        slope[r * chunk:(r + 1) * chunk, :] = tilt.astype(bf16)
        for n in range(chunk // POOL):
            b = r * (chunk // POOL) + n
            pools[b:b + 1, :] = jnp.sum(after[n * POOL:(n + 1) * POOL], axis=0, keepdims=True) * (1.0 / POOL)
    hidden = jnp.dot(pools[...].astype(bf16), up[...], preferred_element_type=f32)
    inverse = lax.rsqrt(jnp.mean(hidden * hidden, axis=1, keepdims=True) + 1e-06)
    normed = (hidden * inverse * gain[...]).astype(bf16)
    sides = lax.dot_general(normed, pair[...], NT, preferred_element_type=f32)
    hidden_out[...] = hidden
    inverse_out[...] = jnp.broadcast_to(inverse, inverse_out.shape)
    full = jnp.concatenate([sides, jnp.zeros_like(sides)], axis=1).astype(bf16)
    parts[...] = jnp.broadcast_to(full[None], parts.shape)

def forward_stage(tokens, ends, stem, taps, bias, up, gain, pair, count, chunk=256):
    vmem = pl.BlockSpec(memory_space=pltpu.VMEM)
    lines = tokens.shape[0]
    patches = lines * LANES // PATCH
    channels = stem.shape[1]
    bins = patches // POOL
    tall = patches + 2 * PAD
    return pl.pallas_call(
        functools.partial(forward_kernel, chunk),
        out_shape=[
            jax.ShapeDtypeStruct((tall, channels), bf16),
            jax.ShapeDtypeStruct((patches, channels), bf16),
            jax.ShapeDtypeStruct((bins, up.shape[1]), f32),
            jax.ShapeDtypeStruct((bins, LANES), f32),
            jax.ShapeDtypeStruct((count, bins, LANES), bf16),
        ],
        in_specs=[vmem] * 8, out_specs=[vmem] * 5,
        scratch_shapes=[
            pltpu.VMEM((channels // LANES, tall, LANES), f32),
            pltpu.VMEM((2, chunk, taps.shape[0]), bf16),
            pltpu.VMEM((bins, channels), f32),
        ],
        compiler_params=pltpu.CompilerParams(vmem_limit_bytes=40 << 20),
        cost_estimate=pl.CostEstimate(flops=6_200_000_000, bytes_accessed=14_000_000, transcendentals=800_000),
        name="forward",
    )(tokens, ends, stem, taps, bias, up, gain, pair)

def input_kernel(chunk, slope, d_pooled, ends, taps, out, cells, shifted):
    patches, channels = slope.shape
    blocks = channels // LANES
    kernel = taps.shape[0] // channels
    reach = (kernel - 1) // 2
    for c in range(blocks):
        at = slice(c * LANES, (c + 1) * LANES)
        cells[c, :PAD, :] = ends[:PAD, at].astype(f32)
        cells[c, PAD + patches:, :] = ends[PAD:, at].astype(f32)
        for n in range(patches // POOL):
            rows = slice(n * POOL, (n + 1) * POOL)
            cells[c, PAD + n * POOL:PAD + (n + 1) * POOL, :] = slope[rows, at].astype(f32) * d_pooled[n:n + 1, at]
    for r in range(patches // chunk):
        total = None
        for k in range(kernel):
            for c in range(blocks):
                start = r * chunk + PAD + reach - k
                j = c * LANES
                shifted[(r * kernel + k) % 2, :, j:j + LANES] = cells[c, start:start + chunk, :].astype(bf16)
            term = lax.dot_general(shifted[(r * kernel + k) % 2], taps[k * channels:(k + 1) * channels, :], NT, preferred_element_type=f32)
            total = term if total is None else total + term
        out[r * chunk:(r + 1) * chunk, :] = total.astype(bf16)

def input_stage(slope, d_pooled, ends, taps, chunk=256):
    vmem = pl.BlockSpec(memory_space=pltpu.VMEM)
    patches, channels = slope.shape
    tall = patches + 2 * PAD
    return pl.pallas_call(
        functools.partial(input_kernel, chunk),
        out_shape=jax.ShapeDtypeStruct((patches, channels), bf16),
        in_specs=[vmem] * 4, out_specs=vmem,
        scratch_shapes=[
            pltpu.VMEM((channels // LANES, tall, LANES), f32),
            pltpu.VMEM((2, chunk, channels), bf16),
        ],
        compiler_params=pltpu.CompilerParams(vmem_limit_bytes=40 << 20),
        cost_estimate=pl.CostEstimate(flops=6_200_000_000, bytes_accessed=10_000_000, transcendentals=0),
        name="input",
    )(slope, d_pooled, ends, taps)

def tail_kernel(received, along, turned, hidden_up, inverse, kept, projection, slope, d_pooled, sketch, edges):
    patches, channels = slope.shape
    grads = jnp.sum(received[...], axis=0)[:, :2 * OP]
    inner = jnp.sum(grads * along[...], axis=1, keepdims=True)
    scale = inverse[:, :1]
    both = jnp.dot(grads, turned[...], precision=highest, preferred_element_type=f32)
    scaled = (scale * both - scale * scale * scale * inner * hidden_up[...]) * (1.0 / POOL)
    d_pooled[...] = scaled
    bins = kept.shape[0]
    total = scaled[0:1] * kept[0]
    for n in range(1, bins):
        total = total + scaled[n:n + 1] * kept[n]
    part = jnp.dot(total, projection[...], precision=highest, preferred_element_type=f32)
    sketch[...] = jnp.broadcast_to(part[None], sketch.shape)
    edges[:PAD, :] = (scaled[:1] * slope[:PAD, :].astype(f32)).astype(bf16)
    edges[PAD:, :] = (scaled[bins - 1:] * slope[patches - PAD:, :].astype(f32)).astype(bf16)


def tail_stage(received, along, turned, hidden_up, inverse, kept, projection, slope, fan):
    vmem = pl.BlockSpec(memory_space=pltpu.VMEM)
    bins, channels = hidden_up.shape
    return pl.pallas_call(
        tail_kernel,
        out_shape=[
            jax.ShapeDtypeStruct((bins, channels), f32),
            jax.ShapeDtypeStruct((fan, kept.shape[1], projection.shape[1]), f32),
            jax.ShapeDtypeStruct((2 * PAD, channels), bf16),
        ],
        in_specs=[vmem] * 8,
        out_specs=[vmem] * 3,
        compiler_params=pltpu.CompilerParams(vmem_limit_bytes=24 << 20),
        cost_estimate=pl.CostEstimate(flops=20_000_000, bytes_accessed=4_000_000, transcendentals=0),
        name="tail",
    )(received, along, turned, hidden_up, inverse, kept, projection, slope)


def to_neighbours(head, tail, axes):
    count = lax.axis_size(axes)
    ends = count - 1
    before = lax.ppermute(tail, axes, [(i, i + 1) for i in range(ends)])
    behind = lax.ppermute(head, axes, [(i + 1, i) for i in range(ends)])
    return before, behind


def one_hot(bases):
    return (
        (bases[:, :, None] == jnp.arange(4, dtype=jnp.int32))
        .astype(bf16)
        .reshape(bases.shape[0], PATCH * 4)
    )


def shards(
    tokens,
    stem_weight,
    conv_weight,
    conv_bias,
    up_weight,
    norm_gain,
    pair_weight,
    out_weight,
    cotangent,
    projection,
    buckets,
):
    channels = conv_weight.shape[1]
    wide_channels = up_weight.shape[1]
    kernel = conv_weight.shape[0] // channels
    reach = (kernel - 1) // 2
    patches = tokens.shape[1] // PATCH
    bins = patches // POOL
    line = ("seq", "col")
    count = lax.axis_size(line)
    where = jnp.stack([lax.axis_index("seq"), lax.axis_index("col")]).astype(jnp.int32)

    edge = reach * PATCH
    ahead, behind = to_neighbours(
        one_hot(tokens[0, :edge].reshape(reach, PATCH)),
        one_hot(tokens[0, -edge:].reshape(reach, PATCH)),
        line,
    )
    spread_ends = jnp.pad(jnp.concatenate([ahead, behind], axis=0), ((PAD - reach, PAD - reach), (0, 0)))
    padded, slope, hidden, inverse, parts = forward_stage(
        tokens[0].reshape(-1, LANES),
        spread_ends,
        stem_weight,
        conv_weight,
        conv_bias[None],
        up_weight,
        norm_gain[None],
        pair_weight.T,
        count,
    )
    parts = lax.all_to_all(parts, line, 0, 0, tiled=True)
    member = (
        buckets.reshape(kernel, 1, channels)
        == jnp.arange(BUCKETS, dtype=jnp.int32)[None, :, None]
    ).astype(bf16)
    tapped = lax.dot_general(
        member.reshape(kernel * BUCKETS, channels), padded, NT, preferred_element_type=f32
    )
    mixed = sum(
        tapped[k * BUCKETS : (k + 1) * BUCKETS, PAD - reach + k : PAD - reach + k + patches]
        for k in range(kernel)
    )
    mixed_hi, mixed_lo = split(mixed)
    mixed_both = jnp.concatenate([mixed_hi, mixed_lo], axis=0).reshape(2 * BUCKETS, bins, POOL)
    slopes = slope.reshape(bins, POOL, channels)
    kept = jnp.einsum("mnt,nto->nmo", mixed_both, slopes, preferred_element_type=f32)
    kept = kept[:, :BUCKETS] + kept[:, BUCKETS:]

    scaled_pair = pair_weight.astype(f32).T * norm_gain
    through = lax.dot_general(
        jnp.concatenate([split_rows(scaled_pair), split_rows(hidden)], axis=0),
        up_weight,
        NT,
        preferred_element_type=f32,
    )
    turned = through[: 2 * OP] + through[2 * OP : 4 * OP]
    hidden_up = through[4 * OP : 4 * OP + bins] + through[4 * OP + bins :]
    along = lax.dot_general(hidden, scaled_pair, NT, precision=highest)
    wide = out_weight.reshape(OP, OP * out_weight.shape[1])

    sent = pair_stage(where, parts, cotangent[0], wide)
    received = lax.all_to_all(sent, line, 0, 0, tiled=True)
    d_pooled, sketch, edges = tail_stage(
        received, along / wide_channels, turned, hidden_up, inverse, kept, projection, slope,
        lax.axis_size("seq"),
    )
    sketch = jnp.sum(lax.all_to_all(sketch, "seq", 0, 0, tiled=True), axis=0)
    col_count = lax.axis_size("col")
    batches = lax.axis_size("batch")
    every = lax.all_to_all(
        jnp.broadcast_to(sketch[None], (batches * col_count,) + sketch.shape),
        ("batch", "col"),
        0,
        0,
        tiled=True,
    )
    sketches = jnp.sum(every.reshape(batches, col_count, *sketch.shape), axis=1)
    units = sketches * lax.rsqrt(
        jnp.mean(sketches * sketches, axis=(1, 2), keepdims=True) + 1e-06
    )
    own = lax.dynamic_slice_in_dim(units, lax.axis_index("batch"), 1, 0)
    embedding = own - jnp.sum(units, axis=0, keepdims=True) / batches

    ahead, behind = to_neighbours(edges[:reach], edges[-reach:], line)
    grad_ends = jnp.pad(jnp.concatenate([ahead, behind], axis=0), ((PAD - reach, PAD - reach), (0, 0)))
    input_grad = input_stage(slope, d_pooled, grad_ends, conv_weight)
    return (input_grad[None], embedding)


def solution(mesh):
    in_specs = (
        P("batch", ("seq", "col")),
        P(),
        P(),
        P(),
        P(),
        P(),
        P(),
        P(),
        P("batch", "seq", "col", None),
        P(),
        P(),
    )
    out_specs = (P("batch", ("seq", "col"), None), P("batch", None, None))
    return jax.shard_map(shards, mesh=mesh, in_specs=in_specs, out_specs=out_specs, check_vma=False)
```

time: 927 us -> 113 us (0.12); the launches traced: 916 us -> 112 us
  blocking collectives: 517 us -> 0 us
  waiting for transfers between devices: 216 us -> 19.1 us
  matrix products: 118 us -> 3.56 us
  Pallas kernels: 0 us -> 22.7 us
  starting transfers between devices: 22.9 us -> 45.3 us
  between operations: 15.8 us -> 0.86 us
    psum x2 -> x0, blocking collectives: 325 us -> none  [the longest x1 320 us: shards(): lax.psum(jnp.dot(member, projected, precision=highest), ('seq', 'col'))]
    unnamed x1 -> x0, blocking collectives: 192 us -> none
    reduce_scatter x1 -> x0, waiting for transfers between devices: 141 us -> none  [shards(): lax.psum_scatter(placed, ('seq', 'col'), scatter_dimension=0, tiled=True)]
    dot_general x24 -> x4, matrix products: 118 us -> 3.56 us  [the longest x1 1.52 us: shards(): jnp.einsum('mnt,nto->nmo', mixed_both, slopes, preferred_element_type=f32)]
    all_gather x1 -> x0, waiting for transfers between devices: 73.3 us -> none  [shards(): every = lax.all_gather(normed, ('seq', 'col'), axis=0, tiled=True)]
    all_to_all x0 -> x4, starting transfers between devices: none -> 30.9 us  [the longest x1 12.2 us: shards(): parts = lax.all_to_all(parts, line, 0, 0, tiled=True)]
    pallas_call x0 -> x4, Pallas kernels: none -> 22.7 us  [the longest x1 10.4 us: forward_stage(): pl.pallas_call(functools.partial(forward_kernel, chunk), out_shape=[jax.S...]
    all_to_all x0 -> x4, waiting for transfers between devices: none -> 18.4 us  [the longest x1 9.65 us: shards(): received = lax.all_to_all(sent, line, 0, 0, tiled=True)]
  transfers between devices with their start and end apart: 10 -> 8, of which waited for: 3 -> 4; matrix products, arithmetic and copies ran while one was open for 22% -> 7% of each run, Pallas kernels for 0% -> 8%
where the time goes in v1:
time: 113 us; the launch traced here: 112 us
  starting transfers between devices  45.3 us (40%)
  Pallas kernels  22.7 us (20%)
  waiting for transfers between devices  19.1 us (17%)
  local copies, waits for them, and re-layouts  15.7 us (14%)
  other arithmetic  4.59 us (4%)
  matrix products  3.56 us (3%)
    all_to_all x1, starting transfers between devices, shards(): parts = lax.all_to_all(parts, line, 0, 0, tiled=True)  12.2 us
    unnamed x20, local copies, waits for them, and re-layouts  10.4 us
    pallas_call x1, Pallas kernels, forward_stage(): pl.pallas_call(functools.partial(forward_kernel, chunk), out_shape=[jax.S...  10.4 us
    all_to_all x1, waiting for transfers between devices, shards(): received = lax.all_to_all(sent, line, 0, 0, tiled=True)  9.65 us
    all_to_all x1, starting transfers between devices, shards(): lax.all_to_all(jnp.broadcast_to(sketch[None], (batches * col_count,) + sk...  9.57 us
    pallas_call x1, Pallas kernels, input_stage(): pl.pallas_call(functools.partial(input_kernel, chunk), out_shape=jax.Shap...  8.42 us
    ppermute x2, starting transfers between devices, to_neighbours(): behind = lax.ppermute(head, axes, [(i + 1, i) for i in range(ends)])  8.32 us
    all_to_all x1, waiting for transfers between devices, shards(): parts = lax.all_to_all(parts, line, 0, 0, tiled=True)  7.52 us
  transfers between devices with their start and end apart: 8, of which 4 were waited for; matrix products, arithmetic and copies ran while one was open for 7% of the time, Pallas kernels for 8%

profile of v1, /device:TPU:1, one launch (start us, length us, event | category | flops | bytes accessed | tf_op | source)
XLA Modules:
  0.0 111.8 jit_solution(12751953466805155512)
XLA Ops:
  0.6 0.8 slice_reduce_fusion.1
  2.0 3.9 %collective-permute-start = (bf16[2,64]{1,0:T(2,128)(2,1)S(1)}, bf16[2,64]{1,0:T(2,128)(2,1)S(1)}, u32[]{:S(2)}, u32[]{:S(2)}) collective-permute-start(bf16[2,64]{1,0:T(2,128)(2,1)S(1)} %get-tuple-element.30), channel_id=1, source_target_pairs={{0,2},{2,4},{4,6},{6,8},{8,10},{10,12},{12,14},{14,16},{16,18},{18... | collective-permute-start | bytes 776 | tf_op jit(solution)/shard_map/ppermute | solution.py:248
  5.9 3.7 %collective-permute-start.1 = (bf16[2,64]{1,0:T(2,128)(2,1)S(1)}, bf16[2,64]{1,0:T(2,128)(2,1)S(1)}, u32[]{:S(2)}, u32[]{:S(2)}) collective-permute-start(bf16[2,64]{1,0:T(2,128)(2,1)S(1)} %get-tuple-element.31), channel_id=1, source_target_pairs={{2,0},{4,2},{6,4},{8,6},{10,8},{12,10},{14,12},{16,14},{18,16},{20... | collective-permute-start | bytes 776 | tf_op jit(solution)/shard_map/ppermute | solution.py:249
  11.1 0.7 eq.77
  11.8 1.0 reduce-precision_convert_fusion
  13.0 1.1 reshape.49.wide
  14.2 0.9 copy-done.1
  15.2 0.8 copy-done.3
  16.0 2.7 %copy-done.4 = bf16[3840,768]{1,0:T(8,128)(2,1)S(1)} copy-done((bf16[3840,768]{1,0:T(8,128)(2,1)S(1)}, bf16[3840,768]{1,0:T(8,128)(2,1)}, u32[]{:S(2)}) %copy-start.4) | copy-done | bytes 5898264
  18.7 1.7 %copy-done.6 = bf16[768,1536]{1,0:T(8,128)(2,1)S(1)} copy-done((bf16[768,1536]{1,0:T(8,128)(2,1)S(1)}, bf16[768,1536]{1,0:T(8,128)(2,1)}, u32[]{:S(2)}) %copy-start.6) | copy-done | bytes 2359320
  20.3 0.9 copy-done.7
  21.2 10.4 %forward.1 = (bf16[1040,768]{1,0:T(8,128)(2,1)S(1)}, bf16[1024,768]{1,0:T(8,128)(2,1)S(1)}, f32[8,1536]{1,0:T(8,128)S(1)}, f32[8,128]{1,0:T(8,128)S(1)}, bf16[64,8,128]{2,1,0:T(8,128)(2,1)}) custom-call(s32[128,128]{1,0:T(8,128)S(1)} %bitcast.31, bf16[16,64]{1,0:T(8,128)(2,1)S(1)} %fusion.22.ends, bf16[64,768]{1,0:T(8,128)(2,1)S(1)} %copy-done.7, ...), custom_call_target="tpu_custom_call" | custom-call | flops 6200000000 | bytes 14000000 | tf_op jit(solution)/shard_map/forward/pallas_call | solution.py:149
  32.0 0.7 fusion.26
  33.1 0.9 fusion
  34.0 0.8 copy-done.8
  34.8 12.2 %all-to-all-start = ((bf16[64,8,128]{2,1,0:T(8,128)(2,1)}), bf16[64,8,128]{2,1,0:T(8,128)(2,1)S(1)}, u32[]{:S(2)}, u32[]{:S(2)}) async-start(bf16[64,8,128]{2,1,0:T(8,128)(2,1)} %get-tuple-element.11), calls=%async_computation | async-start | bytes 262144 | tf_op jit(solution)/shard_map/all_to_all | solution.py:302
  47.0 1.5 %fusion.11 = f32[8,64,768]{2,1,0:T(8,128)} fusion(bf16[8,128,768]{2,1,0:T(8,128)(2,1)S(1)} %bitcast.28, bf16[32,1024]{1,0:T(8,128)(2,1)S(1)} %fusion.10, bf16[32,1024]{1,0:T(8,128)(2,1)S(1)} %get-tuple-element.22), kind=kOutput, calls=%fused_computation.20 | convolution fusion | flops 100925440 | bytes 3276800 | tf_op jit(solution)/shard_map/mnt,nto->nmo/dot_general | solution.py:317
  48.5 0.8 slice_add_fusion.6.hidden_up
  49.2 7.5 %all-to-all-done.parts = bf16[64,8,128]{2,1,0:T(8,128)(2,1)S(1)} async-done(((bf16[64,8,128]{2,1,0:T(8,128)(2,1)}), bf16[64,8,128]{2,1,0:T(8,128)(2,1)S(1)}, u32[]{:S(2)}, u32[]{:S(2)}) %all-to-all-start) | async-done | bytes 131104 | tf_op jit(solution)/shard_map/all_to_all | solution.py:302
  56.8 2.6 %pair.1 = f32[64,8,128]{2,1,0:T(8,128)} custom-call(s32[2]{0:T(128)S(1)} %pad_add_fusion.where, bf16[64,8,128]{2,1,0:T(8,128)(2,1)S(1)} %all-to-all-done.parts, bf16[32,128,128]{2,1,0:T(8,128)(2,1)S(1)} %bitcast.29, bf16[32,4096]{1,0:T(8,128)(2,1)S(1)} %reshape.49.wide), custom_call_target="tpu_custom_call" | custom-call | flops 200000000 | bytes 2000000 | tf_op jit(solution)/shard_map/pair/pallas_call | solution.py:75
  59.4 4.9 %all-to-all-start.1 = ((f32[64,8,128]{2,1,0:T(8,128)}), f32[64,8,128]{2,1,0:T(8,128)S(1)}, u32[]{:S(2)}, u32[]{:S(2)}) async-start(f32[64,8,128]{2,1,0:T(8,128)} %pair.1), calls=%async_computation.1 | async-start | bytes 524288 | tf_op jit(solution)/shard_map/all_to_all | solution.py:333
  64.3 1.5 %slice_add_fusion.kept = f32[8,32,768]{2,1,0:T(8,128)S(1)} fusion(f32[8,64,768]{2,1,0:T(8,128)} %fusion.11), kind=kLoop, calls=%fused_computation.1 | loop fusion | flops 196608 | bytes 2359296 | tf_op jit(solution)/shard_map/add | solution.py:318
  65.7 9.7 %all-to-all-done.1.received = f32[64,8,128]{2,1,0:T(8,128)S(1)} async-done(((f32[64,8,128]{2,1,0:T(8,128)}), f32[64,8,128]{2,1,0:T(8,128)S(1)}, u32[]{:S(2)}, u32[]{:S(2)}) %all-to-all-start.1) | async-done | bytes 262176 | tf_op jit(solution)/shard_map/all_to_all | solution.py:333
  75.4 1.3 %tail.1 = (f32[8,768]{1,0:T(8,128)S(1)}, f32[16,32,128]{2,1,0:T(8,128)}, bf16[16,768]{1,0:T(8,128)(2,1)S(1)}) custom-call(f32[64,8,128]{2,1,0:T(8,128)S(1)} %all-to-all-done.1.received, f32[8,64]{1,0:T(8,128)S(1)} %convolution_multiply_fusion.along, f32[64,768]{1,0:T(8,128)S(1)} %slice_add_fusion.1.turned, f32[8,768]{1,0:T(8,128)S(1)} %slice_add_fusion.6.hidden_up, ...), custom_call_target="tpu_custom_call" | custom-call | flops 20000000 | bytes 4000000 | tf_op jit(solution)/shard_map/tail/pallas_call | solution.py:230
  76.7 4.2 %all-to-all-start.2 = ((f32[16,32,128]{2,1,0:T(8,128)}), f32[16,32,128]{2,1,0:T(8,128)S(1)}, u32[]{:S(2)}, u32[]{:S(2)}) async-start(f32[16,32,128]{2,1,0:T(8,128)} %get-tuple-element.17), calls=%async_computation.2 | async-start | bytes 524288 | tf_op jit(solution)/shard_map/all_to_all | solution.py:338
  80.9 2.2 %collective-permute-start.2 = (bf16[2,768]{1,0:T(2,128)(2,1)S(1)}, bf16[2,768]{1,0:T(2,128)(2,1)S(1)}, u32[]{:S(2)}, u32[]{:S(2)}) collective-permute-start(bf16[2,768]{1,0:T(2,128)(2,1)S(1)} %get-tuple-element.28), channel_id=1, source_target_pairs={{0,2},{2,4},{4,6},{6,8},{8,10},{10,12},{12,14},{14,16},{16,18},{18... | collective-permute-start | bytes 9224 | tf_op jit(solution)/shard_map/ppermute | solution.py:248
  83.1 4.6 %collective-permute-start.3 = (bf16[2,768]{1,0:T(2,128)(2,1)S(1)}, bf16[2,768]{1,0:T(2,128)(2,1)S(1)}, u32[]{:S(2)}, u32[]{:S(2)}) collective-permute-start(bf16[2,768]{1,0:T(2,128)(2,1)S(1)} %get-tuple-element.29), channel_id=1, source_target_pairs={{2,0},{4,2},{6,4},{8,6},{10,8},{12,10},{14,12},{16,14},{18,16},{20... | collective-permute-start | bytes 9224 | tf_op jit(solution)/shard_map/ppermute | solution.py:249
  87.7 0.7 collective-permute-done.3
  88.5 1.2 %all-to-all-done.2 = f32[16,32,128]{2,1,0:T(8,128)S(1)} async-done(((f32[16,32,128]{2,1,0:T(8,128)}), f32[16,32,128]{2,1,0:T(8,128)S(1)}, u32[]{:S(2)}, u32[]{:S(2)}) %all-to-all-start.2) | async-done | bytes 262176 | tf_op jit(solution)/shard_map/all_to_all | solution.py:338
  90.4 9.6 %all-to-all-start.3 = ((f32[8,32,128]{2,1,0:T(8,128)}), f32[8,32,128]{2,1,0:T(8,128)S(1)}, u32[]{:S(2)}, u32[]{:S(2)}) async-start(f32[8,32,128]{2,1,0:T(8,128)} %broadcast_in_dim.11), calls=%async_computation.3 | async-start | bytes 262144 | tf_op jit(solution)/shard_map/all_to_all | solution.py:341
  99.9 2.7 %copy-done.5 = bf16[3840,768]{1,0:T(8,128)(2,1)S(1)} copy-done((bf16[3840,768]{1,0:T(8,128)(2,1)S(1)}, bf16[3840,768]{1,0:T(8,128)(2,1)}, u32[]{:S(2)}) %copy-start.5) | copy-done | bytes 5898264
  102.6 8.4 %input.2 = bf16[1024,768]{1,0:T(8,128)(2,1)} custom-call(bf16[1024,768]{1,0:T(8,128)(2,1)S(1)} %get-tuple-element.10.slope, f32[8,768]{1,0:T(8,128)S(1)} %get-tuple-element.15.d_pooled, bf16[16,768]{1,0:T(8,128)(2,1)S(1)} %fusion.18.ends, bf16[3840,768]{1,0:T(8,128)(2,1)S(1)} %copy-done.5), custom_call_target="tpu_custom_call" | custom-call | flops 6200000000 | bytes 10000000 | tf_op jit(solution)/shard_map/input/pallas_call | solution.py:196
  (47 shorter events, 4.5 us)
Async XLA Ops:
  2.0 12.2 %collective-permute-start = (bf16[2,64]{1,0:T(2,128)(2,1)S(1)}, bf16[2,64]{1,0:T(2,128)(2,1)S(1)}, u32[]{:S(2)}, u32[]{:S(2)}) collective-permute-start(bf16[2,64]{1,0:T(2,128)(2,1)S(1)} %get-tuple-element.30), channel_id=1, source_target_pairs={{0,2},{2,4},{4,6},{6,8},{8,10},{10,12},{12,14},{14,16},{16,18},{18... | collective-permute-start | bytes 776 | tf_op jit(solution)/shard_map/ppermute | solution.py:248
  5.9 8.3 %collective-permute-start.1 = (bf16[2,64]{1,0:T(2,128)(2,1)S(1)}, bf16[2,64]{1,0:T(2,128)(2,1)S(1)}, u32[]{:S(2)}, u32[]{:S(2)}) collective-permute-start(bf16[2,64]{1,0:T(2,128)(2,1)S(1)} %get-tuple-element.31), channel_id=1, source_target_pairs={{2,0},{4,2},{6,4},{8,6},{10,8},{12,10},{14,12},{16,14},{18,16},{20... | collective-permute-start | bytes 776 | tf_op jit(solution)/shard_map/ppermute | solution.py:249
  14.2 0.9 copy-start.1
  15.2 0.8 copy-start.3
  16.0 2.7 %copy-start.4 = (bf16[3840,768]{1,0:T(8,128)(2,1)S(1)}, bf16[3840,768]{1,0:T(8,128)(2,1)}, u32[]{:S(2)}) copy-start(bf16[3840,768]{1,0:T(8,128)(2,1)} %taps.3) | copy-start | bytes 17694724
  18.7 1.7 %copy-start.6 = (bf16[768,1536]{1,0:T(8,128)(2,1)S(1)}, bf16[768,1536]{1,0:T(8,128)(2,1)}, u32[]{:S(2)}) copy-start(bf16[768,1536]{1,0:T(8,128)(2,1)} %up.1) | copy-start | bytes 7077892
  20.3 0.9 copy-start.7
  21.2 10.4 %copy-start.9 = (f32[1536]{0:T(1024)S(1)}, f32[1536]{0:T(1024)}, u32[]{:S(2)}) copy-start(f32[1536]{0:T(1024)} %param.16) | copy-start | bytes 18436
  34.0 0.8 copy-start.8
  34.8 22.0 %all-to-all-start = ((bf16[64,8,128]{2,1,0:T(8,128)(2,1)}), bf16[64,8,128]{2,1,0:T(8,128)(2,1)S(1)}, u32[]{:S(2)}, u32[]{:S(2)}) async-start(bf16[64,8,128]{2,1,0:T(8,128)(2,1)} %get-tuple-element.11), calls=%async_computation | async-start | bytes 262144 | tf_op jit(solution)/shard_map/all_to_all | solution.py:302
  46.9 9.8 %copy-start = (bf16[1,32,128,128]{3,2,1,0:T(8,128)(2,1)S(1)}, bf16[1,32,128,128]{3,2,1,0:T(8,128)(2,1)}, u32[]{:S(2)}) copy-start(bf16[1,32,128,128]{3,2,1,0:T(8,128)(2,1)} %param.19) | copy-start | bytes 3145732
  59.4 16.0 %copy-start.2 = (f32[768,128]{1,0:T(8,128)S(1)}, f32[768,128]{1,0:T(8,128)}, u32[]{:S(2)}) copy-start(f32[768,128]{1,0:T(8,128)} %projection.1) | copy-start | bytes 1179652
  59.4 16.0 %all-to-all-start.1 = ((f32[64,8,128]{2,1,0:T(8,128)}), f32[64,8,128]{2,1,0:T(8,128)S(1)}, u32[]{:S(2)}, u32[]{:S(2)}) async-start(f32[64,8,128]{2,1,0:T(8,128)} %pair.1), calls=%async_computation.1 | async-start | bytes 524288 | tf_op jit(solution)/shard_map/all_to_all | solution.py:333
  76.7 13.0 %all-to-all-start.2 = ((f32[16,32,128]{2,1,0:T(8,128)}), f32[16,32,128]{2,1,0:T(8,128)S(1)}, u32[]{:S(2)}, u32[]{:S(2)}) async-start(f32[16,32,128]{2,1,0:T(8,128)} %get-tuple-element.17), calls=%async_computation.2 | async-start | bytes 524288 | tf_op jit(solution)/shard_map/all_to_all | solution.py:338
  80.9 6.8 %collective-permute-start.2 = (bf16[2,768]{1,0:T(2,128)(2,1)S(1)}, bf16[2,768]{1,0:T(2,128)(2,1)S(1)}, u32[]{:S(2)}, u32[]{:S(2)}) collective-permute-start(bf16[2,768]{1,0:T(2,128)(2,1)S(1)} %get-tuple-element.28), channel_id=1, source_target_pairs={{0,2},{2,4},{4,6},{6,8},{8,10},{10,12},{12,14},{14,16},{16,18},{18... | collective-permute-start | bytes 9224 | tf_op jit(solution)/shard_map/ppermute | solution.py:248
  83.1 5.3 %collective-permute-start.3 = (bf16[2,768]{1,0:T(2,128)(2,1)S(1)}, bf16[2,768]{1,0:T(2,128)(2,1)S(1)}, u32[]{:S(2)}, u32[]{:S(2)}) collective-permute-start(bf16[2,768]{1,0:T(2,128)(2,1)S(1)} %get-tuple-element.29), channel_id=1, source_target_pairs={{2,0},{4,2},{6,4},{8,6},{10,8},{12,10},{14,12},{16,14},{18,16},{20... | collective-permute-start | bytes 9224 | tf_op jit(solution)/shard_map/ppermute | solution.py:249
  90.4 20.7 %all-to-all-start.3 = ((f32[8,32,128]{2,1,0:T(8,128)}), f32[8,32,128]{2,1,0:T(8,128)S(1)}, u32[]{:S(2)}, u32[]{:S(2)}) async-start(f32[8,32,128]{2,1,0:T(8,128)} %broadcast_in_dim.11), calls=%async_computation.3 | async-start | bytes 262144 | tf_op jit(solution)/shard_map/all_to_all | solution.py:341
  99.9 2.7 %copy-start.5 = (bf16[3840,768]{1,0:T(8,128)(2,1)S(1)}, bf16[3840,768]{1,0:T(8,128)(2,1)}, u32[]{:S(2)}) copy-start(bf16[3840,768]{1,0:T(8,128)(2,1)} %taps.3) | copy-start | bytes 17694724

commit v2 on v1

v2 whole, which is shorter than its diff:
```python
import functools
import jax
import jax.numpy as jnp
from jax import lax
from jax.experimental import pallas as pl
from jax.experimental.pallas import tpu as pltpu
from jax.sharding import PartitionSpec as P


OP = 32
PATCH = 16
POOL = 128
BUCKETS = 32
LANES = 128
PAD = 8
ROOT = 0.7978845608028654
CUBIC = 0.044715

f32 = jnp.float32
bf16 = jnp.bfloat16
NT = (((1,), (1,)), ((), ()))
highest = lax.Precision.HIGHEST
HBM = pl.BlockSpec(memory_space=pl.ANY)
FULL = 67_000_000
MOST = 60 * 1024 * 1024


def split_in_kernel(x):
    hi = x.astype(bf16)
    return hi, (x - hi.astype(f32)).astype(bf16)


def pair_kernel(where, parts, cot, wide, out, moved):
    rows, cols, _ = cot.shape
    bins = parts.shape[1]
    seq, col = where[0], where[1]
    mine = parts[pl.ds(seq * (rows // bins), rows // bins)].astype(f32).reshape(rows, LANES)
    left = mine[:, :OP].astype(bf16)
    other = parts[pl.ds(col * (cols // bins), cols // bins)].astype(f32).reshape(cols, LANES)
    right = other.T[OP : 2 * OP].astype(bf16)
    grid = jnp.concatenate([cot[i] for i in range(rows)], axis=1)
    weighted = jnp.dot(left, wide[...], preferred_element_type=f32)
    for l in range(OP):
        moved[pl.ds(l, rows, stride=OP), :] = weighted[:, l * LANES : (l + 1) * LANES]
    stacked = jnp.concatenate([moved[i * OP : (i + 1) * OP, :] for i in range(rows)], axis=1)
    hi, lo = split_in_kernel(stacked)
    both = lax.dot_general(
        grid, jnp.concatenate([hi, lo], axis=0), NT, preferred_element_type=f32
    )
    grad_right = both[:, :OP] + both[:, OP:]
    summed = jnp.dot(right, grid, preferred_element_type=f32)
    for i in range(rows):
        moved[i * OP : (i + 1) * OP, :] = summed[:, i * LANES : (i + 1) * LANES]
    by_row = jnp.concatenate([moved[pl.ds(l, rows, stride=OP), :] for l in range(OP)], axis=1)
    hi, lo = split_in_kernel(by_row)
    both = lax.dot_general(
        jnp.concatenate([hi, lo], axis=0), wide[...], NT, preferred_element_type=f32
    )
    grad_left = both[:rows] + both[rows:]
    out[...] = jnp.zeros_like(out)
    out[pl.ds(seq * (rows // bins), rows // bins), :, :OP] = grad_left.reshape(-1, bins, OP)
    out[pl.ds(col * (cols // bins), cols // bins), :, OP : 2 * OP] = grad_right.reshape(
        -1, bins, OP
    )


def pair_stage(where, parts, cot, wide):
    vmem = pl.BlockSpec(memory_space=pltpu.VMEM)
    return pl.pallas_call(
        pair_kernel,
        out_shape=jax.ShapeDtypeStruct(parts.shape, f32),
        in_specs=[pl.BlockSpec(memory_space=pltpu.SMEM), vmem, vmem, vmem],
        out_specs=vmem,
        scratch_shapes=[pltpu.VMEM((cot.shape[0] * OP, LANES), f32)],
        compiler_params=pltpu.CompilerParams(vmem_limit_bytes=32 << 20),
        cost_estimate=pl.CostEstimate(flops=200_000_000, bytes_accessed=2_000_000, transcendentals=0),
        name="pair",
    )(where, parts, cot, wide)


def iota(shape, dim): return lax.broadcasted_iota(jnp.int32, shape, dim)


def forward_kernel(chunk, *refs):
    sources = refs[:8]
    spread, slope, parts, hidden_out, inverse_out, rim = refs[8:14]
    tokens, ends, stem, taps, bias, up, gain, pair = refs[14:22]
    cells, unfolded, pools, spread_here, slope_here, parts_here, sems = refs[22:]
    copies = [
        pltpu.make_async_copy(source, here, sems.at[j])
        for j, (source, here) in enumerate(zip(sources, refs[14:22]))
    ]
    for copy in copies:
        copy.start()
    patches = slope.shape[0]
    per = LANES // PATCH
    channels = stem.shape[1]
    blocks = channels // LANES
    kernel = taps.shape[0] // channels
    reach = (kernel - 1) // 2
    t = iota((patches, LANES), 0)
    lane = iota((patches, LANES), 1)
    repeat = (t // per == lane).astype(bf16)
    fold = (iota((LANES, 4 * PATCH), 0) % PATCH == iota((LANES, 4 * PATCH), 1) // 4).astype(bf16)
    copies[0].wait()
    bases = tokens[...].astype(f32).astype(bf16)
    rows = jnp.dot(repeat, bases, preferred_element_type=f32)
    own = jnp.where(lane // PATCH == t % per, rows + 1.0, 0.0).astype(bf16)
    base = jnp.dot(own, fold, preferred_element_type=f32)
    onehot = (base == (iota((patches, 4 * PATCH), 1) % 4 + 1).astype(f32)).astype(f32).astype(bf16)
    copies[1].wait()
    copies[2].wait()
    main = jnp.dot(onehot, stem[...], preferred_element_type=f32).astype(bf16)
    edges = jnp.dot(ends[...], stem[...], preferred_element_type=f32).astype(bf16)
    spread_here[:PAD, :] = edges[:PAD]
    spread_here[PAD : PAD + patches, :] = main
    spread_here[PAD + patches :, :] = edges[PAD:]
    wide = main.astype(f32)
    edges = edges.astype(f32)
    for c in range(blocks):
        at = slice(c * LANES, (c + 1) * LANES)
        cells[c, :PAD, :] = edges[:PAD, at]
        cells[c, PAD : PAD + patches, :] = wide[:, at]
        cells[c, PAD + patches :, :] = edges[PAD:, at]
    outs = [pltpu.make_async_copy(spread_here, spread, sems.at[8])]
    outs[0].start()
    for r in range(patches // chunk):
        for k in range(kernel):
            for c in range(blocks):
                start = r * chunk + PAD - reach + k
                j = (k * blocks + c) * LANES
                unfolded[r % 2, :, j : j + LANES] = cells[c, start : start + chunk, :].astype(bf16)
        if r == 0:
            copies[3].wait()
            copies[4].wait()
        before = jnp.dot(unfolded[r % 2], taps[...], preferred_element_type=f32) + bias[...]
        square = before * before
        bent = jnp.tanh(before * (ROOT + ROOT * CUBIC * square))
        half = 0.5 * (1.0 + bent)
        after = before * half
        tilt = half + before * (0.5 - 0.5 * bent * bent) * (ROOT + 3.0 * ROOT * CUBIC * square)
        slope_here[r * chunk : (r + 1) * chunk, :] = tilt.astype(bf16)
        out = pltpu.make_async_copy(
            slope_here.at[pl.ds(r * chunk, chunk)], slope.at[pl.ds(r * chunk, chunk)], sems.at[10 + r]
        )
        out.start()
        outs.append(out)
        for n in range(chunk // POOL):
            b = r * (chunk // POOL) + n
            pools[b : b + 1, :] = jnp.sum(
                after[n * POOL : (n + 1) * POOL], axis=0, keepdims=True
            ) * (1.0 / POOL)
    rim[:PAD, :] = slope_here[:PAD, :]
    rim[PAD:, :] = slope_here[patches - PAD :, :]
    for copy in copies[5:]:
        copy.wait()
    hidden = jnp.dot(pools[...].astype(bf16), up[...], preferred_element_type=f32)
    inverse = lax.rsqrt(jnp.mean(hidden * hidden, axis=1, keepdims=True) + 1e-06)
    normed = (hidden * inverse * gain[...]).astype(bf16)
    sides = lax.dot_general(normed, pair[...], NT, preferred_element_type=f32)
    full = jnp.concatenate([sides, jnp.zeros_like(sides)], axis=1).astype(bf16)
    parts_here[...] = jnp.broadcast_to(full[None], parts.shape)
    out = pltpu.make_async_copy(parts_here, parts, sems.at[9])
    out.start()
    outs.append(out)
    hidden_out[...] = hidden
    inverse_out[...] = jnp.broadcast_to(inverse, inverse_out.shape)
    for out in outs:
        out.wait()


def forward_stage(tokens, ends, stem, taps, bias, up, gain, pair, count, chunk=512):
    vmem = pl.BlockSpec(memory_space=pltpu.VMEM)
    patches = tokens.size // PATCH
    channels = stem.shape[1]
    bins = patches // POOL
    tall = patches + 2 * PAD
    inputs = (tokens, ends, stem, taps, bias, up, gain, pair)
    return pl.pallas_call(
        functools.partial(forward_kernel, chunk),
        out_shape=[
            jax.ShapeDtypeStruct((tall, channels), bf16),
            jax.ShapeDtypeStruct((patches, channels), bf16),
            jax.ShapeDtypeStruct((count, bins, LANES), bf16),
            jax.ShapeDtypeStruct((bins, up.shape[1]), f32),
            jax.ShapeDtypeStruct((bins, LANES), f32),
            jax.ShapeDtypeStruct((2 * PAD, channels), bf16),
        ],
        in_specs=[HBM] * 8,
        out_specs=[HBM] * 3 + [vmem] * 3,
        scratch_shapes=[pltpu.VMEM(x.shape, x.dtype) for x in inputs]
        + [
            pltpu.VMEM((channels // LANES, tall, LANES), f32),
            pltpu.VMEM((2, chunk, taps.shape[0]), bf16),
            pltpu.VMEM((bins, channels), f32),
            pltpu.VMEM((tall, channels), bf16),
            pltpu.VMEM((patches, channels), bf16),
            pltpu.VMEM((count, bins, LANES), bf16),
            pltpu.SemaphoreType.DMA((10 + patches // chunk,)),
        ],
        compiler_params=pltpu.CompilerParams(vmem_limit_bytes=FULL),
        cost_estimate=pl.CostEstimate(
            flops=6_200_000_000, bytes_accessed=14_000_000, transcendentals=800_000
        ),
        name="forward",
    )(*inputs)


def input_rows(segments, fills, source, d_pooled, ends, taps, out, cells, shifted, taps_here, block, slope, sems):
    patches, channels = slope.shape
    first = pltpu.make_async_copy(source, slope, sems.at[sems.shape[0] - 1])
    first.start()
    blocks = channels // LANES
    kernel = taps.shape[0] // channels
    reach = (kernel - 1) // 2
    copies = [
        pltpu.make_async_copy(
            taps.at[pl.ds(k * channels, channels)],
            taps_here.at[pl.ds(k * channels, channels)],
            sems.at[k],
        )
        for k in range(kernel)
    ]
    for copy in copies:
        copy.start()
    first.wait()
    for c in range(blocks):
        at = slice(c * LANES, (c + 1) * LANES)
        if ends is not None:
            cells[c, :PAD, :] = ends[:PAD, at].astype(f32)
            cells[c, PAD + patches :, :] = ends[PAD:, at].astype(f32)
        for low, high in fills:
            n = low // POOL
            cells[c, PAD + low : PAD + high, :] = (
                slope[low:high, at].astype(f32) * d_pooled[n : n + 1, at]
            )
    total = None
    for k in range(kernel):
        at = 0
        for low, rows in segments:
            start = low + PAD + reach - k
            for c in range(blocks):
                shifted[k % 2, at : at + rows, c * LANES : (c + 1) * LANES] = cells[
                    c, start : start + rows, :
                ].astype(bf16)
            at += rows
        copies[k].wait()
        term = lax.dot_general(
            shifted[k % 2],
            taps_here[k * channels : (k + 1) * channels, :],
            NT,
            preferred_element_type=f32,
        )
        total = term if total is None else total + term
    block[...] = total.astype(bf16)
    at = 0
    backs = []
    for j, (low, rows) in enumerate(segments):
        backs.append(
            pltpu.make_async_copy(
                block.at[pl.ds(at, rows)], out.at[pl.ds(low, rows)], sems.at[kernel + j]
            )
        )
        at += rows
    for back in backs:
        back.start()
    for back in backs:
        back.wait()


def inner_kernel(segments, fills, slope, d_pooled, taps, out, *scratch):
    input_rows(segments, fills, slope, d_pooled, None, taps, out, *scratch)


def outer_kernel(segments, fills, slope, d_pooled, ends, taps, partial, out, *scratch):
    input_rows(segments, fills, slope, d_pooled, ends, taps, out, *scratch)


def input_scratch(rows, slope, taps):
    patches, channels = slope.shape
    kernel = taps.shape[0] // channels
    return [
        pltpu.VMEM((channels // LANES, patches + 2 * PAD, LANES), f32),
        pltpu.VMEM((2, rows, channels), bf16),
        pltpu.VMEM(taps.shape, bf16),
        pltpu.VMEM((rows, channels), bf16),
        pltpu.VMEM(slope.shape, bf16),
        pltpu.SemaphoreType.DMA((kernel + 3,)),
    ]


def inner_stage(slope, d_pooled, taps):
    vmem = pl.BlockSpec(memory_space=pltpu.VMEM)
    patches, channels = slope.shape
    bins = patches // POOL
    rows = patches - 2 * POOL
    fills = [(POOL - 16, POOL)]
    fills += [(n * POOL, (n + 1) * POOL) for n in range(1, bins - 1)]
    fills += [(patches - POOL, patches - POOL + 16)]
    return pl.pallas_call(
        functools.partial(inner_kernel, [(POOL, rows)], fills),
        out_shape=jax.ShapeDtypeStruct((patches, channels), bf16),
        in_specs=[HBM, vmem, HBM],
        out_specs=HBM,
        scratch_shapes=input_scratch(rows, slope, taps),
        compiler_params=pltpu.CompilerParams(vmem_limit_bytes=MOST),
        cost_estimate=pl.CostEstimate(
            flops=4_600_000_000, bytes_accessed=9_000_000, transcendentals=0
        ),
        name="inner",
    )(slope, d_pooled, taps)


def outer_stage(slope, d_pooled, ends, taps, partial):
    vmem = pl.BlockSpec(memory_space=pltpu.VMEM)
    patches, channels = slope.shape
    far = patches - POOL
    fills = [(0, POOL), (POOL, POOL + 16), (far - 16, far), (far, patches)]
    return pl.pallas_call(
        functools.partial(outer_kernel, [(0, POOL), (far, POOL)], fills),
        out_shape=jax.ShapeDtypeStruct((patches, channels), bf16),
        in_specs=[HBM, vmem, vmem, HBM, HBM],
        out_specs=HBM,
        scratch_shapes=input_scratch(2 * POOL, slope, taps),
        input_output_aliases={4: 0},
        compiler_params=pltpu.CompilerParams(vmem_limit_bytes=MOST),
        cost_estimate=pl.CostEstimate(
            flops=1_600_000_000, bytes_accessed=7_000_000, transcendentals=0
        ),
        name="outer",
    )(slope, d_pooled, ends, taps, partial)


def weights_kernel(hidden, pair, gain, up, turned, hidden_up, along, up_here, sems):
    _, wide = up.shape
    bins = hidden.shape[0]
    part = up_here.shape[0] // sems.shape[0]
    copies = [
        pltpu.make_async_copy(
            up.at[pl.ds(j * part, part)], up_here.at[pl.ds(j * part, part)], sems.at[j]
        )
        for j in range(sems.shape[0])
    ]
    for copy in copies:
        copy.start()
    scaled = pair[...].astype(f32) * gain[...]
    along[...] = lax.dot_general(
        hidden[...], scaled, NT, precision=highest, preferred_element_type=f32
    ) * (1.0 / wide)
    scaled_hi, scaled_lo = split_in_kernel(scaled)
    hidden_hi, hidden_lo = split_in_kernel(hidden[...])
    stacked = jnp.concatenate(
        [scaled_hi.astype(f32), scaled_lo.astype(f32), hidden_hi.astype(f32), hidden_lo.astype(f32)],
        axis=0,
    ).astype(bf16)
    for j, copy in enumerate(copies):
        copy.wait()
        at = slice(j * part, (j + 1) * part)
        through = lax.dot_general(stacked, up_here[at, :], NT, preferred_element_type=f32)
        turned[:, at] = through[: 2 * OP] + through[2 * OP : 4 * OP]
        hidden_up[:, at] = through[4 * OP : 4 * OP + bins] + through[4 * OP + bins :]


def weights_stage(hidden, pair, gain, up):
    vmem = pl.BlockSpec(memory_space=pltpu.VMEM)
    bins, _ = hidden.shape
    channels = up.shape[0]
    return pl.pallas_call(
        weights_kernel,
        out_shape=[
            jax.ShapeDtypeStruct((2 * OP, channels), f32),
            jax.ShapeDtypeStruct((bins, channels), f32),
            jax.ShapeDtypeStruct((bins, 2 * OP), f32),
        ],
        in_specs=[vmem, vmem, vmem, HBM],
        out_specs=[vmem] * 3,
        scratch_shapes=[pltpu.VMEM(up.shape, bf16), pltpu.SemaphoreType.DMA((3,))],
        compiler_params=pltpu.CompilerParams(vmem_limit_bytes=16 << 20),
        cost_estimate=pl.CostEstimate(
            flops=340_000_000, bytes_accessed=3_000_000, transcendentals=0
        ),
        name="weights",
    )(hidden, pair, gain, up)


def bins_kernel(buckets, spread, slope, kept):
    kernel, channels = buckets.shape
    patches = slope.shape[0]
    reach = (kernel - 1) // 2
    slots = iota((BUCKETS, channels), 0)
    member = jnp.concatenate(
        [(buckets[k : k + 1, :] == slots).astype(f32) for k in range(kernel)], axis=0
    ).astype(bf16)
    tapped = lax.dot_general(member, spread[...], NT, preferred_element_type=f32)
    mixed = None
    for k in range(kernel):
        start = PAD - reach + k
        term = tapped[k * BUCKETS : (k + 1) * BUCKETS, start : start + patches]
        mixed = term if mixed is None else mixed + term
    hi, lo = split_in_kernel(mixed)
    both = jnp.concatenate([hi, lo], axis=0)
    for n in range(patches // POOL):
        rows = slice(n * POOL, (n + 1) * POOL)
        part = jnp.dot(both[:, rows], slope[rows, :], preferred_element_type=f32)
        kept[n] = part[:BUCKETS] + part[BUCKETS:]


def bins_stage(buckets, spread, slope):
    vmem = pl.BlockSpec(memory_space=pltpu.VMEM)
    patches, channels = slope.shape
    return pl.pallas_call(
        bins_kernel,
        out_shape=jax.ShapeDtypeStruct((patches // POOL, BUCKETS, channels), f32),
        in_specs=[vmem] * 3,
        out_specs=vmem,
        compiler_params=pltpu.CompilerParams(vmem_limit_bytes=24 << 20),
        cost_estimate=pl.CostEstimate(
            flops=400_000_000, bytes_accessed=4_000_000, transcendentals=0
        ),
        name="bins",
    )(buckets, spread, slope)


def tail_kernel(received, along, turned, hidden_up, inverse, kept, projection, rim, d_pooled, sketch, edges):
    grads = jnp.sum(received[...], axis=0)[:, :2 * OP]
    inner = jnp.sum(grads * along[...], axis=1, keepdims=True)
    scale = inverse[:, :1]
    both = jnp.dot(grads, turned[...], precision=highest, preferred_element_type=f32)
    scaled = (scale * both - scale * scale * scale * inner * hidden_up[...]) * (1.0 / POOL)
    d_pooled[...] = scaled
    bins = kept.shape[0]
    total = scaled[0:1] * kept[0]
    for n in range(1, bins):
        total = total + scaled[n:n + 1] * kept[n]
    part = jnp.dot(total, projection[...], precision=highest, preferred_element_type=f32)
    sketch[...] = jnp.broadcast_to(part[None], sketch.shape)
    edges[:PAD, :] = (scaled[:1] * rim[:PAD, :].astype(f32)).astype(bf16)
    edges[PAD:, :] = (scaled[bins - 1:] * rim[PAD:, :].astype(f32)).astype(bf16)


def tail_stage(received, along, turned, hidden_up, inverse, kept, projection, rim, fan):
    vmem = pl.BlockSpec(memory_space=pltpu.VMEM)
    bins, channels = hidden_up.shape
    return pl.pallas_call(
        tail_kernel,
        out_shape=[
            jax.ShapeDtypeStruct((bins, channels), f32),
            jax.ShapeDtypeStruct((fan, kept.shape[1], projection.shape[1]), f32),
            jax.ShapeDtypeStruct((2 * PAD, channels), bf16),
        ],
        in_specs=[vmem] * 8,
        out_specs=[vmem] * 3,
        compiler_params=pltpu.CompilerParams(vmem_limit_bytes=24 << 20),
        cost_estimate=pl.CostEstimate(flops=20_000_000, bytes_accessed=4_000_000, transcendentals=0),
        name="tail",
    )(received, along, turned, hidden_up, inverse, kept, projection, rim)


def to_neighbours(head, tail, axes):
    count = lax.axis_size(axes)
    place = lax.axis_index(axes)
    even = place % 2 == 0
    inside = [(i, i ^ 1) for i in range(count)]
    across = [(0, 0), (count - 1, count - 1)] + [
        (i, i + 1 if i % 2 else i - 1) for i in range(1, count - 1)
    ]
    far = lax.ppermute(jnp.where(even, head, tail), axes, across)
    near = lax.ppermute(jnp.where(even, tail, head), axes, inside)
    before = jnp.where(even, far, near)
    behind = jnp.where(even, near, far)
    before = jnp.where(place > 0, before, jnp.zeros_like(before))
    behind = jnp.where(place < count - 1, behind, jnp.zeros_like(behind))
    reach = head.shape[0]
    return jnp.pad(
        jnp.concatenate([before, behind], axis=0), ((PAD - reach, PAD - reach), (0, 0))
    )


def one_hot(bases):
    return (
        (bases[:, :, None] == jnp.arange(4, dtype=jnp.int32))
        .astype(bf16)
        .reshape(bases.shape[0], PATCH * 4)
    )


def exchange(value, axes):
    return lax.all_to_all(value, axes, 0, 0, tiled=True)


def whole(
    tokens,
    stem_weight,
    conv_weight,
    conv_bias,
    up_weight,
    norm_gain,
    pair_weight,
    out_weight,
    cotangent,
    projection,
    buckets,
):
    channels = conv_weight.shape[1]
    kernel = conv_weight.shape[0] // channels
    reach = (kernel - 1) // 2
    line = ("seq", "col")
    count = lax.axis_size(line)
    where = jnp.stack([lax.axis_index("seq"), lax.axis_index("col")]).astype(jnp.int32)

    edge = reach * PATCH
    ends = to_neighbours(
        one_hot(tokens[0, :edge].reshape(reach, PATCH)),
        one_hot(tokens[0, -edge:].reshape(reach, PATCH)),
        line,
    )
    pair = pair_weight.T
    gain = norm_gain[None]
    spread, slope, parts, hidden, inverse, rim = forward_stage(
        tokens[0].reshape(-1, LANES), ends, stem_weight, conv_weight, conv_bias[None], up_weight,
        gain, pair, count,
    )
    parts = exchange(parts, line)
    turned, hidden_up, along = weights_stage(hidden, pair, gain, up_weight)
    wide = out_weight.reshape(OP, OP * out_weight.shape[1])
    sent = pair_stage(where, parts, cotangent[0], wide)
    received = exchange(sent, line)
    kept = bins_stage(buckets.reshape(kernel, channels), spread, slope)
    d_pooled, sketch, edges = tail_stage(
        received, along, turned, hidden_up, inverse, kept, projection, rim,
        lax.axis_size("seq"),
    )
    sketch = jnp.sum(exchange(sketch, "seq"), axis=0)
    partial = inner_stage(slope, d_pooled, conv_weight)
    grad_ends = to_neighbours(edges[:reach], edges[-reach:], line)
    col_count = lax.axis_size("col")
    batches = lax.axis_size("batch")
    every = exchange(
        jnp.broadcast_to(sketch[None], (batches * col_count,) + sketch.shape), ("batch", "col")
    )
    input_grad = outer_stage(slope, d_pooled, grad_ends, conv_weight, partial)
    sketches = jnp.sum(every.reshape(batches, col_count, *sketch.shape), axis=1)
    units = sketches * lax.rsqrt(
        jnp.mean(sketches * sketches, axis=(1, 2), keepdims=True) + 1e-06
    )
    own = lax.dynamic_slice_in_dim(units, lax.axis_index("batch"), 1, 0)
    embedding = own - jnp.sum(units, axis=0, keepdims=True) / batches
    return (input_grad[None], embedding)


def solution(mesh):
    in_specs = (
        P("batch", ("seq", "col")),
        P(),
        P(),
        P(),
        P(),
        P(),
        P(),
        P(),
        P("batch", "seq", "col", None),
        P(),
        P(),
    )
    out_specs = (P("batch", ("seq", "col"), None), P("batch", None, None))
    return jax.shard_map(whole, mesh=mesh, in_specs=in_specs, out_specs=out_specs, check_vma=False)
```

time: 113 us -> 102 us (0.903)
  Pallas kernels: 22.7 us -> 37.9 us
  starting transfers between devices: 45.3 us -> 37.6 us
  waiting for transfers between devices: 19.1 us -> 12.9 us
  local copies, waits for them, and re-layouts: 15.7 us -> 9.99 us
  matrix products: 3.56 us -> 0 us
  other arithmetic: 4.59 us -> 2.19 us
    pallas_call x1 -> x4, Pallas kernels: 8.42 us -> 21.4 us  [the longest x1 11.4 us: inner_stage(): pl.pallas_call(functools.partial(inner_kernel, [(POOL, rows)], fills), ou...]
    unnamed x20 -> x24, local copies, waits for them, and re-layouts: 10.4 us -> 4.34 us
    all_to_all x4, waiting for transfers between devices: 18.4 us -> 12.9 us  [exchange(): return lax.all_to_all(value, axes, 0, 0, tiled=True)]
    ppermute x4, starting transfers between devices: 14.5 us -> 9.28 us  [the longest x2 9.11 us: to_neighbours(): far = lax.ppermute(jnp.where(even, head, tail), axes, across)]
    dot_general x4 -> x0, matrix products: 3.56 us -> none  [the longest x1 1.52 us: shards(): jnp.einsum('mnt,nto->nmo', mixed_both, slopes, preferred_element_type=f32)]
    all_to_all x4, starting transfers between devices: 30.9 us -> 28.3 us  [exchange(): return lax.all_to_all(value, axes, 0, 0, tiled=True)]
    pallas_call x1, Pallas kernels: 10.4 us -> 12.7 us  [forward_stage(): pl.pallas_call(functools.partial(forward_kernel, chunk), out_shape=[jax.S...]
    add x3 -> x0, other arithmetic: 2.25 us -> none  [the longest x1 1.46 us: shards(): kept = kept[:, :BUCKETS] + kept[:, BUCKETS:]]
  transfers between devices with their start and end apart: 8 -> 8, of which waited for: 4 -> 2; matrix products, arithmetic and copies ran while one was open for 7% -> 4% of each run, Pallas kernels for 8% -> 21%
where the time goes in v2:
time: 102 us
  Pallas kernels  37.9 us (37%)
  starting transfers between devices  37.6 us (37%)
  waiting for transfers between devices  12.9 us (13%)
  local copies, waits for them, and re-layouts  9.99 us (10%)
  other arithmetic  2.19 us (2%)
    all_to_all x4, starting transfers between devices, exchange(): return lax.all_to_all(value, axes, 0, 0, tiled=True)  28.3 us
    all_to_all x4, waiting for transfers between devices, exchange(): return lax.all_to_all(value, axes, 0, 0, tiled=True)  12.9 us
    pallas_call x1, Pallas kernels, forward_stage(): pl.pallas_call(functools.partial(forward_kernel, chunk), out_shape=[jax.S...  12.7 us
    pallas_call x1, Pallas kernels, inner_stage(): pl.pallas_call(functools.partial(inner_kernel, [(POOL, rows)], fills), ou...  11.4 us
    ppermute x2, starting transfers between devices, to_neighbours(): far = lax.ppermute(jnp.where(even, head, tail), axes, across)  9.11 us
    pallas_call x1, Pallas kernels, outer_stage(): pl.pallas_call(functools.partial(outer_kernel, [(0, POOL), (far, POOL)],...  6.29 us
    unnamed x24, local copies, waits for them, and re-layouts  4.34 us
    pallas_call x1, Pallas kernels, pair_stage(): pl.pallas_call(pair_kernel, out_shape=jax.ShapeDtypeStruct(parts.shape, f...  2.58 us
  transfers between devices with their start and end apart: 8, of which 2 were waited for; matrix products, arithmetic and copies ran while one was open for 4% of the time, Pallas kernels for 21%

profile of v2, /device:TPU:1, one launch (start us, length us, event | category | flops | bytes accessed | tf_op | source)
XLA Modules:
  0.0 101.6 jit_solution(13082893204282534740)
XLA Ops:
  0.6 0.8 slice_reduce_fusion
  1.6 0.1 eq.56
  1.7 0.1 eq.54
  1.9 0.1 eq.61
  2.0 5.8 %collective-permute-start = (bf16[2,64]{1,0:T(2,128)(2,1)S(1)}, bf16[2,64]{1,0:T(2,128)(2,1)S(1)}, u32[]{:S(2)}, u32[]{:S(2)}) collective-permute-start(bf16[2,64]{1,0:T(2,128)(2,1)S(1)} %get-tuple-element.34), channel_id=1, source_target_pairs={{0,0},{126,126},{2,4},{4,2},{6,8},{8,6},{10,12},{12,10},{14,16},{1... | collective-permute-start | bytes 776 | tf_op jit(solution)/shard_map/ppermute | solution.py:467
  7.8 0.1 collective-permute-start.1
  7.9 1.3 %broadcast_in_dim.8.refs_4_ = f32[1,768]{1,0:T(1,128)} reshape(f32[768]{0:T(1024)} %param.14) | data formatting | bytes 6144 | tf_op jit(solution)/shard_map/broadcast_in_dim | solution.py:520
  9.2 1.3 %broadcast_in_dim.9.refs_6_.gain = f32[1,1536]{1,0:T(1,128)} reshape(f32[1536]{0:T(1024)} %param.16) | data formatting | bytes 12288 | tf_op jit(solution)/shard_map/broadcast_in_dim | solution.py:518
  10.5 0.6 fusion.7.refs_1_
  11.1 12.7 %forward.1 = (bf16[1040,768]{1,0:T(8,128)(2,1)}, bf16[1024,768]{1,0:T(8,128)(2,1)}, bf16[64,8,128]{2,1,0:T(8,128)(2,1)}, f32[8,1536]{1,0:T(8,128)}, f32[8,128]{1,0:T(8,128)}, /*index=5*/bf16[16,768]{1,0:T(8,128)(2,1)}) custom-call(s32[128,128]{1,0:T(8,128)} %bitcast.14, bf16[16,64]{1,0:T(8,128)(2,1)} %fusion.7.refs_1_, bf16[64,768]{1,0:T(8,128)(2,1)} %refs_2_.1, ...), custom_call_target="tpu_custom_call" | custom-call | flops 6200000000 | bytes 14000000 | tf_op jit(solution)/shard_map/forward/pallas_call | solution.py:179
  23.8 12.6 %all-to-all-start = ((bf16[64,8,128]{2,1,0:T(8,128)(2,1)}), bf16[64,8,128]{2,1,0:T(8,128)(2,1)S(1)}, u32[]{:S(2)}, u32[]{:S(2)}) async-start(bf16[64,8,128]{2,1,0:T(8,128)(2,1)} %get-tuple-element.15), calls=%async_computation | async-start | bytes 262144 | tf_op jit(solution)/shard_map/all_to_all | solution.py:488
  36.4 1.1 %reshape.40.wide = bf16[32,4096]{1,0:T(8,128)(2,1)S(1)} reshape(bf16[1024,128]{1,0:T(8,128)(2,1)} %param.18) | data formatting | bytes 524288 | tf_op jit(solution)/shard_map/reshape | solution.py:525
  37.5 8.7 %all-to-all-done.parts = bf16[64,8,128]{2,1,0:T(8,128)(2,1)S(1)} async-done(((bf16[64,8,128]{2,1,0:T(8,128)(2,1)}), bf16[64,8,128]{2,1,0:T(8,128)(2,1)S(1)}, u32[]{:S(2)}, u32[]{:S(2)}) %all-to-all-start) | async-done | bytes 131104 | tf_op jit(solution)/shard_map/all_to_all | solution.py:488
  46.2 1.2 %copy-done.3 = bf16[1,32,128,128]{3,2,1,0:T(8,128)(2,1)S(1)} copy-done((bf16[1,32,128,128]{3,2,1,0:T(8,128)(2,1)S(1)}, bf16[1,32,128,128]{3,2,1,0:T(8,128)(2,1)}, u32[]{:S(2)}) %copy-start.3) | copy-done | bytes 1048600
  47.4 2.6 %pair.1 = f32[64,8,128]{2,1,0:T(8,128)} custom-call(s32[2]{0:T(128)S(1)} %pad_add_fusion.where, bf16[64,8,128]{2,1,0:T(8,128)(2,1)S(1)} %all-to-all-done.parts, bf16[32,128,128]{2,1,0:T(8,128)(2,1)S(1)} %bitcast.10, bf16[32,4096]{1,0:T(8,128)(2,1)S(1)} %reshape.40.wide), custom_call_target="tpu_custom_call" | custom-call | flops 200000000 | bytes 2000000 | tf_op jit(solution)/shard_map/pair/pallas_call | solution.py:69
  50.0 4.9 %all-to-all-start.1 = ((f32[64,8,128]{2,1,0:T(8,128)}), f32[64,8,128]{2,1,0:T(8,128)S(1)}, u32[]{:S(2)}, u32[]{:S(2)}) async-start(f32[64,8,128]{2,1,0:T(8,128)} %pair.1), calls=%async_computation.1 | async-start | bytes 524288 | tf_op jit(solution)/shard_map/all_to_all | solution.py:488
  55.0 1.7 %copy-done.1 = bf16[768,1536]{1,0:T(8,128)(2,1)S(1)} copy-done((bf16[768,1536]{1,0:T(8,128)(2,1)S(1)}, bf16[768,1536]{1,0:T(8,128)(2,1)}, u32[]{:S(2)}) %copy-start.1) | copy-done | bytes 2359320
  56.6 2.5 %weights.1 = (f32[64,768]{1,0:T(8,128)S(1)}, f32[8,768]{1,0:T(8,128)S(1)}, f32[8,64]{1,0:T(8,128)S(1)}) custom-call(f32[8,1536]{1,0:T(8,128)S(1)} %copy-done.6, bf16[64,1536]{1,0:T(8,128)(2,1)S(1)} %bitcast.12, f32[1,1536]{1,0:T(1,128)S(1)} %copy-done.8, bf16[768,1536]{1,0:T(8,128)(2,1)S(1)} %copy-done.1), custom_call_target="tpu_custom_call" | custom-call | flops 340000000 | bytes 3000000 | tf_op jit(solution)/shard_map/weights/pallas_call | solution.py:368
  59.2 1.4 %copy-done.2 = bf16[1040,768]{1,0:T(8,128)(2,1)S(1)} copy-done((bf16[1040,768]{1,0:T(8,128)(2,1)S(1)}, bf16[1040,768]{1,0:T(8,128)(2,1)}, u32[]{:S(2)}) %copy-start.2) | copy-done | bytes 1597464
  60.6 1.2 %bins.1.kept = f32[8,32,768]{2,1,0:T(8,128)S(1)} custom-call(s32[5,768]{1,0:T(8,128)S(1)} %reshape.41.buckets, bf16[1040,768]{1,0:T(8,128)(2,1)S(1)} %copy-done.2, bf16[1024,768]{1,0:T(8,128)(2,1)S(1)} %copy-done), custom_call_target="tpu_custom_call" | custom-call | flops 400000000 | bytes 4000000 | tf_op jit(solution)/shard_map/bins/pallas_call | solution.py:411
  61.8 4.2 %all-to-all-done.1.received = f32[64,8,128]{2,1,0:T(8,128)S(1)} async-done(((f32[64,8,128]{2,1,0:T(8,128)}), f32[64,8,128]{2,1,0:T(8,128)S(1)}, u32[]{:S(2)}, u32[]{:S(2)}) %all-to-all-start.1) | async-done | bytes 262176 | tf_op jit(solution)/shard_map/all_to_all | solution.py:488
  66.0 1.3 %tail.1 = (f32[8,768]{1,0:T(8,128)S(1)}, f32[16,32,128]{2,1,0:T(8,128)}, bf16[16,768]{1,0:T(8,128)(2,1)S(1)}) custom-call(f32[64,8,128]{2,1,0:T(8,128)S(1)} %all-to-all-done.1.received, f32[8,64]{1,0:T(8,128)S(1)} %get-tuple-element.17.along, f32[64,768]{1,0:T(8,128)S(1)} %get-tuple-element.18.turned, f32[8,768]{1,0:T(8,128)S(1)} %get-tuple-element.19.hidden_up, ...), custom_call_target="tpu_custom_call" | custom-call | flops 20000000 | bytes 4000000 | tf_op jit(solution)/shard_map/tail/pallas_call | solution.py:444
  67.4 4.2 %all-to-all-start.2 = ((f32[16,32,128]{2,1,0:T(8,128)}), f32[16,32,128]{2,1,0:T(8,128)S(1)}, u32[]{:S(2)}, u32[]{:S(2)}) async-start(f32[16,32,128]{2,1,0:T(8,128)} %get-tuple-element.25), calls=%async_computation.2 | async-start | bytes 524288 | tf_op jit(solution)/shard_map/all_to_all | solution.py:488
  71.6 3.3 %collective-permute-start.2 = (bf16[2,768]{1,0:T(2,128)(2,1)S(1)}, bf16[2,768]{1,0:T(2,128)(2,1)S(1)}, u32[]{:S(2)}, u32[]{:S(2)}) collective-permute-start(bf16[2,768]{1,0:T(2,128)(2,1)S(1)} %get-tuple-element.30), channel_id=1, source_target_pairs={{0,0},{126,126},{2,4},{4,2},{6,8},{8,6},{10,12},{12,10},{14,16},{1... | collective-permute-start | bytes 9224 | tf_op jit(solution)/shard_map/ppermute | solution.py:467
  74.9 0.1 collective-permute-start.3
  75.0 11.4 %inner.1.partial = bf16[1024,768]{1,0:T(8,128)(2,1)} custom-call(bf16[1024,768]{1,0:T(8,128)(2,1)} %get-tuple-element.14.slope, f32[8,768]{1,0:T(8,128)} %copy-done.9, bf16[3840,768]{1,0:T(8,128)(2,1)} %taps.3), custom_call_target="tpu_custom_call" | custom-call | flops 4600000000 | bytes 9000000 | tf_op jit(solution)/shard_map/inner/pallas_call | solution.py:300
  86.5 0.6 fusion.3.ends
  87.2 0.7 broadcast_in_dim.22
  87.8 6.6 %all-to-all-start.3 = ((f32[8,32,128]{2,1,0:T(8,128)}), f32[8,32,128]{2,1,0:T(8,128)S(1)}, u32[]{:S(2)}, u32[]{:S(2)}) async-start(f32[8,32,128]{2,1,0:T(8,128)} %broadcast_in_dim.22), calls=%async_computation.3 | async-start | bytes 262144 | tf_op jit(solution)/shard_map/all_to_all | solution.py:488
  94.5 6.3 %outer.1 = bf16[1024,768]{1,0:T(8,128)(2,1)} custom-call(bf16[1024,768]{1,0:T(8,128)(2,1)} %get-tuple-element.14.slope, f32[8,768]{1,0:T(8,128)} %copy-done.9, bf16[16,768]{1,0:T(8,128)(2,1)} %fusion.3.ends, bf16[3840,768]{1,0:T(8,128)(2,1)} %taps.3, bf16[1024,768]{1,0:T(8,128)(2,1)} %inner.1.partial), custom_call_target="tpu_custom_call", output_to_operand_aliasing={{}: (4, {})} | custom-call | flops 1600000000 | bytes 7000000 | tf_op jit(solution)/shard_map/outer/pallas_call | solution.py:319
  100.8 0.1 multiply_reduce_fusion
  101.0 0.6 bitcast_subtract_fusion
  (42 shorter events, 0.6 us)
Async XLA Ops:
  2.0 8.5 %collective-permute-start = (bf16[2,64]{1,0:T(2,128)(2,1)S(1)}, bf16[2,64]{1,0:T(2,128)(2,1)S(1)}, u32[]{:S(2)}, u32[]{:S(2)}) collective-permute-start(bf16[2,64]{1,0:T(2,128)(2,1)S(1)} %get-tuple-element.34), channel_id=1, source_target_pairs={{0,0},{126,126},{2,4},{4,2},{6,8},{8,6},{10,12},{12,10},{14,16},{1... | collective-permute-start | bytes 776 | tf_op jit(solution)/shard_map/ppermute | solution.py:467
  7.8 2.7 %collective-permute-start.1 = (bf16[2,64]{1,0:T(2,128)(2,1)S(1)}, bf16[2,64]{1,0:T(2,128)(2,1)S(1)}, u32[]{:S(2)}, u32[]{:S(2)}) collective-permute-start(bf16[2,64]{1,0:T(2,128)(2,1)S(1)} %get-tuple-element.35), channel_id=1, source_target_pairs={{0,2},{2,0},{4,6},{6,4},{8,10},{10,8},{12,14},{14,12},{16,18},{18,... | collective-permute-start | bytes 776 | tf_op jit(solution)/shard_map/ppermute | solution.py:468
  23.7 31.2 %copy-start.11 = (s32[3840]{0:T(1024)S(1)}, s32[3840]{0:T(1024)}, u32[]{:S(2)}) copy-start(s32[3840]{0:T(1024)} %param.21) | copy-start | bytes 46084
  23.8 31.2 %copy-start.5 = (bf16[1536,64]{0,1:T(8,128)(2,1)S(1)}, bf16[1536,64]{0,1:T(8,128)(2,1)}, u32[]{:S(2)}) copy-start(bf16[1536,64]{0,1:T(8,128)(2,1)} %param.17) | copy-start | bytes 589828
  23.8 31.2 %copy-start.6 = (f32[8,1536]{1,0:T(8,128)S(1)}, f32[8,1536]{1,0:T(8,128)}, u32[]{:S(2)}) copy-start(f32[8,1536]{1,0:T(8,128)} %get-tuple-element.16.hidden) | copy-start | bytes 147460
  23.8 31.2 %copy-start.8 = (f32[1,1536]{1,0:T(1,128)S(1)}, f32[1,1536]{1,0:T(1,128)}, u32[]{:S(2)}) copy-start(f32[1,1536]{1,0:T(1,128)} %broadcast_in_dim.9.refs_6_.gain) | copy-start | bytes 18436
  23.8 22.4 %all-to-all-start = ((bf16[64,8,128]{2,1,0:T(8,128)(2,1)}), bf16[64,8,128]{2,1,0:T(8,128)(2,1)S(1)}, u32[]{:S(2)}, u32[]{:S(2)}) async-start(bf16[64,8,128]{2,1,0:T(8,128)(2,1)} %get-tuple-element.15), calls=%async_computation | async-start | bytes 262144 | tf_op jit(solution)/shard_map/all_to_all | solution.py:488
  46.2 1.2 %copy-start.3 = (bf16[1,32,128,128]{3,2,1,0:T(8,128)(2,1)S(1)}, bf16[1,32,128,128]{3,2,1,0:T(8,128)(2,1)}, u32[]{:S(2)}) copy-start(bf16[1,32,128,128]{3,2,1,0:T(8,128)(2,1)} %param.19) | copy-start | bytes 3145732
  50.0 9.2 %copy-start = (bf16[1024,768]{1,0:T(8,128)(2,1)S(1)}, bf16[1024,768]{1,0:T(8,128)(2,1)}, u32[]{:S(2)}) copy-start(bf16[1024,768]{1,0:T(8,128)(2,1)} %get-tuple-element.14.slope) | copy-start | bytes 4718596
  50.0 16.1 %all-to-all-start.1 = ((f32[64,8,128]{2,1,0:T(8,128)}), f32[64,8,128]{2,1,0:T(8,128)S(1)}, u32[]{:S(2)}, u32[]{:S(2)}) async-start(f32[64,8,128]{2,1,0:T(8,128)} %pair.1), calls=%async_computation.1 | async-start | bytes 524288 | tf_op jit(solution)/shard_map/all_to_all | solution.py:488
  55.0 1.7 %copy-start.1 = (bf16[768,1536]{1,0:T(8,128)(2,1)S(1)}, bf16[768,1536]{1,0:T(8,128)(2,1)}, u32[]{:S(2)}) copy-start(bf16[768,1536]{1,0:T(8,128)(2,1)} %up.1) | copy-start | bytes 7077892
  59.2 1.4 %copy-start.2 = (bf16[1040,768]{1,0:T(8,128)(2,1)S(1)}, bf16[1040,768]{1,0:T(8,128)(2,1)}, u32[]{:S(2)}) copy-start(bf16[1040,768]{1,0:T(8,128)(2,1)} %get-tuple-element.21.spread) | copy-start | bytes 4792324
  60.6 5.4 %copy-start.4 = (f32[768,128]{1,0:T(8,128)S(1)}, f32[768,128]{1,0:T(8,128)}, u32[]{:S(2)}) copy-start(f32[768,128]{1,0:T(8,128)} %projection.1) | copy-start | bytes 1179652
  60.6 5.4 %copy-start.7 = (bf16[16,768]{1,0:T(8,128)(2,1)S(1)}, bf16[16,768]{1,0:T(8,128)(2,1)}, u32[]{:S(2)}) copy-start(bf16[16,768]{1,0:T(8,128)(2,1)} %get-tuple-element.22.rim) | copy-start | bytes 73732
  60.6 5.4 %copy-start.10 = (f32[8,128]{1,0:T(8,128)S(1)}, f32[8,128]{1,0:T(8,128)}, u32[]{:S(2)}) copy-start(f32[8,128]{1,0:T(8,128)} %get-tuple-element.20.inverse) | copy-start | bytes 12292
  67.3 7.7 %copy-start.9 = (f32[8,768]{1,0:T(8,128)}, f32[8,768]{1,0:T(8,128)S(1)}, u32[]{:S(2)}) copy-start(f32[8,768]{1,0:T(8,128)S(1)} %get-tuple-element.23.d_pooled) | copy-start | bytes 73732
  67.4 19.8 %all-to-all-start.2 = ((f32[16,32,128]{2,1,0:T(8,128)}), f32[16,32,128]{2,1,0:T(8,128)S(1)}, u32[]{:S(2)}, u32[]{:S(2)}) async-start(f32[16,32,128]{2,1,0:T(8,128)} %get-tuple-element.25), calls=%async_computation.2 | async-start | bytes 524288 | tf_op jit(solution)/shard_map/all_to_all | solution.py:488
  71.6 14.9 %collective-permute-start.2 = (bf16[2,768]{1,0:T(2,128)(2,1)S(1)}, bf16[2,768]{1,0:T(2,128)(2,1)S(1)}, u32[]{:S(2)}, u32[]{:S(2)}) collective-permute-start(bf16[2,768]{1,0:T(2,128)(2,1)S(1)} %get-tuple-element.30), channel_id=1, source_target_pairs={{0,0},{126,126},{2,4},{4,2},{6,8},{8,6},{10,12},{12,10},{14,16},{1... | collective-permute-start | bytes 9224 | tf_op jit(solution)/shard_map/ppermute | solution.py:467
  74.9 11.5 %collective-permute-start.3 = (bf16[2,768]{1,0:T(2,128)(2,1)S(1)}, bf16[2,768]{1,0:T(2,128)(2,1)S(1)}, u32[]{:S(2)}, u32[]{:S(2)}) collective-permute-start(bf16[2,768]{1,0:T(2,128)(2,1)S(1)} %get-tuple-element.31), channel_id=1, source_target_pairs={{0,2},{2,0},{4,6},{6,4},{8,10},{10,8},{12,14},{14,12},{16,18},{18,... | collective-permute-start | bytes 9224 | tf_op jit(solution)/shard_map/ppermute | solution.py:468
  87.8 12.9 %all-to-all-start.3 = ((f32[8,32,128]{2,1,0:T(8,128)}), f32[8,32,128]{2,1,0:T(8,128)S(1)}, u32[]{:S(2)}, u32[]{:S(2)}) async-start(f32[8,32,128]{2,1,0:T(8,128)} %broadcast_in_dim.22), calls=%async_computation.3 | async-start | bytes 262144 | tf_op jit(solution)/shard_map/all_to_all | solution.py:488

commit v3 on v2

v3 whole, which is shorter than its diff:
```python
import functools
import jax
import jax.numpy as jnp
from jax import lax
from jax.experimental import pallas as pl
from jax.experimental.pallas import tpu as pltpu
from jax.sharding import PartitionSpec as P


OP = 32
PATCH = 16
POOL = 128
BUCKETS = 32
LANES = 128
PAD = 8
ROOT = 0.7978845608028654
CUBIC = 0.044715

f32 = jnp.float32
bf16 = jnp.bfloat16
NT = (((1,), (1,)), ((), ()))
highest = lax.Precision.HIGHEST
HBM = pl.BlockSpec(memory_space=pl.ANY)
FULL = 67_000_000
MOST = 60 * 1024 * 1024


def split_in_kernel(x):
    hi = x.astype(bf16)
    return hi, (x - hi.astype(f32)).astype(bf16)


def pair_kernel(where, parts_in, cot_in, wide_in, out, moved, placed, parts, cot, wide, sems):
    copies = [
        pltpu.make_async_copy(source, here, sems.at[j])
        for j, (source, here) in enumerate(((parts_in, parts), (wide_in, wide), (cot_in, cot)))
    ]
    for copy in copies:
        copy.start()
    for copy in copies[:2]:
        copy.wait()
    rows, cols, _ = cot.shape
    bins = parts.shape[1]
    seq, col = where[0], where[1]
    mine = parts[pl.ds(seq * (rows // bins), rows // bins)].astype(f32).reshape(rows, LANES)
    left = mine[:, :OP].astype(bf16)
    other = parts[pl.ds(col * (cols // bins), cols // bins)].astype(f32).reshape(cols, LANES)
    right = other.T[OP : 2 * OP].astype(bf16)
    weighted = jnp.dot(left, wide[...], preferred_element_type=f32)
    for l in range(OP):
        moved[pl.ds(l, rows, stride=OP), :] = weighted[:, l * LANES : (l + 1) * LANES]
    copies[2].wait()
    grid = jnp.concatenate([cot[i] for i in range(rows)], axis=1)
    stacked = jnp.concatenate([moved[i * OP : (i + 1) * OP, :] for i in range(rows)], axis=1)
    hi, lo = split_in_kernel(stacked)
    both = lax.dot_general(
        grid, jnp.concatenate([hi, lo], axis=0), NT, preferred_element_type=f32
    )
    grad_right = both[:, :OP] + both[:, OP:]
    summed = jnp.dot(right, grid, preferred_element_type=f32)
    for i in range(rows):
        moved[i * OP : (i + 1) * OP, :] = summed[:, i * LANES : (i + 1) * LANES]
    by_row = jnp.concatenate([moved[pl.ds(l, rows, stride=OP), :] for l in range(OP)], axis=1)
    hi, lo = split_in_kernel(by_row)
    both = lax.dot_general(
        jnp.concatenate([hi, lo], axis=0), wide[...], NT, preferred_element_type=f32
    )
    grad_left = both[:rows] + both[rows:]
    placed[...] = jnp.zeros_like(placed)
    for index, grads, lane in (
        (seq * (rows // bins), grad_left, 0),
        (col * (cols // bins), grad_right, OP),
    ):
        grads = grads.reshape(-1, bins, OP)
        many = grads.shape[0]
        own = slice(lane, lane + OP)
        beside = slice(2 * OP + lane, 3 * OP + lane)
        placed[pl.ds(index + 1, many), :, own] = grads
        placed[pl.ds(index + 2, many), :1, beside] = grads[:, bins - 1 :, :]
        placed[pl.ds(index, many), bins - 1 :, beside] = grads[:, :1, :]
    out[...] = placed[1 : 1 + out.shape[0]].astype(bf16)


def pair_stage(where, parts, cot, wide):
    vmem = pl.BlockSpec(memory_space=pltpu.VMEM)
    return pl.pallas_call(
        pair_kernel,
        out_shape=jax.ShapeDtypeStruct(parts.shape, bf16),
        in_specs=[pl.BlockSpec(memory_space=pltpu.SMEM), HBM, HBM, HBM],
        out_specs=vmem,
        scratch_shapes=[
            pltpu.VMEM((cot.shape[0] * OP, LANES), f32),
            pltpu.VMEM((parts.shape[0] + 2,) + parts.shape[1:], f32),
            pltpu.VMEM(parts.shape, bf16),
            pltpu.VMEM(cot.shape, bf16),
            pltpu.VMEM(wide.shape, bf16),
            pltpu.SemaphoreType.DMA((3,)),
        ],
        compiler_params=pltpu.CompilerParams(vmem_limit_bytes=FULL),
        cost_estimate=pl.CostEstimate(flops=200_000_000, bytes_accessed=2_000_000, transcendentals=0),
        name="pair",
    )(where, parts, cot, wide)


def iota(shape, dim): return lax.broadcasted_iota(jnp.int32, shape, dim)


def from_sides(where, far, near):
    even = where[2] % 2 == 0
    before = jnp.where(even, far, near)
    behind = jnp.where(even, near, far)
    before = jnp.where(where[2] > 0, before, jnp.zeros_like(before))
    behind = jnp.where(where[2] < where[3] - 1, behind, jnp.zeros_like(behind))
    return before, behind


def forward_kernel(chunk, where, *refs):
    sources = refs[:9]
    spread, slope, parts, hidden_out, inverse_out, rim = refs[9:15]
    tokens, far, near, stem, taps, bias, up, gain, pair = refs[15:24]
    cells, unfolded, pools, spread_here, slope_here, parts_here, sems = refs[24:]
    copies = [
        pltpu.make_async_copy(source, here, sems.at[j])
        for j, (source, here) in enumerate(zip(sources, refs[15:24]))
    ]
    for copy in copies:
        copy.start()
    patches = slope.shape[0]
    per = LANES // PATCH
    channels = stem.shape[1]
    blocks = channels // LANES
    kernel = taps.shape[0] // channels
    reach = (kernel - 1) // 2
    t = iota((patches, LANES), 0)
    lane = iota((patches, LANES), 1)
    repeat = (t // per == lane).astype(bf16)
    fold = (iota((LANES, 4 * PATCH), 0) % PATCH == iota((LANES, 4 * PATCH), 1) // 4).astype(bf16)
    copies[0].wait()
    bases = tokens[...].astype(f32).astype(bf16)
    rows = jnp.dot(repeat, bases, preferred_element_type=f32)
    own = jnp.where(lane // PATCH == t % per, rows + 1.0, 0.0).astype(bf16)
    base = jnp.dot(own, fold, preferred_element_type=f32)
    onehot = (base == (iota((patches, 4 * PATCH), 1) % 4 + 1).astype(f32)).astype(f32).astype(bf16)
    for copy in copies[1:4]:
        copy.wait()
    main = jnp.dot(onehot, stem[...], preferred_element_type=f32).astype(bf16)
    before, behind = from_sides(where, far[...].astype(f32), near[...].astype(f32))
    ends = jnp.concatenate([before[:PAD], behind[PAD:]], axis=0).astype(bf16)
    edges = jnp.dot(ends, stem[...], preferred_element_type=f32).astype(bf16)
    spread_here[:PAD, :] = edges[:PAD]
    spread_here[PAD : PAD + patches, :] = main
    spread_here[PAD + patches :, :] = edges[PAD:]
    wide = main.astype(f32)
    edges = edges.astype(f32)
    for c in range(blocks):
        at = slice(c * LANES, (c + 1) * LANES)
        cells[c, :PAD, :] = edges[:PAD, at]
        cells[c, PAD : PAD + patches, :] = wide[:, at]
        cells[c, PAD + patches :, :] = edges[PAD:, at]
    outs = [pltpu.make_async_copy(spread_here, spread, sems.at[9])]
    outs[0].start()
    for r in range(patches // chunk):
        for k in range(kernel):
            for c in range(blocks):
                start = r * chunk + PAD - reach + k
                j = (k * blocks + c) * LANES
                unfolded[r % 2, :, j : j + LANES] = cells[c, start : start + chunk, :].astype(bf16)
        if r == 0:
            copies[4].wait()
            copies[5].wait()
        before = jnp.dot(unfolded[r % 2], taps[...], preferred_element_type=f32) + bias[...].reshape(1, channels)
        square = before * before
        bent = jnp.tanh(before * (ROOT + ROOT * CUBIC * square))
        half = 0.5 * (1.0 + bent)
        after = before * half
        tilt = half + before * (0.5 - 0.5 * bent * bent) * (ROOT + 3.0 * ROOT * CUBIC * square)
        slope_here[r * chunk : (r + 1) * chunk, :] = tilt.astype(bf16)
        out = pltpu.make_async_copy(
            slope_here.at[pl.ds(r * chunk, chunk)], slope.at[pl.ds(r * chunk, chunk)], sems.at[11 + r]
        )
        out.start()
        outs.append(out)
        for n in range(chunk // POOL):
            b = r * (chunk // POOL) + n
            pools[b : b + 1, :] = jnp.sum(
                after[n * POOL : (n + 1) * POOL], axis=0, keepdims=True
            ) * (1.0 / POOL)
    rim[:PAD, :] = slope_here[:PAD, :]
    rim[PAD:, :] = slope_here[patches - PAD :, :]
    for copy in copies[6:]:
        copy.wait()
    hidden = jnp.dot(pools[...].astype(bf16), up[...], preferred_element_type=f32)
    inverse = lax.rsqrt(jnp.mean(hidden * hidden, axis=1, keepdims=True) + 1e-06)
    normed = (hidden * inverse * gain[...].reshape(1, -1)).astype(bf16)
    sides = lax.dot_general(normed, pair[...], NT, preferred_element_type=f32)
    full = jnp.concatenate([sides, jnp.zeros_like(sides)], axis=1).astype(bf16)
    parts_here[...] = jnp.broadcast_to(full[None], parts.shape)
    out = pltpu.make_async_copy(parts_here, parts, sems.at[10])
    out.start()
    outs.append(out)
    hidden_out[...] = hidden
    inverse_out[...] = jnp.broadcast_to(inverse, inverse_out.shape)
    for out in outs:
        out.wait()


def forward_stage(where, tokens, far, near, stem, taps, bias, up, gain, pair, count, chunk=512):
    vmem = pl.BlockSpec(memory_space=pltpu.VMEM)
    patches = tokens.size // PATCH
    channels = stem.shape[1]
    bins = patches // POOL
    tall = patches + 2 * PAD
    inputs = (tokens, far, near, stem, taps, bias, up, gain, pair)
    return pl.pallas_call(
        functools.partial(forward_kernel, chunk),
        out_shape=[
            jax.ShapeDtypeStruct((tall, channels), bf16),
            jax.ShapeDtypeStruct((patches, channels), bf16),
            jax.ShapeDtypeStruct((count, bins, LANES), bf16),
            jax.ShapeDtypeStruct((bins, up.shape[1]), f32),
            jax.ShapeDtypeStruct((bins, LANES), f32),
            jax.ShapeDtypeStruct((2 * PAD, channels), bf16),
        ],
        in_specs=[pl.BlockSpec(memory_space=pltpu.SMEM)] + [HBM] * 9,
        out_specs=[HBM] * 3 + [vmem] * 3,
        scratch_shapes=[pltpu.VMEM(x.shape, x.dtype) for x in inputs]
        + [
            pltpu.VMEM((channels // LANES, tall, LANES), f32),
            pltpu.VMEM((2, chunk, taps.shape[0]), bf16),
            pltpu.VMEM((bins, channels), f32),
            pltpu.VMEM((tall, channels), bf16),
            pltpu.VMEM((patches, channels), bf16),
            pltpu.VMEM((count, bins, LANES), bf16),
            pltpu.SemaphoreType.DMA((11 + patches // chunk,)),
        ],
        compiler_params=pltpu.CompilerParams(vmem_limit_bytes=FULL),
        cost_estimate=pl.CostEstimate(
            flops=6_200_000_000, bytes_accessed=14_000_000, transcendentals=800_000
        ),
        name="forward",
    )(where, *inputs)


def input_kernel(chunk, source, d_pooled, ends, taps_in, out, cells, shifted, taps, slope, block, sems):
    patches, channels = slope.shape
    blocks = channels // LANES
    kernel = taps.shape[0] // channels
    reach = (kernel - 1) // 2
    halves = 1
    part = patches // halves
    reads = [
        pltpu.make_async_copy(
            source.at[pl.ds(h * part, part)], slope.at[pl.ds(h * part, part)], sems.at[h]
        )
        for h in range(halves)
    ]
    copies = [
        pltpu.make_async_copy(
            taps_in.at[pl.ds(k * channels, channels)],
            taps.at[pl.ds(k * channels, channels)],
            sems.at[halves + k],
        )
        for k in range(kernel)
    ]
    for copy in reads + copies:
        copy.start()
    for copy in reads:
        copy.wait()
    for c in range(blocks):
        at = slice(c * LANES, (c + 1) * LANES)
        cells[c, :PAD, :] = ends[:PAD, at].astype(f32)
        cells[c, PAD + patches :, :] = ends[PAD:, at].astype(f32)
        for n in range(patches // POOL):
            low, high = n * POOL, (n + 1) * POOL
            cells[c, PAD + low : PAD + high, :] = (
                slope[low:high, at].astype(f32) * d_pooled[n : n + 1, at]
            )

    def shift(r):
        for k in range(kernel):
            start = r * chunk + PAD + reach - k
            for c in range(blocks):
                j = (k * blocks + c) * LANES
                shifted[r % 2, :, j : j + LANES] = cells[c, start : start + chunk, :].astype(bf16)

    shift(0)
    for copy in copies:
        copy.wait()
    backs = []
    for r in range(patches // chunk):
        if r > 0:
            shift(r)
        total = None
        for k in range(kernel):
            at = slice(k * channels, (k + 1) * channels)
            term = lax.dot_general(
                shifted[r % 2, :, at], taps[at, :], NT, preferred_element_type=f32
            )
            total = term if total is None else total + term
        block[r * chunk : (r + 1) * chunk, :] = total.astype(bf16)
        back = pltpu.make_async_copy(
            block.at[pl.ds(r * chunk, chunk)],
            out.at[pl.ds(r * chunk, chunk)],
            sems.at[halves + kernel + r],
        )
        back.start()
        backs.append(back)
    for back in backs:
        back.wait()


def input_stage(slope, d_pooled, ends, taps, chunk=512):
    vmem = pl.BlockSpec(memory_space=pltpu.VMEM)
    patches, channels = slope.shape
    kernel = taps.shape[0] // channels
    return pl.pallas_call(
        functools.partial(input_kernel, chunk),
        out_shape=jax.ShapeDtypeStruct((patches, channels), bf16),
        in_specs=[HBM, vmem, vmem, HBM],
        out_specs=HBM,
        scratch_shapes=[
            pltpu.VMEM((channels // LANES, patches + 2 * PAD, LANES), f32),
            pltpu.VMEM((2, chunk, taps.shape[0]), bf16),
            pltpu.VMEM(taps.shape, bf16),
            pltpu.VMEM(slope.shape, bf16),
            pltpu.VMEM((patches, channels), bf16),
            pltpu.SemaphoreType.DMA((1 + kernel + patches // chunk,)),
        ],
        compiler_params=pltpu.CompilerParams(vmem_limit_bytes=MOST),
        cost_estimate=pl.CostEstimate(
            flops=6_100_000_000, bytes_accessed=10_000_000, transcendentals=0
        ),
        name="inner",
    )(slope, d_pooled, ends, taps)


def weights_kernel(*refs):
    turned, hidden_up, along, shared, wide = refs[7:12]
    hidden, inverse, rim, pair, gain, up, mixing = refs[12:19]
    moved, sems = refs[19:]
    copies = [
        pltpu.make_async_copy(source, here, sems.at[j])
        for j, (source, here) in enumerate(zip(refs[:7], refs[12:19]))
    ]
    for copy in copies:
        copy.start()
    for copy in copies:
        copy.wait()
    _, width = up.shape
    bins = hidden.shape[0]
    scaled = pair[...].astype(f32) * gain[...].reshape(1, width)
    near = lax.dot_general(
        hidden[...], scaled, NT, precision=highest, preferred_element_type=f32
    ) * (1.0 / width)
    along[...] = near
    scaled_hi, scaled_lo = split_in_kernel(scaled)
    hidden_hi, hidden_lo = split_in_kernel(hidden[...])
    stacked = jnp.concatenate(
        [scaled_hi.astype(f32), scaled_lo.astype(f32), hidden_hi.astype(f32), hidden_lo.astype(f32)],
        axis=0,
    ).astype(bf16)
    through = lax.dot_general(stacked, up[...], NT, preferred_element_type=f32)
    turned[...] = through[: 2 * OP] + through[2 * OP : 4 * OP]
    lifted = through[4 * OP : 4 * OP + bins] + through[4 * OP + bins :]
    hidden_up[...] = lifted
    shared[...] = jnp.zeros_like(shared)
    for base, bin_at, row in ((0, bins - 1, 2 * PAD - 2), (PAD, 0, 0)):
        shared[base : base + 2, :] = rim[...].astype(f32)[row : row + 2]
        shared[base + 2 : base + 3, :] = lifted[bin_at : bin_at + 1]
        shared[base + 3 : base + 4, : 2 * OP] = near[bin_at : bin_at + 1]
        shared[base + 4 : base + 5, :LANES] = inverse[bin_at : bin_at + 1, :]
    moved[...] = mixing[...].astype(f32)
    for l in range(OP):
        wide[:, l * LANES : (l + 1) * LANES] = moved[pl.ds(l, OP, stride=OP), :].astype(bf16)


def weights_stage(hidden, inverse, rim, pair, gain, up, mixing):
    vmem = pl.BlockSpec(memory_space=pltpu.VMEM)
    bins, _ = hidden.shape
    channels = up.shape[0]
    inputs = (hidden, inverse, rim, pair, gain, up, mixing)
    return pl.pallas_call(
        weights_kernel,
        out_shape=[
            jax.ShapeDtypeStruct((2 * OP, channels), f32),
            jax.ShapeDtypeStruct((bins, channels), f32),
            jax.ShapeDtypeStruct((bins, 2 * OP), f32),
            jax.ShapeDtypeStruct((2 * PAD, channels), f32),
            jax.ShapeDtypeStruct((OP, OP * LANES), bf16),
        ],
        in_specs=[HBM] * 7,
        out_specs=[vmem] * 5,
        scratch_shapes=[pltpu.VMEM(x.shape, x.dtype) for x in inputs]
        + [pltpu.VMEM(mixing.shape, f32), pltpu.SemaphoreType.DMA((7,))],
        compiler_params=pltpu.CompilerParams(vmem_limit_bytes=FULL),
        cost_estimate=pl.CostEstimate(
            flops=340_000_000, bytes_accessed=3_000_000, transcendentals=0
        ),
        name="weights",
    )(*inputs)


def bins_kernel(buckets, spread, slope, kept):
    kernel, channels = buckets.shape
    patches = slope.shape[0]
    reach = (kernel - 1) // 2
    slots = iota((BUCKETS, channels), 0)
    member = jnp.concatenate(
        [(buckets[k : k + 1, :] == slots).astype(f32) for k in range(kernel)], axis=0
    ).astype(bf16)
    tapped = lax.dot_general(member, spread[...], NT, preferred_element_type=f32)
    mixed = None
    for k in range(kernel):
        start = PAD - reach + k
        term = tapped[k * BUCKETS : (k + 1) * BUCKETS, start : start + patches]
        mixed = term if mixed is None else mixed + term
    hi, lo = split_in_kernel(mixed)
    both = jnp.concatenate([hi, lo], axis=0)
    for n in range(patches // POOL):
        rows = slice(n * POOL, (n + 1) * POOL)
        part = jnp.dot(both[:, rows], slope[rows, :], preferred_element_type=f32)
        kept[n] = part[:BUCKETS] + part[BUCKETS:]


def bins_stage(buckets, spread, slope):
    vmem = pl.BlockSpec(memory_space=pltpu.VMEM)
    patches, channels = slope.shape
    return pl.pallas_call(
        bins_kernel,
        out_shape=jax.ShapeDtypeStruct((patches // POOL, BUCKETS, channels), f32),
        in_specs=[vmem] * 3,
        out_specs=vmem,
        compiler_params=pltpu.CompilerParams(vmem_limit_bytes=24 << 20),
        cost_estimate=pl.CostEstimate(
            flops=400_000_000, bytes_accessed=4_000_000, transcendentals=0
        ),
        name="bins",
    )(buckets, spread, slope)


def tail_kernel(where, received, along, turned, hidden_up, inverse, kept, projection, far, near, d_pooled, sketch, edges):
    bins = kept.shape[0]
    summed = jnp.sum(received[...].astype(f32), axis=0)
    prior, later = from_sides(where, far[...], near[...])
    grads = jnp.concatenate([summed[:, : 2 * OP], summed[:, 2 * OP :]], axis=0)
    both = jnp.dot(grads, turned[...], precision=highest, preferred_element_type=f32)

    def finish(rows, grad, line, scale, lifted):
        inner = jnp.sum(grad * line, axis=1, keepdims=True)
        return (scale * rows - scale * scale * scale * inner * lifted) * (1.0 / POOL)

    scaled = finish(both[:bins], grads[:bins], along[...], inverse[:, :1], hidden_up[...])
    d_pooled[...] = scaled
    total = scaled[0:1] * kept[0]
    for n in range(1, bins):
        total = total + scaled[n : n + 1] * kept[n]
    part = jnp.dot(total, projection[...], precision=highest, preferred_element_type=f32)
    sketch[...] = jnp.broadcast_to(part[None], sketch.shape)
    first = finish(
        both[bins : bins + 1], grads[bins : bins + 1], prior[3:4, : 2 * OP], prior[4:5, :1], prior[2:3]
    )
    last = finish(
        both[2 * bins - 1 :], grads[2 * bins - 1 :], later[PAD + 3 : PAD + 4, : 2 * OP],
        later[PAD + 4 : PAD + 5, :1], later[PAD + 2 : PAD + 3],
    )
    blank = jnp.zeros((PAD - 2, first.shape[1]), f32)
    edges[...] = jnp.concatenate(
        [blank, first * prior[:2], last * later[PAD : PAD + 2], blank], axis=0
    ).astype(bf16)


def tail_stage(where, received, along, turned, hidden_up, inverse, kept, projection, far, near, fan):
    vmem = pl.BlockSpec(memory_space=pltpu.VMEM)
    bins, channels = hidden_up.shape
    return pl.pallas_call(
        tail_kernel,
        out_shape=[
            jax.ShapeDtypeStruct((bins, channels), f32),
            jax.ShapeDtypeStruct((fan, kept.shape[1], projection.shape[1]), f32),
            jax.ShapeDtypeStruct((2 * PAD, channels), bf16),
        ],
        in_specs=[pl.BlockSpec(memory_space=pltpu.SMEM)] + [vmem] * 9,
        out_specs=[vmem] * 3,
        compiler_params=pltpu.CompilerParams(vmem_limit_bytes=24 << 20),
        cost_estimate=pl.CostEstimate(flops=20_000_000, bytes_accessed=4_000_000, transcendentals=0),
        name="tail",
    )(where, received, along, turned, hidden_up, inverse, kept, projection, far, near)


def to_sides(value, axes):
    count = lax.axis_size(axes)
    inside = [(i, i ^ 1) for i in range(count)]
    across = [(0, 0), (count - 1, count - 1)] + [
        (i, i + 1 if i % 2 else i - 1) for i in range(1, count - 1)
    ]
    far = lax.ppermute(value, axes, across)
    near = lax.ppermute(value, axes, inside)
    return far, near


def one_hot(bases):
    return (
        (bases[:, :, None] == jnp.arange(4, dtype=jnp.int32))
        .astype(bf16)
        .reshape(bases.shape[0], PATCH * 4)
    )


def exchange(value, axes):
    return lax.all_to_all(value, axes, 0, 0, tiled=True)


def whole(
    tokens,
    stem_weight,
    conv_weight,
    conv_bias,
    up_weight,
    norm_gain,
    pair_weight,
    out_weight,
    cotangent,
    projection,
    buckets,
):
    channels = conv_weight.shape[1]
    kernel = conv_weight.shape[0] // channels
    reach = (kernel - 1) // 2
    line = ("seq", "col")
    count = lax.axis_size(line)
    place = lax.axis_index(line)
    where = jnp.stack(
        [lax.axis_index("seq"), lax.axis_index("col"), place, count + 0 * place]
    ).astype(jnp.int32)

    edge = reach * PATCH
    rims = one_hot(
        jnp.concatenate([tokens[0, -edge:], tokens[0, :edge]]).reshape(2 * reach, PATCH)
    )
    rims = jnp.pad(rims, ((PAD - reach, PAD - reach), (0, 0)))
    far, near = to_sides(rims, line)
    pair = pair_weight.T
    spread, slope, parts, hidden, inverse, rim = forward_stage(
        where, tokens[0].reshape(-1, LANES), far, near, stem_weight, conv_weight, conv_bias,
        up_weight, norm_gain, pair, count,
    )
    parts = exchange(parts, line)
    turned, hidden_up, along, shared, wide = weights_stage(
        hidden, inverse, rim, pair, norm_gain, up_weight, out_weight
    )
    sent = pair_stage(where, parts, cotangent[0], wide)
    received = exchange(sent, line)
    far, near = to_sides(shared, line)
    kept = bins_stage(buckets.reshape(kernel, channels), spread, slope)
    d_pooled, sketch, grad_ends = tail_stage(
        where, received, along, turned, hidden_up, inverse, kept, projection, far, near,
        lax.axis_size("seq"),
    )
    sketch = jnp.sum(exchange(sketch, "seq"), axis=0)
    input_grad = input_stage(slope, d_pooled, grad_ends, conv_weight)
    col_count = lax.axis_size("col")
    batches = lax.axis_size("batch")
    every = exchange(
        jnp.broadcast_to(sketch[None], (batches * col_count,) + sketch.shape), ("batch", "col")
    )
    sketches = jnp.sum(every.reshape(batches, col_count, *sketch.shape), axis=1)
    units = sketches * lax.rsqrt(
        jnp.mean(sketches * sketches, axis=(1, 2), keepdims=True) + 1e-06
    )
    own = lax.dynamic_slice_in_dim(units, lax.axis_index("batch"), 1, 0)
    embedding = own - jnp.sum(units, axis=0, keepdims=True) / batches
    return (input_grad[None], embedding)


def solution(mesh):
    in_specs = (
        P("batch", ("seq", "col")),
        P(),
        P(),
        P(),
        P(),
        P(),
        P(),
        P(),
        P("batch", "seq", "col", None),
        P(),
        P(),
    )
    out_specs = (P("batch", ("seq", "col"), None), P("batch", None, None))
    return jax.shard_map(whole, mesh=mesh, in_specs=in_specs, out_specs=out_specs, check_vma=False)
```

time: 102 us -> 102 us (level)
  waiting for transfers between devices: 12.9 us -> 17.1 us
  local copies, waits for them, and re-layouts: 9.99 us -> 5.89 us
  Pallas kernels: 37.9 us -> 35.7 us
  starting transfers between devices: 37.6 us -> 39.7 us
    pallas_call x3 -> x2, Pallas kernels: 20.3 us -> 15.2 us  [the longest x1 11.4 us: input_stage(): pl.pallas_call(functools.partial(input_kernel, chunk), out_shape=jax.Shap...]
    broadcast_in_dim x2 -> x0, local copies, waits for them, and re-layouts: 2.58 us -> none  [the longest x1 1.29 us: whole(): gain = norm_gain[None]]
    all_to_all x4, waiting for transfers between devices: 12.9 us -> 15.3 us  [exchange(): return lax.all_to_all(value, axes, 0, 0, tiled=True)]
    ppermute x4, waiting for transfers between devices: 0.01 us -> 1.78 us  [the longest x2 1.26 us: to_sides(): near = lax.ppermute(value, axes, inside)]
    pallas_call x1, Pallas kernels: 2.52 us -> 4.06 us  [weights_stage(): pl.pallas_call(weights_kernel, out_shape=[jax.ShapeDtypeStruct((2 * OP, c...]
    ppermute x4, starting transfers between devices: 9.28 us -> 10.7 us  [the longest x2 10.5 us: to_sides(): far = lax.ppermute(value, axes, across)]
    concatenate x2 -> x0, other arithmetic: 1.23 us -> none  [to_neighbours(): jnp.concatenate([before, behind], axis=0)]
    reshape x1 -> x0, local copies, waits for them, and re-layouts: 1.07 us -> none  [whole(): wide = out_weight.reshape(OP, OP * out_weight.shape[1])]
  transfers between devices with their start and end apart: 8 -> 8, of which waited for: 2 -> 5; matrix products, arithmetic and copies ran while one was open for 4% -> 1% of each run, Pallas kernels for 21% -> 17%
where the time goes in v3:
time: 102 us; the launch traced here: 101 us
  starting transfers between devices  39.7 us (39%)
  Pallas kernels  35.7 us (35%)
  waiting for transfers between devices  17.1 us (17%)
  local copies, waits for them, and re-layouts  5.89 us (6%)
  other arithmetic  1.53 us (2%)
    all_to_all x4, starting transfers between devices, exchange(): return lax.all_to_all(value, axes, 0, 0, tiled=True)  29 us
    all_to_all x4, waiting for transfers between devices, exchange(): return lax.all_to_all(value, axes, 0, 0, tiled=True)  15.3 us
    pallas_call x1, Pallas kernels, forward_stage(): pl.pallas_call(functools.partial(forward_kernel, chunk), out_shape=[jax.S...  13.3 us
    pallas_call x1, Pallas kernels, input_stage(): pl.pallas_call(functools.partial(input_kernel, chunk), out_shape=jax.Shap...  11.4 us
    ppermute x2, starting transfers between devices, to_sides(): far = lax.ppermute(value, axes, across)  10.5 us
    pallas_call x1, Pallas kernels, weights_stage(): pl.pallas_call(weights_kernel, out_shape=[jax.ShapeDtypeStruct((2 * OP, c...  4.06 us
    unnamed x26, local copies, waits for them, and re-layouts  4.05 us
    pallas_call x1, Pallas kernels, pair_stage(): pl.pallas_call(pair_kernel, out_shape=jax.ShapeDtypeStruct(parts.shape, b...  3.75 us
  transfers between devices with their start and end apart: 8, of which 5 were waited for; matrix products, arithmetic and copies ran while one was open for 1% of the time, Pallas kernels for 17%

profile of v3, /device:TPU:1, one launch (start us, length us, event | category | flops | bytes accessed | tf_op | source)
XLA Modules:
  0.0 100.8 jit_solution(14167913662050092617)
XLA Ops:
  0.6 0.8 slice_reduce_fusion.1
  1.4 0.1 concatenate.9
  1.5 0.1 concatenate.8
  1.6 0.1 eq.24
  1.7 0.1 eq.26
  1.9 5.8 %collective-permute-start = (bf16[16,64]{1,0:T(8,128)(2,1)S(1)}, bf16[16,64]{1,0:T(8,128)(2,1)S(1)}, u32[]{:S(2)}, u32[]{:S(2)}) collective-permute-start(bf16[16,64]{1,0:T(8,128)(2,1)S(1)} %pad_convert_fusion), channel_id=1, source_target_pairs={{0,0},{126,126},{2,4},{4,2},{6,8},{8,6},{10,12},{12,10},{14,16},{1... | collective-permute-start | bytes 6152 | tf_op jit(solution)/shard_map/ppermute | solution.py:496
  7.6 0.1 collective-permute-start.1
  7.7 0.7 pad_add_fusion.where
  8.4 0.5 collective-permute-done.refs_1_
  8.9 1.3 %collective-permute-done.1.refs_2_ = bf16[16,64]{1,0:T(8,128)(2,1)S(1)} collective-permute-done((bf16[16,64]{1,0:T(8,128)(2,1)S(1)}, bf16[16,64]{1,0:T(8,128)(2,1)S(1)}, u32[]{:S(2)}, u32[]{:S(2)}) %collective-permute-start.1) | collective-permute-done | bytes 2080 | tf_op jit(solution)/shard_map/ppermute | solution.py:497
  10.2 0.6 copy-done.12
  10.8 13.3 %forward.1 = (bf16[1040,768]{1,0:T(8,128)(2,1)}, bf16[1024,768]{1,0:T(8,128)(2,1)}, bf16[64,8,128]{2,1,0:T(8,128)(2,1)}, f32[8,1536]{1,0:T(8,128)}, f32[8,128]{1,0:T(8,128)}, /*index=5*/bf16[16,768]{1,0:T(8,128)(2,1)}) custom-call(s32[4]{0:T(128)} %pad_add_fusion.where, s32[128,128]{1,0:T(8,128)} %bitcast.16, bf16[16,64]{1,0:T(8,128)(2,1)} %copy-done.11, ...), custom_call_target="tpu_custom_call" | custom-call | flops 6200000000 | bytes 14000000 | tf_op jit(solution)/shard_map/forward/pallas_call | solution.py:214
  24.1 12.8 %all-to-all-start = ((bf16[64,8,128]{2,1,0:T(8,128)(2,1)}), bf16[64,8,128]{2,1,0:T(8,128)(2,1)}, u32[]{:S(2)}, u32[]{:S(2)}) async-start(bf16[64,8,128]{2,1,0:T(8,128)(2,1)} %get-tuple-element.17), calls=%async_computation | async-start | bytes 262144 | tf_op jit(solution)/shard_map/all_to_all | solution.py:510
  36.9 4.1 %weights.1 = (f32[64,768]{1,0:T(8,128)}, f32[8,768]{1,0:T(8,128)}, f32[8,64]{1,0:T(8,128)}, f32[16,768]{1,0:T(8,128)}, bf16[32,4096]{1,0:T(8,128)(2,1)}) custom-call(f32[8,1536]{1,0:T(8,128)} %get-tuple-element.18.refs_0_, f32[8,128]{1,0:T(8,128)} %get-tuple-element.19.refs_1_.inverse, bf16[16,768]{1,0:T(8,128)(2,1)} %get-tuple-element.20.refs_2_, ...), custom_call_target="tpu_custom_call" | custom-call | flops 340000000 | bytes 3000000 | tf_op jit(solution)/shard_map/weights/pallas_call | solution.py:382
  41.0 5.7 %all-to-all-done.parts_in = bf16[64,8,128]{2,1,0:T(8,128)(2,1)} async-done(((bf16[64,8,128]{2,1,0:T(8,128)(2,1)}), bf16[64,8,128]{2,1,0:T(8,128)(2,1)}, u32[]{:S(2)}, u32[]{:S(2)}) %all-to-all-start) | async-done | bytes 131104 | tf_op jit(solution)/shard_map/all_to_all | solution.py:510
  46.7 3.8 %pair.1 = bf16[64,8,128]{2,1,0:T(8,128)(2,1)} custom-call(s32[4]{0:T(128)} %pad_add_fusion.where, bf16[64,8,128]{2,1,0:T(8,128)(2,1)} %all-to-all-done.parts_in, bf16[32,128,128]{2,1,0:T(8,128)(2,1)} %bitcast.13, bf16[32,4096]{1,0:T(8,128)(2,1)} %get-tuple-element.21.wide_in), custom_call_target="tpu_custom_call" | custom-call | flops 200000000 | bytes 2000000 | tf_op jit(solution)/shard_map/pair/pallas_call | solution.py:86
  50.4 5.0 %all-to-all-start.1 = ((bf16[64,8,128]{2,1,0:T(8,128)(2,1)}), bf16[64,8,128]{2,1,0:T(8,128)(2,1)S(1)}, u32[]{:S(2)}, u32[]{:S(2)}) async-start(bf16[64,8,128]{2,1,0:T(8,128)(2,1)} %pair.1), calls=%async_computation.1 | async-start | bytes 262144 | tf_op jit(solution)/shard_map/all_to_all | solution.py:510
  55.4 4.7 %collective-permute-start.2 = (f32[16,768]{1,0:T(8,128)}, f32[16,768]{1,0:T(8,128)S(1)}, u32[]{:S(2)}, u32[]{:S(2)}) collective-permute-start(f32[16,768]{1,0:T(8,128)} %get-tuple-element.26), channel_id=1, source_target_pairs={{0,0},{126,126},{2,4},{4,2},{6,8},{8,6},{10,12},{12,10},{14,16},{1... | collective-permute-start | bytes 147464 | tf_op jit(solution)/shard_map/ppermute | solution.py:496
  60.2 0.1 collective-permute-start.3
  60.3 1.4 %copy-done = bf16[1040,768]{1,0:T(8,128)(2,1)S(1)} copy-done((bf16[1040,768]{1,0:T(8,128)(2,1)S(1)}, bf16[1040,768]{1,0:T(8,128)(2,1)}, u32[]{:S(2)}) %copy-start) | copy-done | bytes 1597464
  61.7 1.4 %copy-done.1 = bf16[1024,768]{1,0:T(8,128)(2,1)S(1)} copy-done((bf16[1024,768]{1,0:T(8,128)(2,1)S(1)}, bf16[1024,768]{1,0:T(8,128)(2,1)}, u32[]{:S(2)}) %copy-start.1) | copy-done | bytes 1572888
  63.1 1.2 %bins.1.kept = f32[8,32,768]{2,1,0:T(8,128)S(1)} custom-call(s32[5,768]{1,0:T(8,128)S(1)} %reshape.36.buckets, bf16[1040,768]{1,0:T(8,128)(2,1)S(1)} %copy-done, bf16[1024,768]{1,0:T(8,128)(2,1)S(1)} %copy-done.1), custom_call_target="tpu_custom_call" | custom-call | flops 400000000 | bytes 4000000 | tf_op jit(solution)/shard_map/bins/pallas_call | solution.py:428
  64.3 1.0 all-to-all-done.1.received
  65.4 1.9 %tail.1 = (f32[8,768]{1,0:T(8,128)S(1)}, f32[16,32,128]{2,1,0:T(8,128)}, bf16[16,768]{1,0:T(8,128)(2,1)S(1)}) custom-call(s32[4]{0:T(128)S(1)} %copy-done.6, bf16[64,8,128]{2,1,0:T(8,128)(2,1)S(1)} %all-to-all-done.1.received, f32[8,64]{1,0:T(8,128)S(1)} %copy-done.7, f32[64,768]{1,0:T(8,128)S(1)} %copy-done.3, f32[8,768]{1,0:T(8,128)S(1)} %copy-done.4, ...), custom_call_target="tpu_custom_call" | custom-call | flops 20000000 | bytes 4000000 | tf_op jit(solution)/shard_map/tail/pallas_call | solution.py:475
  67.3 0.6 copy-done.9
  67.9 6.8 %all-to-all-start.2 = ((f32[16,32,128]{2,1,0:T(8,128)}), f32[16,32,128]{2,1,0:T(8,128)S(1)}, u32[]{:S(2)}, u32[]{:S(2)}) async-start(f32[16,32,128]{2,1,0:T(8,128)} %get-tuple-element.29), calls=%async_computation.2 | async-start | bytes 524288 | tf_op jit(solution)/shard_map/all_to_all | solution.py:510
  74.7 8.7 %all-to-all-done.2 = f32[16,32,128]{2,1,0:T(8,128)S(1)} async-done(((f32[16,32,128]{2,1,0:T(8,128)}), f32[16,32,128]{2,1,0:T(8,128)S(1)}, u32[]{:S(2)}, u32[]{:S(2)}) %all-to-all-start.2) | async-done | bytes 262176 | tf_op jit(solution)/shard_map/all_to_all | solution.py:510
  83.4 0.7 broadcast_in_dim.5
  84.1 4.5 %all-to-all-start.3 = ((f32[8,32,128]{2,1,0:T(8,128)}), f32[8,32,128]{2,1,0:T(8,128)S(1)}, u32[]{:S(2)}, u32[]{:S(2)}) async-start(f32[8,32,128]{2,1,0:T(8,128)} %broadcast_in_dim.5), calls=%async_computation.3 | async-start | bytes 262144 | tf_op jit(solution)/shard_map/all_to_all | solution.py:510
  88.5 11.4 %inner.1 = bf16[1024,768]{1,0:T(8,128)(2,1)} custom-call(bf16[1024,768]{1,0:T(8,128)(2,1)} %get-tuple-element.16.slope.source, f32[8,768]{1,0:T(8,128)} %copy-done.8, bf16[16,768]{1,0:T(8,128)(2,1)} %copy-done.9, bf16[3840,768]{1,0:T(8,128)(2,1)} %taps_in.1), custom_call_target="tpu_custom_call" | custom-call | flops 6099999744 | bytes 10000000 | tf_op jit(solution)/shard_map/inner/pallas_call | solution.py:316
  100.0 0.1 multiply_reduce_fusion
  100.2 0.6 bitcast_subtract_fusion
  (35 shorter events, 0.3 us)
Async XLA Ops:
  1.9 7.0 %collective-permute-start = (bf16[16,64]{1,0:T(8,128)(2,1)S(1)}, bf16[16,64]{1,0:T(8,128)(2,1)S(1)}, u32[]{:S(2)}, u32[]{:S(2)}) collective-permute-start(bf16[16,64]{1,0:T(8,128)(2,1)S(1)} %pad_convert_fusion), channel_id=1, source_target_pairs={{0,0},{126,126},{2,4},{4,2},{6,8},{8,6},{10,12},{12,10},{14,16},{1... | collective-permute-start | bytes 6152 | tf_op jit(solution)/shard_map/ppermute | solution.py:496
  7.6 2.5 %collective-permute-start.1 = (bf16[16,64]{1,0:T(8,128)(2,1)S(1)}, bf16[16,64]{1,0:T(8,128)(2,1)S(1)}, u32[]{:S(2)}, u32[]{:S(2)}) collective-permute-start(bf16[16,64]{1,0:T(8,128)(2,1)S(1)} %pad_convert_fusion), channel_id=1, source_target_pairs={{0,2},{2,0},{4,6},{6,4},{8,10},{10,8},{12,14},{14,12},{16,18},{18,... | collective-permute-start | bytes 6152 | tf_op jit(solution)/shard_map/ppermute | solution.py:497
  8.9 1.3 %copy-start.11 = (bf16[16,64]{1,0:T(8,128)(2,1)}, bf16[16,64]{1,0:T(8,128)(2,1)S(1)}, u32[]{:S(2)}) copy-start(bf16[16,64]{1,0:T(8,128)(2,1)S(1)} %collective-permute-done.refs_1_) | copy-start | bytes 6148
  10.2 0.6 copy-start.12
  24.1 22.5 %all-to-all-start = ((bf16[64,8,128]{2,1,0:T(8,128)(2,1)}), bf16[64,8,128]{2,1,0:T(8,128)(2,1)}, u32[]{:S(2)}, u32[]{:S(2)}) async-start(bf16[64,8,128]{2,1,0:T(8,128)(2,1)} %get-tuple-element.17), calls=%async_computation | async-start | bytes 262144 | tf_op jit(solution)/shard_map/all_to_all | solution.py:510
  41.0 19.3 %copy-start.10 = (s32[3840]{0:T(1024)S(1)}, s32[3840]{0:T(1024)}, u32[]{:S(2)}) copy-start(s32[3840]{0:T(1024)} %param.21) | copy-start | bytes 46084
  50.4 14.9 %all-to-all-start.1 = ((bf16[64,8,128]{2,1,0:T(8,128)(2,1)}), bf16[64,8,128]{2,1,0:T(8,128)(2,1)S(1)}, u32[]{:S(2)}, u32[]{:S(2)}) async-start(bf16[64,8,128]{2,1,0:T(8,128)(2,1)} %pair.1), calls=%async_computation.1 | async-start | bytes 262144 | tf_op jit(solution)/shard_map/all_to_all | solution.py:510
  55.4 8.9 %collective-permute-start.2 = (f32[16,768]{1,0:T(8,128)}, f32[16,768]{1,0:T(8,128)S(1)}, u32[]{:S(2)}, u32[]{:S(2)}) collective-permute-start(f32[16,768]{1,0:T(8,128)} %get-tuple-element.26), channel_id=1, source_target_pairs={{0,0},{126,126},{2,4},{4,2},{6,8},{8,6},{10,12},{12,10},{14,16},{1... | collective-permute-start | bytes 147464 | tf_op jit(solution)/shard_map/ppermute | solution.py:496
  60.2 4.2 %collective-permute-start.3 = (f32[16,768]{1,0:T(8,128)}, f32[16,768]{1,0:T(8,128)S(1)}, u32[]{:S(2)}, u32[]{:S(2)}) collective-permute-start(f32[16,768]{1,0:T(8,128)} %get-tuple-element.26), channel_id=1, source_target_pairs={{0,2},{2,0},{4,6},{6,4},{8,10},{10,8},{12,14},{14,12},{16,18},{18,... | collective-permute-start | bytes 147464 | tf_op jit(solution)/shard_map/ppermute | solution.py:497
  60.3 1.4 %copy-start = (bf16[1040,768]{1,0:T(8,128)(2,1)S(1)}, bf16[1040,768]{1,0:T(8,128)(2,1)}, u32[]{:S(2)}) copy-start(bf16[1040,768]{1,0:T(8,128)(2,1)} %get-tuple-element.25.spread) | copy-start | bytes 4792324
  61.7 1.4 %copy-start.1 = (bf16[1024,768]{1,0:T(8,128)(2,1)S(1)}, bf16[1024,768]{1,0:T(8,128)(2,1)}, u32[]{:S(2)}) copy-start(bf16[1024,768]{1,0:T(8,128)(2,1)} %get-tuple-element.16.slope.source) | copy-start | bytes 4718596
  63.1 2.2 %copy-start.2 = (f32[768,128]{1,0:T(8,128)S(1)}, f32[768,128]{1,0:T(8,128)}, u32[]{:S(2)}) copy-start(f32[768,128]{1,0:T(8,128)} %projection.1) | copy-start | bytes 1179652
  63.1 2.2 %copy-start.3 = (f32[64,768]{1,0:T(8,128)S(1)}, f32[64,768]{1,0:T(8,128)}, u32[]{:S(2)}) copy-start(f32[64,768]{1,0:T(8,128)} %get-tuple-element.23.turned) | copy-start | bytes 589828
  63.1 2.2 %copy-start.4 = (f32[8,768]{1,0:T(8,128)S(1)}, f32[8,768]{1,0:T(8,128)}, u32[]{:S(2)}) copy-start(f32[8,768]{1,0:T(8,128)} %get-tuple-element.24.hidden_up) | copy-start | bytes 73732
  63.1 2.2 %copy-start.5 = (f32[8,128]{1,0:T(8,128)S(1)}, f32[8,128]{1,0:T(8,128)}, u32[]{:S(2)}) copy-start(f32[8,128]{1,0:T(8,128)} %get-tuple-element.19.refs_1_.inverse) | copy-start | bytes 12292
  63.1 2.2 %copy-start.6 = (s32[4]{0:T(128)S(1)}, s32[4]{0:T(128)}, u32[]{:S(2)}) copy-start(s32[4]{0:T(128)} %pad_add_fusion.where) | copy-start | bytes 52
  63.1 2.2 %copy-start.7 = (f32[8,64]{1,0:T(8,128)S(1)}, f32[8,64]{1,0:T(8,128)}, u32[]{:S(2)}) copy-start(f32[8,64]{1,0:T(8,128)} %get-tuple-element.22.along) | copy-start | bytes 6148
  67.3 0.6 copy-start.9
  67.9 20.6 %copy-start.8 = (f32[8,768]{1,0:T(8,128)}, f32[8,768]{1,0:T(8,128)S(1)}, u32[]{:S(2)}) copy-start(f32[8,768]{1,0:T(8,128)S(1)} %get-tuple-element.27.d_pooled) | copy-start | bytes 73732
  67.9 15.5 %all-to-all-start.2 = ((f32[16,32,128]{2,1,0:T(8,128)}), f32[16,32,128]{2,1,0:T(8,128)S(1)}, u32[]{:S(2)}, u32[]{:S(2)}) async-start(f32[16,32,128]{2,1,0:T(8,128)} %get-tuple-element.29), calls=%async_computation.2 | async-start | bytes 524288 | tf_op jit(solution)/shard_map/all_to_all | solution.py:510
  84.1 15.9 %all-to-all-start.3 = ((f32[8,32,128]{2,1,0:T(8,128)}), f32[8,32,128]{2,1,0:T(8,128)S(1)}, u32[]{:S(2)}, u32[]{:S(2)}) async-start(f32[8,32,128]{2,1,0:T(8,128)} %broadcast_in_dim.5), calls=%async_computation.3 | async-start | bytes 262144 | tf_op jit(solution)/shard_map/all_to_all | solution.py:510

commit v4 on v3

--- a/solution.py
+++ b/solution.py
@@ -241,7 +241,7 @@
     )(where, *inputs)
 
 
-def input_kernel(chunk, source, d_pooled, ends, taps_in, out, cells, shifted, taps, slope, block, sems):
+def input_kernel(chunk, where, source, d_pooled, loose, far, near, taps_in, out, cells, shifted, taps, slope, block, sems):
     patches, channels = slope.shape
     blocks = channels // LANES
     kernel = taps.shape[0] // channels
@@ -264,12 +264,24 @@
     ]
     for copy in reads + copies:
         copy.start()
+    prior, later = from_sides(where, far[...], near[...])
+    wide = 2 * OP
+    sides = []
+    for row, other in ((0, prior[:PAD]), (1, later[PAD:])):
+        grad = finish(
+            loose[row : row + 1, :], loose[2 + row : 3 + row, :wide], other[3:4, :wide],
+            other[4:5, :1], other[2:3],
+        )
+        sides.append(grad * other[:2])
+    blank = jnp.zeros((PAD - 2, channels), f32)
+    above = jnp.concatenate([blank, sides[0]], axis=0)
+    below = jnp.concatenate([sides[1], blank], axis=0)
     for copy in reads:
         copy.wait()
     for c in range(blocks):
         at = slice(c * LANES, (c + 1) * LANES)
-        cells[c, :PAD, :] = ends[:PAD, at].astype(f32)
-        cells[c, PAD + patches :, :] = ends[PAD:, at].astype(f32)
+        cells[c, :PAD, :] = above[:, at]
+        cells[c, PAD + patches :, :] = below[:, at]
         for n in range(patches // POOL):
             low, high = n * POOL, (n + 1) * POOL
             cells[c, PAD + low : PAD + high, :] = (
@@ -309,14 +321,14 @@
         back.wait()
 
 
-def input_stage(slope, d_pooled, ends, taps, chunk=512):
+def input_stage(where, slope, d_pooled, loose, far, near, taps, chunk=512):
     vmem = pl.BlockSpec(memory_space=pltpu.VMEM)
     patches, channels = slope.shape
     kernel = taps.shape[0] // channels
     return pl.pallas_call(
         functools.partial(input_kernel, chunk),
         out_shape=jax.ShapeDtypeStruct((patches, channels), bf16),
-        in_specs=[HBM, vmem, vmem, HBM],
+        in_specs=[pl.BlockSpec(memory_space=pltpu.SMEM), HBM] + [vmem] * 4 + [HBM],
         out_specs=HBM,
         scratch_shapes=[
             pltpu.VMEM((channels // LANES, patches + 2 * PAD, LANES), f32),
@@ -331,7 +343,7 @@
             flops=6_100_000_000, bytes_accessed=10_000_000, transcendentals=0
         ),
         name="inner",
-    )(slope, d_pooled, ends, taps)
+    )(where, slope, d_pooled, loose, far, near, taps)
 
 
 def weights_kernel(*refs):
@@ -438,16 +450,16 @@
     )(buckets, spread, slope)
 
 
-def tail_kernel(where, received, along, turned, hidden_up, inverse, kept, projection, far, near, d_pooled, sketch, edges):
+def finish(rows, grad, line, scale, lifted):
+    inner = jnp.sum(grad * line, axis=1, keepdims=True)
+    return (scale * rows - scale * scale * scale * inner * lifted) * (1.0 / POOL)
+
+
+def tail_kernel(received, along, turned, hidden_up, inverse, kept, projection, d_pooled, sketch, loose):
     bins = kept.shape[0]
     summed = jnp.sum(received[...].astype(f32), axis=0)
-    prior, later = from_sides(where, far[...], near[...])
     grads = jnp.concatenate([summed[:, : 2 * OP], summed[:, 2 * OP :]], axis=0)
     both = jnp.dot(grads, turned[...], precision=highest, preferred_element_type=f32)
-
-    def finish(rows, grad, line, scale, lifted):
-        inner = jnp.sum(grad * line, axis=1, keepdims=True)
-        return (scale * rows - scale * scale * scale * inner * lifted) * (1.0 / POOL)
 
     scaled = finish(both[:bins], grads[:bins], along[...], inverse[:, :1], hidden_up[...])
     d_pooled[...] = scaled
@@ -455,36 +467,30 @@
     for n in range(1, bins):
         total = total + scaled[n : n + 1] * kept[n]
     part = jnp.dot(total, projection[...], precision=highest, preferred_element_type=f32)
-    sketch[...] = jnp.broadcast_to(part[None], sketch.shape)
-    first = finish(
-        both[bins : bins + 1], grads[bins : bins + 1], prior[3:4, : 2 * OP], prior[4:5, :1], prior[2:3]
-    )
-    last = finish(
-        both[2 * bins - 1 :], grads[2 * bins - 1 :], later[PAD + 3 : PAD + 4, : 2 * OP],
-        later[PAD + 4 : PAD + 5, :1], later[PAD + 2 : PAD + 3],
-    )
-    blank = jnp.zeros((PAD - 2, first.shape[1]), f32)
-    edges[...] = jnp.concatenate(
-        [blank, first * prior[:2], last * later[PAD : PAD + 2], blank], axis=0
-    ).astype(bf16)
-
-
-def tail_stage(where, received, along, turned, hidden_up, inverse, kept, projection, far, near, fan):
+    sketch[...] = jnp.broadcast_to(part.astype(bf16)[None], sketch.shape)
+    loose[...] = jnp.zeros_like(loose)
+    loose[:1, :] = both[bins : bins + 1]
+    loose[1:2, :] = both[2 * bins - 1 :]
+    loose[2:3, : 2 * OP] = grads[bins : bins + 1]
+    loose[3:4, : 2 * OP] = grads[2 * bins - 1 :]
+
+
+def tail_stage(received, along, turned, hidden_up, inverse, kept, projection, fan):
     vmem = pl.BlockSpec(memory_space=pltpu.VMEM)
     bins, channels = hidden_up.shape
     return pl.pallas_call(
         tail_kernel,
         out_shape=[
             jax.ShapeDtypeStruct((bins, channels), f32),
-            jax.ShapeDtypeStruct((fan, kept.shape[1], projection.shape[1]), f32),
-            jax.ShapeDtypeStruct((2 * PAD, channels), bf16),
+            jax.ShapeDtypeStruct((fan, kept.shape[1], projection.shape[1]), bf16),
+            jax.ShapeDtypeStruct((PAD, channels), f32),
         ],
-        in_specs=[pl.BlockSpec(memory_space=pltpu.SMEM)] + [vmem] * 9,
+        in_specs=[vmem] * 7,
         out_specs=[vmem] * 3,
         compiler_params=pltpu.CompilerParams(vmem_limit_bytes=24 << 20),
         cost_estimate=pl.CostEstimate(flops=20_000_000, bytes_accessed=4_000_000, transcendentals=0),
         name="tail",
-    )(where, received, along, turned, hidden_up, inverse, kept, projection, far, near)
+    )(received, along, turned, hidden_up, inverse, kept, projection)
 
 
 def to_sides(value, axes):
@@ -550,20 +556,18 @@
     )
     sent = pair_stage(where, parts, cotangent[0], wide)
     received = exchange(sent, line)
+    kept = bins_stage(buckets.reshape(kernel, channels), spread, slope)
+    d_pooled, sketch, loose = tail_stage(
+        received, along, turned, hidden_up, inverse, kept, projection,
+        lax.axis_size(("batch", "seq", "col")),
+    )
+    batches = lax.axis_size("batch")
+    every = exchange(sketch, ("batch", "seq", "col"))
     far, near = to_sides(shared, line)
-    kept = bins_stage(buckets.reshape(kernel, channels), spread, slope)
-    d_pooled, sketch, grad_ends = tail_stage(
-        where, received, along, turned, hidden_up, inverse, kept, projection, far, near,
-        lax.axis_size("seq"),
-    )
-    sketch = jnp.sum(exchange(sketch, "seq"), axis=0)
-    input_grad = input_stage(slope, d_pooled, grad_ends, conv_weight)
-    col_count = lax.axis_size("col")
-    batches = lax.axis_size("batch")
-    every = exchange(
-        jnp.broadcast_to(sketch[None], (batches * col_count,) + sketch.shape), ("batch", "col")
-    )
-    sketches = jnp.sum(every.reshape(batches, col_count, *sketch.shape), axis=1)
+    input_grad = input_stage(where, slope, d_pooled, loose, far, near, conv_weight)
+    sketches = jnp.sum(
+        every.astype(f32).reshape(batches, count, *sketch.shape[1:]), axis=1
+    )
     units = sketches * lax.rsqrt(
         jnp.mean(sketches * sketches, axis=(1, 2), keepdims=True) + 1e-06
     )

time: 102 us -> 101 us (level)
  starting transfers between devices: 39.7 us -> 32.8 us
  waiting for transfers between devices: 17.1 us -> 23.9 us
    ppermute x2, waiting for transfers between devices: 0.52 us -> 11.1 us  [to_sides(): far = lax.ppermute(value, axes, across)]
    all_to_all x4 -> x3, starting transfers between devices: 29 us -> 22 us  [exchange(): return lax.all_to_all(value, axes, 0, 0, tiled=True)]
    all_to_all x4 -> x3, waiting for transfers between devices: 15.3 us -> 11.5 us  [exchange(): return lax.all_to_all(value, axes, 0, 0, tiled=True)]
    unnamed x26 -> x30, local copies, waits for them, and re-layouts: 4.05 us -> 4.66 us
  transfers between devices with their start and end apart: 8 -> 7, of which waited for: 5 -> 5; matrix products, arithmetic and copies ran while one was open for 1% -> 1% of each run, Pallas kernels for 17% -> 17%
where the time goes in v4:
time: 101 us
  Pallas kernels  35.5 us (35%)
  starting transfers between devices  32.8 us (32%)
  waiting for transfers between devices  23.9 us (24%)
  local copies, waits for them, and re-layouts  5.84 us (6%)
  other arithmetic  1.61 us (2%)
    all_to_all x3, starting transfers between devices, exchange(): return lax.all_to_all(value, axes, 0, 0, tiled=True)  22 us
    pallas_call x1, Pallas kernels, forward_stage(): pl.pallas_call(functools.partial(forward_kernel, chunk), out_shape=[jax.S...  13.3 us
    all_to_all x3, waiting for transfers between devices, exchange(): return lax.all_to_all(value, axes, 0, 0, tiled=True)  11.5 us
    pallas_call x1, Pallas kernels, input_stage(): pl.pallas_call(functools.partial(input_kernel, chunk), out_shape=jax.Shap...  11.5 us
    ppermute x2, waiting for transfers between devices, to_sides(): far = lax.ppermute(value, axes, across)  11.1 us
    ppermute x2, starting transfers between devices, to_sides(): far = lax.ppermute(value, axes, across)  10.6 us
    unnamed x30, local copies, waits for them, and re-layouts  4.66 us
    pallas_call x1, Pallas kernels, weights_stage(): pl.pallas_call(weights_kernel, out_shape=[jax.ShapeDtypeStruct((2 * OP, c...  4.05 us
  transfers between devices with their start and end apart: 7, of which 5 were waited for; matrix products, arithmetic and copies ran while one was open for 1% of the time, Pallas kernels for 17%

profile of v4, /device:TPU:1, one launch (start us, length us, event | category | flops | bytes accessed | tf_op | source)
XLA Modules:
  0.0 100.6 jit_solution(13849657301315418493)
XLA Ops:
  0.6 0.8 slice_reduce_fusion.1
  1.4 0.1 concatenate.8
  1.5 0.1 concatenate.9
  1.6 0.1 eq.24
  1.7 0.1 eq.26
  1.9 5.8 %collective-permute-start = (bf16[16,64]{1,0:T(8,128)(2,1)S(1)}, bf16[16,64]{1,0:T(8,128)(2,1)S(1)}, u32[]{:S(2)}, u32[]{:S(2)}) collective-permute-start(bf16[16,64]{1,0:T(8,128)(2,1)S(1)} %pad_convert_fusion), channel_id=1, source_target_pairs={{0,0},{126,126},{2,4},{4,2},{6,8},{8,6},{10,12},{12,10},{14,16},{1... | collective-permute-start | bytes 6152 | tf_op jit(solution)/shard_map/ppermute | solution.py:502
  7.6 0.1 collective-permute-start.1
  7.7 0.6 pad_add_fusion.where
  8.4 0.6 collective-permute-done.refs_1_
  8.9 1.3 %collective-permute-done.1.refs_2_ = bf16[16,64]{1,0:T(8,128)(2,1)S(1)} collective-permute-done((bf16[16,64]{1,0:T(8,128)(2,1)S(1)}, bf16[16,64]{1,0:T(8,128)(2,1)S(1)}, u32[]{:S(2)}, u32[]{:S(2)}) %collective-permute-start.1) | collective-permute-done | bytes 2080 | tf_op jit(solution)/shard_map/ppermute | solution.py:503
  10.2 0.6 copy-done.14
  10.8 13.3 %forward.1 = (bf16[1040,768]{1,0:T(8,128)(2,1)}, bf16[1024,768]{1,0:T(8,128)(2,1)}, bf16[64,8,128]{2,1,0:T(8,128)(2,1)}, f32[8,1536]{1,0:T(8,128)}, f32[8,128]{1,0:T(8,128)}, /*index=5*/bf16[16,768]{1,0:T(8,128)(2,1)}) custom-call(s32[4]{0:T(128)} %pad_add_fusion.where, s32[128,128]{1,0:T(8,128)} %bitcast.17, bf16[16,64]{1,0:T(8,128)(2,1)} %copy-done.13, ...), custom_call_target="tpu_custom_call" | custom-call | flops 6200000000 | bytes 14000000 | tf_op jit(solution)/shard_map/forward/pallas_call | solution.py:214
  24.1 12.8 %all-to-all-start = ((bf16[64,8,128]{2,1,0:T(8,128)(2,1)}), bf16[64,8,128]{2,1,0:T(8,128)(2,1)}, u32[]{:S(2)}, u32[]{:S(2)}) async-start(bf16[64,8,128]{2,1,0:T(8,128)(2,1)} %get-tuple-element.17), calls=%async_computation | async-start | bytes 262144 | tf_op jit(solution)/shard_map/all_to_all | solution.py:516
  36.9 4.1 %weights.1 = (f32[64,768]{1,0:T(8,128)}, f32[8,768]{1,0:T(8,128)}, f32[8,64]{1,0:T(8,128)}, f32[16,768]{1,0:T(8,128)}, bf16[32,4096]{1,0:T(8,128)(2,1)}) custom-call(f32[8,1536]{1,0:T(8,128)} %get-tuple-element.18.refs_0_, f32[8,128]{1,0:T(8,128)} %get-tuple-element.19.refs_1_.inverse, bf16[16,768]{1,0:T(8,128)(2,1)} %get-tuple-element.20.refs_2_, ...), custom_call_target="tpu_custom_call" | custom-call | flops 340000000 | bytes 3000000 | tf_op jit(solution)/shard_map/weights/pallas_call | solution.py:394
  41.0 5.7 %all-to-all-done.parts_in = bf16[64,8,128]{2,1,0:T(8,128)(2,1)} async-done(((bf16[64,8,128]{2,1,0:T(8,128)(2,1)}), bf16[64,8,128]{2,1,0:T(8,128)(2,1)}, u32[]{:S(2)}, u32[]{:S(2)}) %all-to-all-start) | async-done | bytes 131104 | tf_op jit(solution)/shard_map/all_to_all | solution.py:516
  46.7 3.7 %pair.1 = bf16[64,8,128]{2,1,0:T(8,128)(2,1)} custom-call(s32[4]{0:T(128)} %pad_add_fusion.where, bf16[64,8,128]{2,1,0:T(8,128)(2,1)} %all-to-all-done.parts_in, bf16[32,128,128]{2,1,0:T(8,128)(2,1)} %bitcast.14, bf16[32,4096]{1,0:T(8,128)(2,1)} %get-tuple-element.21.wide_in), custom_call_target="tpu_custom_call" | custom-call | flops 200000000 | bytes 2000000 | tf_op jit(solution)/shard_map/pair/pallas_call | solution.py:86
  50.4 5.1 %all-to-all-start.1 = ((bf16[64,8,128]{2,1,0:T(8,128)(2,1)}), bf16[64,8,128]{2,1,0:T(8,128)(2,1)S(1)}, u32[]{:S(2)}, u32[]{:S(2)}) async-start(bf16[64,8,128]{2,1,0:T(8,128)(2,1)} %pair.1), calls=%async_computation.1 | async-start | bytes 262144 | tf_op jit(solution)/shard_map/all_to_all | solution.py:516
  55.6 1.4 %copy-done = bf16[1040,768]{1,0:T(8,128)(2,1)S(1)} copy-done((bf16[1040,768]{1,0:T(8,128)(2,1)S(1)}, bf16[1040,768]{1,0:T(8,128)(2,1)}, u32[]{:S(2)}) %copy-start) | copy-done | bytes 1597464
  57.0 1.4 %copy-done.1 = bf16[1024,768]{1,0:T(8,128)(2,1)S(1)} copy-done((bf16[1024,768]{1,0:T(8,128)(2,1)S(1)}, bf16[1024,768]{1,0:T(8,128)(2,1)}, u32[]{:S(2)}) %copy-start.1) | copy-done | bytes 1572888
  58.4 1.2 %bins.1.kept = f32[8,32,768]{2,1,0:T(8,128)S(1)} custom-call(s32[5,768]{1,0:T(8,128)S(1)} %reshape.38.buckets, bf16[1040,768]{1,0:T(8,128)(2,1)S(1)} %copy-done, bf16[1024,768]{1,0:T(8,128)(2,1)S(1)} %copy-done.1), custom_call_target="tpu_custom_call" | custom-call | flops 400000000 | bytes 4000000 | tf_op jit(solution)/shard_map/bins/pallas_call | solution.py:440
  59.6 5.9 %all-to-all-done.1.received = bf16[64,8,128]{2,1,0:T(8,128)(2,1)S(1)} async-done(((bf16[64,8,128]{2,1,0:T(8,128)(2,1)}), bf16[64,8,128]{2,1,0:T(8,128)(2,1)S(1)}, u32[]{:S(2)}, u32[]{:S(2)}) %all-to-all-start.1) | async-done | bytes 131104 | tf_op jit(solution)/shard_map/all_to_all | solution.py:516
  65.5 1.7 %tail.1 = (f32[8,768]{1,0:T(8,128)S(1)}, bf16[128,32,128]{2,1,0:T(8,128)(2,1)}, f32[8,768]{1,0:T(8,128)S(1)}) custom-call(bf16[64,8,128]{2,1,0:T(8,128)(2,1)S(1)} %all-to-all-done.1.received, f32[8,64]{1,0:T(8,128)S(1)} %copy-done.6, f32[64,768]{1,0:T(8,128)S(1)} %copy-done.3, f32[8,768]{1,0:T(8,128)S(1)} %copy-done.4, f32[8,128]{1,0:T(8,128)S(1)} %copy-done.5, ...), custom_call_target="tpu_custom_call" | custom-call | flops 20000000 | bytes 4000000 | tf_op jit(solution)/shard_map/tail/pallas_call | solution.py:481
  67.2 0.6 copy-done.8
  67.8 4.1 %all-to-all-start.2 = ((bf16[128,32,128]{2,1,0:T(8,128)(2,1)}), bf16[128,32,128]{2,1,0:T(8,128)(2,1)S(1)}, u32[]{:S(2)}, u32[]{:S(2)}) async-start(bf16[128,32,128]{2,1,0:T(8,128)(2,1)} %get-tuple-element.29), calls=%async_computation.2 | async-start | bytes 2097152 | tf_op jit(solution)/shard_map/all_to_all | solution.py:516
  71.9 4.8 %collective-permute-start.2 = (f32[16,768]{1,0:T(8,128)S(1)}, f32[16,768]{1,0:T(8,128)S(1)}, u32[]{:S(2)}, u32[]{:S(2)}) collective-permute-start(f32[16,768]{1,0:T(8,128)S(1)} %copy-done.10), channel_id=1, source_target_pairs={{0,0},{126,126},{2,4},{4,2},{6,8},{8,6},{10,12},{12,10},{14,16},{1... | collective-permute-start | bytes 147464 | tf_op jit(solution)/shard_map/ppermute | solution.py:502
  76.7 0.1 collective-permute-start.3
  76.8 10.6 %collective-permute-done.2.far = f32[16,768]{1,0:T(8,128)S(1)} collective-permute-done((f32[16,768]{1,0:T(8,128)S(1)}, f32[16,768]{1,0:T(8,128)S(1)}, u32[]{:S(2)}, u32[]{:S(2)}) %collective-permute-start.2) | collective-permute-done | bytes 49184 | tf_op jit(solution)/shard_map/ppermute | solution.py:502
  87.4 0.6 copy-done.11
  88.0 11.5 %inner.1 = bf16[1024,768]{1,0:T(8,128)(2,1)} custom-call(s32[4]{0:T(128)} %pad_add_fusion.where, bf16[1024,768]{1,0:T(8,128)(2,1)} %get-tuple-element.16.slope.source, f32[8,768]{1,0:T(8,128)} %copy-done.7, f32[8,768]{1,0:T(8,128)} %copy-done.8, f32[16,768]{1,0:T(8,128)} %copy-done.11, f32[16,768]{1,0:T(8,128)} %copy-done.12, bf16[3840,768]{1,0:T(8,128)(2,1)} %taps_in.1), custom_call_target="tpu_custom_call" | custom-call | flops 6099999744 | bytes 10000000 | tf_op jit(solution)/shard_map/inner/pallas_call | solution.py:328
  99.6 0.2 convert_reduce_fusion
  99.7 0.1 multiply_reduce_fusion
  99.9 0.6 bitcast_subtract_fusion
  (35 shorter events, 0.3 us)
Async XLA Ops:
  1.9 7.0 %collective-permute-start = (bf16[16,64]{1,0:T(8,128)(2,1)S(1)}, bf16[16,64]{1,0:T(8,128)(2,1)S(1)}, u32[]{:S(2)}, u32[]{:S(2)}) collective-permute-start(bf16[16,64]{1,0:T(8,128)(2,1)S(1)} %pad_convert_fusion), channel_id=1, source_target_pairs={{0,0},{126,126},{2,4},{4,2},{6,8},{8,6},{10,12},{12,10},{14,16},{1... | collective-permute-start | bytes 6152 | tf_op jit(solution)/shard_map/ppermute | solution.py:502
  7.6 2.5 %collective-permute-start.1 = (bf16[16,64]{1,0:T(8,128)(2,1)S(1)}, bf16[16,64]{1,0:T(8,128)(2,1)S(1)}, u32[]{:S(2)}, u32[]{:S(2)}) collective-permute-start(bf16[16,64]{1,0:T(8,128)(2,1)S(1)} %pad_convert_fusion), channel_id=1, source_target_pairs={{0,2},{2,0},{4,6},{6,4},{8,10},{10,8},{12,14},{14,12},{16,18},{18,... | collective-permute-start | bytes 6152 | tf_op jit(solution)/shard_map/ppermute | solution.py:503
  8.9 1.3 %copy-start.13 = (bf16[16,64]{1,0:T(8,128)(2,1)}, bf16[16,64]{1,0:T(8,128)(2,1)S(1)}, u32[]{:S(2)}) copy-start(bf16[16,64]{1,0:T(8,128)(2,1)S(1)} %collective-permute-done.refs_1_) | copy-start | bytes 6148
  10.2 0.6 copy-start.14
  24.1 22.5 %all-to-all-start = ((bf16[64,8,128]{2,1,0:T(8,128)(2,1)}), bf16[64,8,128]{2,1,0:T(8,128)(2,1)}, u32[]{:S(2)}, u32[]{:S(2)}) async-start(bf16[64,8,128]{2,1,0:T(8,128)(2,1)} %get-tuple-element.17), calls=%async_computation | async-start | bytes 262144 | tf_op jit(solution)/shard_map/all_to_all | solution.py:516
  36.9 18.6 %copy-start.9 = (s32[3840]{0:T(1024)S(1)}, s32[3840]{0:T(1024)}, u32[]{:S(2)}) copy-start(s32[3840]{0:T(1024)} %param.21) | copy-start | bytes 46084
  50.4 15.1 %copy-start.3 = (f32[64,768]{1,0:T(8,128)S(1)}, f32[64,768]{1,0:T(8,128)}, u32[]{:S(2)}) copy-start(f32[64,768]{1,0:T(8,128)} %get-tuple-element.23.turned) | copy-start | bytes 589828
  50.4 15.1 %copy-start.4 = (f32[8,768]{1,0:T(8,128)S(1)}, f32[8,768]{1,0:T(8,128)}, u32[]{:S(2)}) copy-start(f32[8,768]{1,0:T(8,128)} %get-tuple-element.24.hidden_up) | copy-start | bytes 73732
  50.4 15.1 %copy-start.5 = (f32[8,128]{1,0:T(8,128)S(1)}, f32[8,128]{1,0:T(8,128)}, u32[]{:S(2)}) copy-start(f32[8,128]{1,0:T(8,128)} %get-tuple-element.19.refs_1_.inverse) | copy-start | bytes 12292
  50.4 15.1 %copy-start.6 = (f32[8,64]{1,0:T(8,128)S(1)}, f32[8,64]{1,0:T(8,128)}, u32[]{:S(2)}) copy-start(f32[8,64]{1,0:T(8,128)} %get-tuple-element.22.along) | copy-start | bytes 6148
  50.4 15.0 %all-to-all-start.1 = ((bf16[64,8,128]{2,1,0:T(8,128)(2,1)}), bf16[64,8,128]{2,1,0:T(8,128)(2,1)S(1)}, u32[]{:S(2)}, u32[]{:S(2)}) async-start(bf16[64,8,128]{2,1,0:T(8,128)(2,1)} %pair.1), calls=%async_computation.1 | async-start | bytes 262144 | tf_op jit(solution)/shard_map/all_to_all | solution.py:516
  55.6 1.4 %copy-start = (bf16[1040,768]{1,0:T(8,128)(2,1)S(1)}, bf16[1040,768]{1,0:T(8,128)(2,1)}, u32[]{:S(2)}) copy-start(bf16[1040,768]{1,0:T(8,128)(2,1)} %get-tuple-element.25.spread) | copy-start | bytes 4792324
  57.0 1.4 %copy-start.1 = (bf16[1024,768]{1,0:T(8,128)(2,1)S(1)}, bf16[1024,768]{1,0:T(8,128)(2,1)}, u32[]{:S(2)}) copy-start(bf16[1024,768]{1,0:T(8,128)(2,1)} %get-tuple-element.16.slope.source) | copy-start | bytes 4718596
  58.4 7.1 %copy-start.2 = (f32[768,128]{1,0:T(8,128)S(1)}, f32[768,128]{1,0:T(8,128)}, u32[]{:S(2)}) copy-start(f32[768,128]{1,0:T(8,128)} %projection.1) | copy-start | bytes 1179652
  59.6 12.3 %copy-start.10 = (f32[16,768]{1,0:T(8,128)S(1)}, f32[16,768]{1,0:T(8,128)}, u32[]{:S(2)}) copy-start(f32[16,768]{1,0:T(8,128)} %get-tuple-element.28) | copy-start | bytes 147460
  67.2 0.6 copy-start.8
  67.8 19.6 %copy-start.7 = (f32[8,768]{1,0:T(8,128)}, f32[8,768]{1,0:T(8,128)S(1)}, u32[]{:S(2)}) copy-start(f32[8,768]{1,0:T(8,128)S(1)} %get-tuple-element.26.d_pooled) | copy-start | bytes 73732
  67.8 31.8 %all-to-all-start.2 = ((bf16[128,32,128]{2,1,0:T(8,128)(2,1)}), bf16[128,32,128]{2,1,0:T(8,128)(2,1)S(1)}, u32[]{:S(2)}, u32[]{:S(2)}) async-start(bf16[128,32,128]{2,1,0:T(8,128)(2,1)} %get-tuple-element.29), calls=%async_computation.2 | async-start | bytes 2097152 | tf_op jit(solution)/shard_map/all_to_all | solution.py:516
  71.9 15.5 %collective-permute-start.2 = (f32[16,768]{1,0:T(8,128)S(1)}, f32[16,768]{1,0:T(8,128)S(1)}, u32[]{:S(2)}, u32[]{:S(2)}) collective-permute-start(f32[16,768]{1,0:T(8,128)S(1)} %copy-done.10), channel_id=1, source_target_pairs={{0,0},{126,126},{2,4},{4,2},{6,8},{8,6},{10,12},{12,10},{14,16},{1... | collective-permute-start | bytes 147464 | tf_op jit(solution)/shard_map/ppermute | solution.py:502
  76.7 10.7 %collective-permute-start.3 = (f32[16,768]{1,0:T(8,128)S(1)}, f32[16,768]{1,0:T(8,128)S(1)}, u32[]{:S(2)}, u32[]{:S(2)}) collective-permute-start(f32[16,768]{1,0:T(8,128)S(1)} %copy-done.10), channel_id=1, source_target_pairs={{0,2},{2,0},{4,6},{6,4},{8,10},{10,8},{12,14},{14,12},{16,18},{18,... | collective-permute-start | bytes 147464 | tf_op jit(solution)/shard_map/ppermute | solution.py:503
  87.4 0.6 copy-start.11
  87.4 0.6 copy-start.12

commit v5 on v3

--- a/solution.py
+++ b/solution.py
@@ -22,7 +22,6 @@
 highest = lax.Precision.HIGHEST
 HBM = pl.BlockSpec(memory_space=pl.ANY)
 FULL = 67_000_000
-MOST = 60 * 1024 * 1024
 
 
 def split_in_kernel(x):
@@ -326,7 +325,7 @@
             pltpu.VMEM((patches, channels), bf16),
             pltpu.SemaphoreType.DMA((1 + kernel + patches // chunk,)),
         ],
-        compiler_params=pltpu.CompilerParams(vmem_limit_bytes=MOST),
+        compiler_params=pltpu.CompilerParams(vmem_limit_bytes=36 << 20),
         cost_estimate=pl.CostEstimate(
             flops=6_100_000_000, bytes_accessed=10_000_000, transcendentals=0
         ),
@@ -455,7 +454,7 @@
     for n in range(1, bins):
         total = total + scaled[n : n + 1] * kept[n]
     part = jnp.dot(total, projection[...], precision=highest, preferred_element_type=f32)
-    sketch[...] = jnp.broadcast_to(part[None], sketch.shape)
+    sketch[...] = jnp.broadcast_to(part.astype(bf16)[None], sketch.shape)
     first = finish(
         both[bins : bins + 1], grads[bins : bins + 1], prior[3:4, : 2 * OP], prior[4:5, :1], prior[2:3]
     )
@@ -476,7 +475,7 @@
         tail_kernel,
         out_shape=[
             jax.ShapeDtypeStruct((bins, channels), f32),
-            jax.ShapeDtypeStruct((fan, kept.shape[1], projection.shape[1]), f32),
+            jax.ShapeDtypeStruct((fan, kept.shape[1], projection.shape[1]), bf16),
             jax.ShapeDtypeStruct((2 * PAD, channels), bf16),
         ],
         in_specs=[pl.BlockSpec(memory_space=pltpu.SMEM)] + [vmem] * 9,
@@ -554,16 +553,14 @@
     kept = bins_stage(buckets.reshape(kernel, channels), spread, slope)
     d_pooled, sketch, grad_ends = tail_stage(
         where, received, along, turned, hidden_up, inverse, kept, projection, far, near,
-        lax.axis_size("seq"),
-    )
-    sketch = jnp.sum(exchange(sketch, "seq"), axis=0)
+        lax.axis_size(("batch", "seq", "col")),
+    )
+    batches = lax.axis_size("batch")
+    every = exchange(sketch, ("batch", "seq", "col"))
     input_grad = input_stage(slope, d_pooled, grad_ends, conv_weight)
-    col_count = lax.axis_size("col")
-    batches = lax.axis_size("batch")
-    every = exchange(
-        jnp.broadcast_to(sketch[None], (batches * col_count,) + sketch.shape), ("batch", "col")
-    )
-    sketches = jnp.sum(every.reshape(batches, col_count, *sketch.shape), axis=1)
+    sketches = jnp.sum(
+        every.astype(f32).reshape(batches, count, *sketch.shape[1:]), axis=1
+    )
     units = sketches * lax.rsqrt(
         jnp.mean(sketches * sketches, axis=(1, 2), keepdims=True) + 1e-06
     )

time: 102 us -> 98 us (0.961)
  waiting for transfers between devices: 17.1 us -> 13.9 us
  Pallas kernels: 35.7 us -> 34.1 us
  starting transfers between devices: 39.7 us -> 38.2 us
  local copies, waits for them, and re-layouts: 5.89 us -> 7.29 us
  other arithmetic: 1.53 us -> 2.89 us
    all_to_all x4 -> x3, waiting for transfers between devices: 15.3 us -> 12.2 us  [exchange(): return lax.all_to_all(value, axes, 0, 0, tiled=True)]
    unnamed x26, local copies, waits for them, and re-layouts: 4.05 us -> 6.11 us
    pallas_call x1, Pallas kernels: 11.4 us -> 9.53 us  [input_stage(): pl.pallas_call(functools.partial(input_kernel, chunk), out_shape=jax.Shap...]
    all_to_all x4 -> x3, starting transfers between devices: 29 us -> 27.5 us  [exchange(): return lax.all_to_all(value, axes, 0, 0, tiled=True)]
    reduce_sum x2 -> x1, other arithmetic: 0.03 us -> 1.39 us  [whole(): jnp.sum(every.astype(f32).reshape(batches, count, *sketch.shape[1:]), axi...]
  transfers between devices with their start and end apart: 8 -> 7, of which waited for: 5 -> 5; matrix products, arithmetic and copies ran while one was open for 1% -> 1% of each run, Pallas kernels for 17% -> 15%
where the time goes in v5:
time: 98 us; the launch traced here: 97.4 us
  starting transfers between devices  38.2 us (39%)
  Pallas kernels  34.1 us (35%)
  waiting for transfers between devices  13.9 us (14%)
  local copies, waits for them, and re-layouts  7.29 us (7%)
  other arithmetic  2.89 us (3%)
    all_to_all x3, starting transfers between devices, exchange(): return lax.all_to_all(value, axes, 0, 0, tiled=True)  27.5 us
    pallas_call x1, Pallas kernels, forward_stage(): pl.pallas_call(functools.partial(forward_kernel, chunk), out_shape=[jax.S...  13.3 us
    all_to_all x3, waiting for transfers between devices, exchange(): return lax.all_to_all(value, axes, 0, 0, tiled=True)  12.2 us
    ppermute x2, starting transfers between devices, to_sides(): far = lax.ppermute(value, axes, across)  10.5 us
    pallas_call x1, Pallas kernels, input_stage(): pl.pallas_call(functools.partial(input_kernel, chunk), out_shape=jax.Shap...  9.53 us
    unnamed x26, local copies, waits for them, and re-layouts  6.11 us
    pallas_call x1, Pallas kernels, weights_stage(): pl.pallas_call(weights_kernel, out_shape=[jax.ShapeDtypeStruct((2 * OP, c...  4.06 us
    pallas_call x1, Pallas kernels, pair_stage(): pl.pallas_call(pair_kernel, out_shape=jax.ShapeDtypeStruct(parts.shape, b...  3.75 us
  transfers between devices with their start and end apart: 7, of which 5 were waited for; matrix products, arithmetic and copies ran while one was open for 1% of the time, Pallas kernels for 15%

profile of v5, /device:TPU:1, one launch (start us, length us, event | category | flops | bytes accessed | tf_op | source)
XLA Modules:
  0.0 97.4 jit_solution(7613675652259623865)
XLA Ops:
  0.6 0.8 slice_reduce_fusion.1
  1.4 0.1 concatenate.9
  1.5 0.1 concatenate.8
  1.6 0.1 eq.24
  1.7 0.1 eq.26
  1.9 5.8 %collective-permute-start = (bf16[16,64]{1,0:T(8,128)(2,1)S(1)}, bf16[16,64]{1,0:T(8,128)(2,1)S(1)}, u32[]{:S(2)}, u32[]{:S(2)}) collective-permute-start(bf16[16,64]{1,0:T(8,128)(2,1)S(1)} %pad_convert_fusion), channel_id=1, source_target_pairs={{0,0},{126,126},{2,4},{4,2},{6,8},{8,6},{10,12},{12,10},{14,16},{1... | collective-permute-start | bytes 6152 | tf_op jit(solution)/shard_map/ppermute | solution.py:495
  7.6 0.1 collective-permute-start.1
  7.7 0.7 pad_add_fusion.where
  8.4 0.5 collective-permute-done.refs_1_
  8.9 1.3 %collective-permute-done.1.refs_2_ = bf16[16,64]{1,0:T(8,128)(2,1)S(1)} collective-permute-done((bf16[16,64]{1,0:T(8,128)(2,1)S(1)}, bf16[16,64]{1,0:T(8,128)(2,1)S(1)}, u32[]{:S(2)}, u32[]{:S(2)}) %collective-permute-start.1) | collective-permute-done | bytes 2080 | tf_op jit(solution)/shard_map/ppermute | solution.py:496
  10.2 0.6 copy-done.12
  10.8 13.3 %forward.1 = (bf16[1040,768]{1,0:T(8,128)(2,1)}, bf16[1024,768]{1,0:T(8,128)(2,1)}, bf16[64,8,128]{2,1,0:T(8,128)(2,1)}, f32[8,1536]{1,0:T(8,128)}, f32[8,128]{1,0:T(8,128)}, /*index=5*/bf16[16,768]{1,0:T(8,128)(2,1)}) custom-call(s32[4]{0:T(128)} %pad_add_fusion.where, s32[128,128]{1,0:T(8,128)} %bitcast.17, bf16[16,64]{1,0:T(8,128)(2,1)} %copy-done.11, ...), custom_call_target="tpu_custom_call" | custom-call | flops 6200000000 | bytes 14000000 | tf_op jit(solution)/shard_map/forward/pallas_call | solution.py:213
  24.1 12.8 %all-to-all-start = ((bf16[64,8,128]{2,1,0:T(8,128)(2,1)}), bf16[64,8,128]{2,1,0:T(8,128)(2,1)}, u32[]{:S(2)}, u32[]{:S(2)}) async-start(bf16[64,8,128]{2,1,0:T(8,128)(2,1)} %get-tuple-element.17), calls=%async_computation | async-start | bytes 262144 | tf_op jit(solution)/shard_map/all_to_all | solution.py:509
  36.9 4.1 %weights.1 = (f32[64,768]{1,0:T(8,128)}, f32[8,768]{1,0:T(8,128)}, f32[8,64]{1,0:T(8,128)}, f32[16,768]{1,0:T(8,128)}, bf16[32,4096]{1,0:T(8,128)(2,1)}) custom-call(f32[8,1536]{1,0:T(8,128)} %get-tuple-element.18.refs_0_, f32[8,128]{1,0:T(8,128)} %get-tuple-element.19.refs_1_.inverse, bf16[16,768]{1,0:T(8,128)(2,1)} %get-tuple-element.20.refs_2_, ...), custom_call_target="tpu_custom_call" | custom-call | flops 340000000 | bytes 3000000 | tf_op jit(solution)/shard_map/weights/pallas_call | solution.py:381
  41.0 5.7 %all-to-all-done.parts_in = bf16[64,8,128]{2,1,0:T(8,128)(2,1)} async-done(((bf16[64,8,128]{2,1,0:T(8,128)(2,1)}), bf16[64,8,128]{2,1,0:T(8,128)(2,1)}, u32[]{:S(2)}, u32[]{:S(2)}) %all-to-all-start) | async-done | bytes 131104 | tf_op jit(solution)/shard_map/all_to_all | solution.py:509
  46.7 3.8 %pair.1 = bf16[64,8,128]{2,1,0:T(8,128)(2,1)} custom-call(s32[4]{0:T(128)} %pad_add_fusion.where, bf16[64,8,128]{2,1,0:T(8,128)(2,1)} %all-to-all-done.parts_in, bf16[32,128,128]{2,1,0:T(8,128)(2,1)} %bitcast.14, bf16[32,4096]{1,0:T(8,128)(2,1)} %get-tuple-element.21.wide_in), custom_call_target="tpu_custom_call" | custom-call | flops 200000000 | bytes 2000000 | tf_op jit(solution)/shard_map/pair/pallas_call | solution.py:85
  50.5 5.1 %all-to-all-start.1 = ((bf16[64,8,128]{2,1,0:T(8,128)(2,1)}), bf16[64,8,128]{2,1,0:T(8,128)(2,1)S(1)}, u32[]{:S(2)}, u32[]{:S(2)}) async-start(bf16[64,8,128]{2,1,0:T(8,128)(2,1)} %pair.1), calls=%async_computation.1 | async-start | bytes 262144 | tf_op jit(solution)/shard_map/all_to_all | solution.py:509
  55.6 4.7 %collective-permute-start.2 = (f32[16,768]{1,0:T(8,128)}, f32[16,768]{1,0:T(8,128)S(1)}, u32[]{:S(2)}, u32[]{:S(2)}) collective-permute-start(f32[16,768]{1,0:T(8,128)} %get-tuple-element.26), channel_id=1, source_target_pairs={{0,0},{126,126},{2,4},{4,2},{6,8},{8,6},{10,12},{12,10},{14,16},{1... | collective-permute-start | bytes 147464 | tf_op jit(solution)/shard_map/ppermute | solution.py:495
  60.3 0.1 collective-permute-start.3
  60.5 1.4 %copy-done = bf16[1040,768]{1,0:T(8,128)(2,1)S(1)} copy-done((bf16[1040,768]{1,0:T(8,128)(2,1)S(1)}, bf16[1040,768]{1,0:T(8,128)(2,1)}, u32[]{:S(2)}) %copy-start) | copy-done | bytes 1597464
  61.9 1.4 %copy-done.1 = bf16[1024,768]{1,0:T(8,128)(2,1)S(1)} copy-done((bf16[1024,768]{1,0:T(8,128)(2,1)S(1)}, bf16[1024,768]{1,0:T(8,128)(2,1)}, u32[]{:S(2)}) %copy-start.1) | copy-done | bytes 1572888
  63.3 1.2 %bins.1.kept = f32[8,32,768]{2,1,0:T(8,128)S(1)} custom-call(s32[5,768]{1,0:T(8,128)S(1)} %reshape.38.buckets, bf16[1040,768]{1,0:T(8,128)(2,1)S(1)} %copy-done, bf16[1024,768]{1,0:T(8,128)(2,1)S(1)} %copy-done.1), custom_call_target="tpu_custom_call" | custom-call | flops 400000000 | bytes 4000000 | tf_op jit(solution)/shard_map/bins/pallas_call | solution.py:427
  64.5 1.0 %all-to-all-done.1.received = bf16[64,8,128]{2,1,0:T(8,128)(2,1)S(1)} async-done(((bf16[64,8,128]{2,1,0:T(8,128)(2,1)}), bf16[64,8,128]{2,1,0:T(8,128)(2,1)S(1)}, u32[]{:S(2)}, u32[]{:S(2)}) %all-to-all-start.1) | async-done | bytes 131104 | tf_op jit(solution)/shard_map/all_to_all | solution.py:509
  65.5 2.3 %tail.1 = (f32[8,768]{1,0:T(8,128)S(1)}, bf16[128,32,128]{2,1,0:T(8,128)(2,1)}, bf16[16,768]{1,0:T(8,128)(2,1)S(1)}) custom-call(s32[4]{0:T(128)S(1)} %copy-done.7, bf16[64,8,128]{2,1,0:T(8,128)(2,1)S(1)} %all-to-all-done.1.received, f32[8,64]{1,0:T(8,128)S(1)} %copy-done.8, f32[64,768]{1,0:T(8,128)S(1)} %copy-done.4, f32[8,768]{1,0:T(8,128)S(1)} %copy-done.5, ...), custom_call_target="tpu_custom_call" | custom-call | flops 20000000 | bytes 4000000 | tf_op jit(solution)/shard_map/tail/pallas_call | solution.py:474
  67.8 9.6 %all-to-all-start.2 = ((bf16[128,32,128]{2,1,0:T(8,128)(2,1)}), bf16[128,32,128]{2,1,0:T(8,128)(2,1)}, u32[]{:S(2)}, u32[]{:S(2)}) async-start(bf16[128,32,128]{2,1,0:T(8,128)(2,1)} %get-tuple-element.29), calls=%async_computation.2 | async-start | bytes 2097152 | tf_op jit(solution)/shard_map/all_to_all | solution.py:509
  77.4 2.7 %copy-done.9 = bf16[3840,768]{1,0:T(8,128)(2,1)S(1)} copy-done((bf16[3840,768]{1,0:T(8,128)(2,1)S(1)}, bf16[3840,768]{1,0:T(8,128)(2,1)}, u32[]{:S(2)}) %copy-start.9) | copy-done | bytes 5898264
  80.1 9.5 %inner.1 = bf16[1024,768]{1,0:T(8,128)(2,1)} custom-call(bf16[1024,768]{1,0:T(8,128)(2,1)S(1)} %copy-done.2, f32[8,768]{1,0:T(8,128)S(1)} %get-tuple-element.27.d_pooled, bf16[16,768]{1,0:T(8,128)(2,1)S(1)} %get-tuple-element.28.ends, bf16[3840,768]{1,0:T(8,128)(2,1)S(1)} %copy-done.9), custom_call_target="tpu_custom_call" | custom-call | flops 6099999744 | bytes 10000000 | tf_op jit(solution)/shard_map/inner/pallas_call | solution.py:315
  89.7 5.5 %all-to-all-done.2 = bf16[128,32,128]{2,1,0:T(8,128)(2,1)} async-done(((bf16[128,32,128]{2,1,0:T(8,128)(2,1)}), bf16[128,32,128]{2,1,0:T(8,128)(2,1)}, u32[]{:S(2)}, u32[]{:S(2)}) %all-to-all-start.2) | async-done | bytes 1048608 | tf_op jit(solution)/shard_map/all_to_all | solution.py:509
  95.2 1.4 %convert_reduce_fusion = f32[2,32,128]{2,1,0:T(8,128)S(1)} fusion(bf16[128,32,128]{2,1,0:T(8,128)(2,1)} %all-to-all-done.2), kind=kLoop, calls=%fused_computation | loop fusion | flops 1040384 | bytes 1081344 | tf_op jit(solution)/shard_map/reduce_sum | solution.py:561
  96.6 0.1 multiply_reduce_fusion
  96.7 0.1 fusion
  96.7 0.6 bitcast_subtract_fusion
  (31 shorter events, 0.2 us)
Async XLA Ops:
  1.9 7.0 %collective-permute-start = (bf16[16,64]{1,0:T(8,128)(2,1)S(1)}, bf16[16,64]{1,0:T(8,128)(2,1)S(1)}, u32[]{:S(2)}, u32[]{:S(2)}) collective-permute-start(bf16[16,64]{1,0:T(8,128)(2,1)S(1)} %pad_convert_fusion), channel_id=1, source_target_pairs={{0,0},{126,126},{2,4},{4,2},{6,8},{8,6},{10,12},{12,10},{14,16},{1... | collective-permute-start | bytes 6152 | tf_op jit(solution)/shard_map/ppermute | solution.py:495
  7.6 2.5 %collective-permute-start.1 = (bf16[16,64]{1,0:T(8,128)(2,1)S(1)}, bf16[16,64]{1,0:T(8,128)(2,1)S(1)}, u32[]{:S(2)}, u32[]{:S(2)}) collective-permute-start(bf16[16,64]{1,0:T(8,128)(2,1)S(1)} %pad_convert_fusion), channel_id=1, source_target_pairs={{0,2},{2,0},{4,6},{6,4},{8,10},{10,8},{12,14},{14,12},{16,18},{18,... | collective-permute-start | bytes 6152 | tf_op jit(solution)/shard_map/ppermute | solution.py:496
  8.9 1.3 %copy-start.11 = (bf16[16,64]{1,0:T(8,128)(2,1)}, bf16[16,64]{1,0:T(8,128)(2,1)S(1)}, u32[]{:S(2)}) copy-start(bf16[16,64]{1,0:T(8,128)(2,1)S(1)} %collective-permute-done.refs_1_) | copy-start | bytes 6148
  10.2 0.6 copy-start.12
  24.1 22.5 %all-to-all-start = ((bf16[64,8,128]{2,1,0:T(8,128)(2,1)}), bf16[64,8,128]{2,1,0:T(8,128)(2,1)}, u32[]{:S(2)}, u32[]{:S(2)}) async-start(bf16[64,8,128]{2,1,0:T(8,128)(2,1)} %get-tuple-element.17), calls=%async_computation | async-start | bytes 262144 | tf_op jit(solution)/shard_map/all_to_all | solution.py:509
  36.9 23.5 %copy-start.10 = (s32[3840]{0:T(1024)S(1)}, s32[3840]{0:T(1024)}, u32[]{:S(2)}) copy-start(s32[3840]{0:T(1024)} %param.21) | copy-start | bytes 46084
  50.4 15.1 %copy-start.4 = (f32[64,768]{1,0:T(8,128)S(1)}, f32[64,768]{1,0:T(8,128)}, u32[]{:S(2)}) copy-start(f32[64,768]{1,0:T(8,128)} %get-tuple-element.23.turned) | copy-start | bytes 589828
  50.4 15.1 %copy-start.5 = (f32[8,768]{1,0:T(8,128)S(1)}, f32[8,768]{1,0:T(8,128)}, u32[]{:S(2)}) copy-start(f32[8,768]{1,0:T(8,128)} %get-tuple-element.24.hidden_up) | copy-start | bytes 73732
  50.4 15.1 %copy-start.6 = (f32[8,128]{1,0:T(8,128)S(1)}, f32[8,128]{1,0:T(8,128)}, u32[]{:S(2)}) copy-start(f32[8,128]{1,0:T(8,128)} %get-tuple-element.19.refs_1_.inverse) | copy-start | bytes 12292
  50.5 15.1 %copy-start.7 = (s32[4]{0:T(128)S(1)}, s32[4]{0:T(128)}, u32[]{:S(2)}) copy-start(s32[4]{0:T(128)} %pad_add_fusion.where) | copy-start | bytes 52
  50.5 15.1 %copy-start.8 = (f32[8,64]{1,0:T(8,128)S(1)}, f32[8,64]{1,0:T(8,128)}, u32[]{:S(2)}) copy-start(f32[8,64]{1,0:T(8,128)} %get-tuple-element.22.along) | copy-start | bytes 6148
  50.5 15.0 %all-to-all-start.1 = ((bf16[64,8,128]{2,1,0:T(8,128)(2,1)}), bf16[64,8,128]{2,1,0:T(8,128)(2,1)S(1)}, u32[]{:S(2)}, u32[]{:S(2)}) async-start(bf16[64,8,128]{2,1,0:T(8,128)(2,1)} %pair.1), calls=%async_computation.1 | async-start | bytes 262144 | tf_op jit(solution)/shard_map/all_to_all | solution.py:509
  55.6 8.9 %collective-permute-start.2 = (f32[16,768]{1,0:T(8,128)}, f32[16,768]{1,0:T(8,128)S(1)}, u32[]{:S(2)}, u32[]{:S(2)}) collective-permute-start(f32[16,768]{1,0:T(8,128)} %get-tuple-element.26), channel_id=1, source_target_pairs={{0,0},{126,126},{2,4},{4,2},{6,8},{8,6},{10,12},{12,10},{14,16},{1... | collective-permute-start | bytes 147464 | tf_op jit(solution)/shard_map/ppermute | solution.py:495
  60.3 4.2 %collective-permute-start.3 = (f32[16,768]{1,0:T(8,128)}, f32[16,768]{1,0:T(8,128)S(1)}, u32[]{:S(2)}, u32[]{:S(2)}) collective-permute-start(f32[16,768]{1,0:T(8,128)} %get-tuple-element.26), channel_id=1, source_target_pairs={{0,2},{2,0},{4,6},{6,4},{8,10},{10,8},{12,14},{14,12},{16,18},{18,... | collective-permute-start | bytes 147464 | tf_op jit(solution)/shard_map/ppermute | solution.py:496
  60.5 1.4 %copy-start = (bf16[1040,768]{1,0:T(8,128)(2,1)S(1)}, bf16[1040,768]{1,0:T(8,128)(2,1)}, u32[]{:S(2)}) copy-start(bf16[1040,768]{1,0:T(8,128)(2,1)} %get-tuple-element.25.spread) | copy-start | bytes 4792324
  61.9 1.4 %copy-start.1 = (bf16[1024,768]{1,0:T(8,128)(2,1)S(1)}, bf16[1024,768]{1,0:T(8,128)(2,1)}, u32[]{:S(2)}) copy-start(bf16[1024,768]{1,0:T(8,128)(2,1)} %get-tuple-element.16.slope.source) | copy-start | bytes 4718596
  63.3 2.3 %copy-start.3 = (f32[768,128]{1,0:T(8,128)S(1)}, f32[768,128]{1,0:T(8,128)}, u32[]{:S(2)}) copy-start(f32[768,128]{1,0:T(8,128)} %projection.1) | copy-start | bytes 1179652
  64.5 13.0 %copy-start.2 = (bf16[1024,768]{1,0:T(8,128)(2,1)S(1)}, bf16[1024,768]{1,0:T(8,128)(2,1)}, u32[]{:S(2)}) copy-start(bf16[1024,768]{1,0:T(8,128)(2,1)} %get-tuple-element.16.slope.source) | copy-start | bytes 4718596
  67.8 27.4 %all-to-all-start.2 = ((bf16[128,32,128]{2,1,0:T(8,128)(2,1)}), bf16[128,32,128]{2,1,0:T(8,128)(2,1)}, u32[]{:S(2)}, u32[]{:S(2)}) async-start(bf16[128,32,128]{2,1,0:T(8,128)(2,1)} %get-tuple-element.29), calls=%async_computation.2 | async-start | bytes 2097152 | tf_op jit(solution)/shard_map/all_to_all | solution.py:509
  77.4 2.7 %copy-start.9 = (bf16[3840,768]{1,0:T(8,128)(2,1)S(1)}, bf16[3840,768]{1,0:T(8,128)(2,1)}, u32[]{:S(2)}) copy-start(bf16[3840,768]{1,0:T(8,128)(2,1)} %taps_in.1) | copy-start | bytes 17694724
